TPU v7x, 32 devices: a whole 2x2x4 slice. The times are simulated.
32 devices in a mesh: frames: 8 (over z, y), band: 4 (over x, core).
Axes of the slice: x: 2, y: 2, z: 4, core: 2. Of those that a mesh axis runs over, the one named last changes fastest.
Arguments:
- tokens: bfloat16 [16, 1024, 1024], P('frames', 'band'), may hold values from -6 to 6
- norm_space: float32 [1024], replicated, may hold values from 0.5 to 1.5
- query_space: bfloat16 [1024, 1024], replicated, may hold values from -0.1875 to 0.1875
- keyval_space: bfloat16 [1024, 512], replicated, may hold values from -0.1875 to 0.1875
- out_space: bfloat16 [1024, 1024], replicated, may hold values from -0.1875 to 0.1875
- qk_space: float32 [2, 64], replicated, may hold values from 0.7 to 7
- norm_time: float32 [1024], replicated, may hold values from 0.5 to 1.5
- query_time: bfloat16 [1024, 1024], replicated, may hold values from -0.1875 to 0.1875
- keyval_time: bfloat16 [1024, 512], replicated, may hold values from -0.1875 to 0.1875
- out_time: bfloat16 [1024, 1024], replicated, may hold values from -0.1875 to 0.1875
- qk_time: float32 [2, 64], replicated, may hold values from 0.7 to 7
Outputs:
- mixed: bfloat16 [16, 1024, 1024], P('frames', 'band')
All inputs are finite; a program needn't handle non-finite values.
Results may differ from a plain program's by a relative error of at most 0.025.
The roundings to bfloat16 on the way count: a program that leaves them out, or rounds other values in their place, can miss the bound.
Values may be sent and summed in bfloat16 or wider, within the bound.
No kernel may reach another device: no remote copies, remote signals or barrier semaphores. Data moves between devices by JAX's collectives and lax.ppermute only.
A program may use at most 128 MiB of HBM per device.

v0:
```python
import jax
import jax.numpy as jnp
from jax import lax
from jax.sharding import PartitionSpec as P

HEADS = 16
KV_HEADS = 4
HEAD_DIM = 64


def rms_rows(values, gain):
    values = values.astype(jnp.float32)
    scaled = lax.rsqrt(jnp.mean(values * values, axis=-1, keepdims=True) + 1e-06)
    return values * scaled * gain


def project(hidden, w_query, w_keyval, qk_gain):
    row_count = hidden.shape[0]
    queries = jnp.dot(hidden, w_query, preferred_element_type=jnp.float32)
    keyval = jnp.dot(hidden, w_keyval, preferred_element_type=jnp.float32)
    queries = rms_rows(queries.reshape(row_count, HEADS, HEAD_DIM), qk_gain[0])
    key_part = keyval[:, : KV_HEADS * HEAD_DIM].reshape(row_count, KV_HEADS, HEAD_DIM)
    key_rows = rms_rows(key_part, qk_gain[1])
    values = keyval[:, KV_HEADS * HEAD_DIM :]
    return (
        queries.reshape(row_count, -1).astype(jnp.bfloat16),
        key_rows.reshape(row_count, -1).astype(jnp.bfloat16),
        values.astype(jnp.bfloat16),
    )


def attend(queries, key_rows, values, causal_mask):
    query_count = queries.shape[0]
    key_count = key_rows.shape[0]
    groups = HEADS // KV_HEADS
    grouped = queries.reshape(query_count, KV_HEADS, groups, HEAD_DIM)
    key_heads = key_rows.reshape(key_count, KV_HEADS, HEAD_DIM)
    value_heads = values.reshape(key_count, KV_HEADS, HEAD_DIM)
    scores = jnp.einsum(
        "nkgd,mkd->kgnm", grouped, key_heads, preferred_element_type=jnp.float32
    ) * HEAD_DIM ** (-0.5)
    if causal_mask is not None:
        scores = jnp.where(causal_mask, scores, -jnp.inf)
    largest = jnp.max(scores, axis=-1, keepdims=True)
    expos = jnp.exp(scores - largest)
    totals = jnp.sum(expos, axis=-1)
    weights = expos.astype(jnp.bfloat16)
    summed = jnp.einsum("kgnm,mkd->nkgd", weights, value_heads, preferred_element_type=jnp.float32)
    summed = summed / jnp.transpose(totals, (2, 0, 1))[..., None]
    return summed.reshape(query_count, HEADS * HEAD_DIM).astype(jnp.bfloat16)


def body(
    tokens,
    norm_space,
    query_space,
    keyval_space,
    out_space,
    qk_space,
    norm_time,
    query_time,
    keyval_time,
    out_time,
    qk_time,
):
    frames_here, rows_here, model_width = tokens.shape
    flat_tokens = tokens.reshape(frames_here * rows_here, model_width)
    normed = rms_rows(flat_tokens, norm_space).astype(jnp.bfloat16)
    queries, key_rows, values = project(normed, query_space, keyval_space, qk_space)
    queries = queries.reshape(frames_here, rows_here, -1)
    key_rows = key_rows.reshape(frames_here, rows_here, -1)
    values = values.reshape(frames_here, rows_here, -1)
    all_keys, all_values = (
        lax.all_gather(key_rows, "band", axis=1, tiled=True),
        lax.all_gather(values, "band", axis=1, tiled=True),
    )

    def space_frame(pieces):
        frame_q, frame_k, frame_v = pieces
        return attend(frame_q, frame_k, frame_v, None)

    attended = lax.map(space_frame, (queries, all_keys, all_values))
    attended = attended.reshape(frames_here * rows_here, HEADS * HEAD_DIM)
    update = jnp.dot(attended, out_space, preferred_element_type=jnp.float32)
    stream = (flat_tokens.astype(jnp.float32) + update).astype(jnp.bfloat16)
    normed_time = rms_rows(stream, norm_time).astype(jnp.bfloat16)
    moved = lax.all_to_all(
        normed_time.reshape(frames_here, rows_here, model_width),
        "frames",
        split_axis=1,
        concat_axis=0,
        tiled=True,
    )
    frame_total, local_positions = (moved.shape[0], moved.shape[1])
    time_q, time_k, time_v = project(
        moved.reshape(frame_total * local_positions, model_width), query_time, keyval_time, qk_time
    )
    time_q = time_q.reshape(frame_total, local_positions, -1)
    time_k = time_k.reshape(frame_total, local_positions, -1)
    time_v = time_v.reshape(frame_total, local_positions, -1)
    order = jnp.arange(frame_total, dtype=jnp.int32)
    causal_mask = order[:, None] >= order[None, :]
    time_att = jax.vmap(lambda qq, kk, vv: attend(qq, kk, vv, causal_mask))(
        jnp.swapaxes(time_q, 0, 1), jnp.swapaxes(time_k, 0, 1), jnp.swapaxes(time_v, 0, 1)
    )
    time_att = jnp.swapaxes(time_att, 0, 1)
    returned = lax.all_to_all(time_att, "frames", split_axis=0, concat_axis=1, tiled=True)
    returned = returned.reshape(frames_here * rows_here, HEADS * HEAD_DIM)
    update_time = jnp.dot(returned, out_time, preferred_element_type=jnp.float32)
    mixed = (stream.astype(jnp.float32) + update_time).astype(jnp.bfloat16)
    return mixed.reshape(frames_here, rows_here, model_width)


def solution(mesh):
    placed = (P("frames", "band", None), P(), P(), P(), P(), P(), P(), P(), P(), P(), P())
    return jax.shard_map(
        body, mesh=mesh, in_specs=placed, out_specs=P("frames", "band", None), check_vma=False
    )
```

profile of v0, /device:TPU:0, one launch (start us, length us, event | category | flops | bytes accessed | tf_op | source)
XLA Modules:
  0.0 223.1 jit_solution(13843182820674432862)
XLA Ops:
  6.5 1.7 fusion.22
  8.2 1.5 fusion.26
  9.8 0.7 fusion.37
  10.5 1.0 copy-done.3
  11.5 0.2 copy.67
  11.9 0.2 copy.68
  12.2 1.1 multiply_convert_fusion.3
  13.4 0.9 copy.69
  14.3 1.1 slice.49
  15.4 0.8 copy.66
  16.3 4.0 %copy.70 = bf16[1024,1024]{0,1:T(8,128)(2,1)} copy(bf16[1024,1024]{1,0:T(8,128)(2,1)} %param.15) | data formatting | bytes 4194304 | tf_op args[2]
  20.3 0.3 fusion.24
  20.6 1.3 copy-done.2
  21.9 1.3 multiply_reduce_fusion.1
  23.2 0.5 multiply_convert_fusion.1
  23.7 1.1 convert_element_type.87
  24.8 2.4 %copy.71 = bf16[2,256,1024]{1,2,0:T(8,128)(2,1)} copy(bf16[2,256,1024]{1,0,2:T(2,128)(2,1)} %convert_element_type.87) | data formatting | bytes 2097152 | tf_op jit(solution)/shard_map/while | solution.py:82
  27.2 6.7 %all-gather.5.cloned.1.call-done = bf16[2,1024,256]{1,2,0:T(8,128)(2,1)} async-done(((bf16[2,256,256]{1,2,0:T(8,128)(2,1)}), bf16[2,1024,256]{1,2,0:T(8,128)(2,1)}) %all-gather.5.cloned.1.call-update) | async-done | bytes 1048592 | tf_op jit(solution)/shard_map/all_gather | solution.py:74
  33.9 18.4 %all-gather.3.cloned.1.call-done = bf16[2,1024,256]{1,2,0:T(8,128)(2,1)} async-done(((bf16[2,256,256]{1,2,0:T(8,128)(2,1)}), bf16[2,1024,256]{1,2,0:T(8,128)(2,1)}) %all-gather.3.cloned.1.call-update) | async-done | bytes 1048592 | tf_op jit(solution)/shard_map/all_gather | solution.py:75
  52.3 57.7 %while.10 = (s32[]{:T(128)}, bf16[2,256,1024]{2,1,0:T(8,128)(2,1)}, bf16[2,1024,256]{1,2,0:T(8,128)(2,1)}, bf16[2,1024,256]{1,2,0:T(8,128)(2,1)}, bf16[2,256,1024]{1,2,0:T(8,128)(2,1)}, /*index=5*/s32[]{:T(128)}) while((s32[]{:T(128)}, bf16[2,256,1024]{2,1,0:T(8,128)(2,1)}, bf16[2,1024,256]{1,2,0:T(8,128)(2,1)}, ...), condition=%wide.region_6.7_spmd, body=%wide.region_3.6_spmd.sunk | while | flops 1107812352 | bytes 57754188 | solution.py:82
  52.3 1.3 constant_dynamic-slice_fusion.5
  53.6 1.1 constant_dynamic-slice_fusion.6
  54.7 8.1 %bitcast_reduce_fusion.4 = (f32[4,4,256]{2,1,0:T(4,128)S(1)}, f32[4,1024,256,4]{2,1,3,0:T(8,128)}) fusion(bf16[1024,4,64,1]{0,2,3,1:T(8,128)(2,1)S(1)} %bitcast.152, bf16[256,4,4,64]{0,3,2,1:T(8,128)(2,1)S(1)} %bitcast.153), kind=kOutput, calls=%fused_computation.1.clone.1 | convolution fusion | flops 545255424 | bytes 17842176 | tf_op jit(solution)/shard_map/while/body/eval_jaxpr/nkgd,mkd->kgnm/dot_general | solution.py:39
  62.8 8.6 %fusion.63 = f32[4,4,256]{2,1,0:T(4,128)S(1)} fusion(f32[4,1024,256,4]{2,1,3,0:T(8,128)} %get-tuple-element.118, f32[4,4,256]{2,1,0:T(4,128)S(1)} %get-tuple-element.119), kind=kLoop, calls=%fused_computation.3.clone.1 | loop fusion | flops 12578816 | bytes 16809984 | tf_op jit(solution)/shard_map/while/body/eval_jaxpr/reduce_sum | solution.py:46
  71.4 8.7 %divide_convert_fusion.2 = bf16[256,4,4,64]{0,3,2,1:T(8,128)(2,1)S(1)} fusion(bf16[1024,4,64,1]{0,2,3,1:T(8,128)(2,1)S(1)} %bitcast.150, f32[4,1024,256,4]{2,1,3,0:T(8,128)} %get-tuple-element.118, f32[4,4,256]{2,1,0:T(4,128)S(1)} %get-tuple-element.119, f32[256,4,4]{0,2,1:T(4,128)S(1)} %bitcast.159), kind=kOutput, calls=%fused_computation.7.clone.1 | convolution fusion | flops 549978112 | bytes 17858560 | tf_op jit(solution)/shard_map/while/body/eval_jaxpr/kgnm,mkd->nkgd/dot_general | solution.py:48
  80.1 0.2 copy.119
  80.3 0.8 constant_dynamic-update-slice_fusion.2
  81.2 1.3 constant_dynamic-slice_fusion.5
  82.4 1.1 constant_dynamic-slice_fusion.6
  83.5 8.1 %bitcast_reduce_fusion.4 = (f32[4,4,256]{2,1,0:T(4,128)S(1)}, f32[4,1024,256,4]{2,1,3,0:T(8,128)}) fusion(bf16[1024,4,64,1]{0,2,3,1:T(8,128)(2,1)S(1)} %bitcast.152, bf16[256,4,4,64]{0,3,2,1:T(8,128)(2,1)S(1)} %bitcast.153), kind=kOutput, calls=%fused_computation.1.clone.1 | convolution fusion | flops 545255424 | bytes 17842176 | tf_op jit(solution)/shard_map/while/body/eval_jaxpr/nkgd,mkd->kgnm/dot_general | solution.py:39
  91.6 8.6 %fusion.63 = f32[4,4,256]{2,1,0:T(4,128)S(1)} fusion(f32[4,1024,256,4]{2,1,3,0:T(8,128)} %get-tuple-element.118, f32[4,4,256]{2,1,0:T(4,128)S(1)} %get-tuple-element.119), kind=kLoop, calls=%fused_computation.3.clone.1 | loop fusion | flops 12578816 | bytes 16809984 | tf_op jit(solution)/shard_map/while/body/eval_jaxpr/reduce_sum | solution.py:46
  100.2 8.7 %divide_convert_fusion.2 = bf16[256,4,4,64]{0,3,2,1:T(8,128)(2,1)S(1)} fusion(bf16[1024,4,64,1]{0,2,3,1:T(8,128)(2,1)S(1)} %bitcast.150, f32[4,1024,256,4]{2,1,3,0:T(8,128)} %get-tuple-element.118, f32[4,4,256]{2,1,0:T(4,128)S(1)} %get-tuple-element.119, f32[256,4,4]{0,2,1:T(4,128)S(1)} %bitcast.159), kind=kOutput, calls=%fused_computation.7.clone.1 | convolution fusion | flops 549978112 | bytes 17858560 | tf_op jit(solution)/shard_map/while/body/eval_jaxpr/kgnm,mkd->nkgd/dot_general | solution.py:48
  108.9 0.2 copy.119
  109.2 0.8 constant_dynamic-update-slice_fusion.2
  110.0 2.9 %fusion.15 = (f32[512]{0:T(512)S(1)}, bf16[512,1024]{1,0:T(8,128)(2,1)S(1)}) fusion(bf16[512,1024]{1,0:T(8,128)(2,1)} %bitcast.178, bf16[1024,1024]{1,0:T(8,128)(2,1)S(1)} %copy-done, bf16[2,256,1024]{2,1,0:T(8,128)(2,1)} %param.13), kind=kOutput, calls=%fused_computation.23 | convolution fusion | flops 1076887040 | bytes 5244928 | tf_op jit(solution)/shard_map/dot_general | solution.py:84
  113.0 1.0 copy-done.5
  113.9 0.3 fusion.17
  114.2 2.1 copy.73
  116.3 5.5 %all-to-all-start = ((bf16[2,256,1024]{2,0,1:T(2,128)(2,1)}), bf16[2,256,1024]{2,0,1:T(2,128)(2,1)S(1)}, u32[]{:S(2)}, u32[]{:S(2)}) async-start(bf16[2,256,1024]{2,0,1:T(2,128)(2,1)} %copy.73), calls=%async_computation | async-start | bytes 2097152 | tf_op jit(solution)/shard_map/all_to_all | solution.py:87
  121.9 3.9 %copy.79 = bf16[1024,1024]{0,1:T(8,128)(2,1)} copy(bf16[1024,1024]{1,0:T(8,128)(2,1)} %param.20) | data formatting | bytes 4194304 | tf_op args[7]
  125.9 22.1 %all-to-all-done = bf16[2,256,1024]{2,0,1:T(2,128)(2,1)S(1)} async-done(((bf16[2,256,1024]{2,0,1:T(2,128)(2,1)}), bf16[2,256,1024]{2,0,1:T(2,128)(2,1)S(1)}, u32[]{:S(2)}, u32[]{:S(2)}) %all-to-all-start) | async-done | bytes 1048608 | tf_op jit(solution)/shard_map/all_to_all | solution.py:87
  148.0 0.3 copy.74
  148.3 0.9 copy-done.14
  149.2 0.7 fusion.38
  150.0 0.9 copy-done.4
  151.0 0.2 copy.76
  151.3 0.2 copy.77
  151.5 1.1 multiply_convert_fusion.2
  152.6 0.2 copy.116
  152.8 1.0 reshape.175
  153.8 3.2 %multiply_reduce_fusion = (f32[512,16]{0,1:T(8,128)S(1)}, f32[512,16,64]{0,2,1:T(8,128)S(1)}) fusion(bf16[512,1024,1]{1,0,2:T(8,128)(2,1)} %bitcast.169, bf16[16,64,1024]{2,1,0:T(8,128)(2,1)} %bitcast.160), kind=kOutput, calls=%fused_computation.43 | convolution fusion | flops 1074782208 | bytes 5275648 | tf_op jit(solution)/shard_map/dot_general | solution.py:19
  157.1 0.5 multiply_convert_fusion
  157.6 2.9 %copy.80 = bf16[512,16,64]{2,1,0:T(8,128)(2,1)} copy(bf16[512,16,64]{0,2,1:T(8,128)(2,1)S(1)} %multiply_convert_fusion) | data formatting | bytes 2097152 | tf_op jit(solution)/shard_map/convert_element_type | solution.py:26
  160.4 3.2 %convert_element_type.93 = bf16[16,32,1024]{2,1,0:T(8,128)(2,1)S(1)} reshape(bf16[512,16,64]{2,1,0:T(8,128)(2,1)} %copy.80) | data formatting | bytes 2097152 | tf_op jit(solution)/shard_map/convert_element_type | solution.py:26
  163.7 2.4 %reshape.186 = bf16[32,16,4,4,64]{4,3,2,0,1:T(4,128)(2,1)} reshape(bf16[32,16,1024]{2,0,1:T(8,128)(2,1)S(1)} %bitcast.154) | data formatting | bytes 2097152 | tf_op jit(solution)/shard_map/vmap()/reshape | solution.py:36
  166.2 0.2 reshape.173
  166.4 6.9 %fusion.14 = (f32[32,4,4,16]{3,2,1,0:T(4,128)S(1)}, f32[32,4,16,16,4]{3,2,4,1,0:T(8,128)S(1)}) fusion(pred[16,16]{0,1:T(8,128)(4,1)S(1)} %iota_compare_fusion, bf16[32,16,4,4,64]{4,3,2,0,1:T(4,128)(2,1)} %reshape.186, bf16[32,16,4,64,1]{3,2,1,0,4:T(4,128)(2,1)} %bitcast.164), kind=kOutput, calls=%fused_computation.19 | convolution fusion | flops 17162240 | bytes 1868032 | tf_op jit(solution)/shard_map/vmap(nkgd,mkd->kgnm)/dot_general | solution.py:39
  173.3 1.6 fusion.12
  175.0 2.4 %fusion.11 = bf16[32,16,4,4,64]{4,1,3,2,0:T(8,128)(2,1)S(1)} fusion(f32[32,4,16,16,4]{3,2,4,1,0:T(8,128)S(1)} %get-tuple-element.80, f32[32,16,4,4]{1,3,2,0:T(4,128)S(1)} %bitcast.176, f32[32,4,4,16]{3,2,1,0:T(4,128)S(1)} %get-tuple-element.79, pred[16,16]{0,1:T(8,128)(4,1)S(1)} %iota_compare_fusion, bf16[32,16,4,64,1]{3,2,1,0,4:T(4,128)(2,1)S(1)} %bitcast.175), kind=kOutput, calls=%fused_computation.14 | convolution fusion | flops 18350080 | bytes 1900800 | tf_op jit(solution)/shard_map/vmap(kgnm,mkd->nkgd)/dot_general | solution.py:48
  177.4 2.5 %copy.86 = bf16[32,16,4,4,64]{4,3,2,1,0:T(4,128)(2,1)} copy(bf16[32,16,4,4,64]{4,1,3,2,0:T(8,128)(2,1)S(1)} %fusion.11) | data formatting | bytes 2097152 | tf_op jit(solution)/shard_map/vmap()/convert_element_type | solution.py:50
  179.8 3.8 %convert_element_type.96 = bf16[32,16,1024]{2,1,0:T(8,128)(2,1)S(1)} reshape(bf16[32,16,4,4,64]{4,3,2,1,0:T(4,128)(2,1)} %copy.86) | data formatting | bytes 2097152 | tf_op jit(solution)/shard_map/vmap()/convert_element_type | solution.py:50
  183.7 0.6 copy.87
  184.3 29.6 %all_to_all.30 = bf16[16,32,1024]{2,1,0:T(8,128)(2,1)S(1)} all-to-all(bf16[16,32,1024]{2,1,0:T(8,128)(2,1)S(1)} %copy.87), channel_id=1, replica_groups=mesh['frames'=8,'band'=4] {'frames'}, dimensions={0} | all-to-all | bytes 2097152 | tf_op jit(solution)/shard_map/all_to_all | solution.py:107
  214.0 2.2 %fusion.18 = bf16[512,1024]{1,0:T(8,128)(2,1)} fusion(bf16[512,1024]{1,0:T(8,128)(2,1)S(1)} %copy-done.6, bf16[512,1024]{1,0:T(8,128)(2,1)S(1)} %bitcast.170, bf16[1024,1024]{1,0:T(8,128)(2,1)S(1)} %copy-done.12), kind=kOutput, calls=%fused_computation.26 | convolution fusion | flops 1075314688 | bytes 5242880 | tf_op jit(solution)/shard_map/dot_general | solution.py:109
  (53 shorter events, 1.1 us)
Async XLA Ops:
  6.5 103.5 %copy-start = (bf16[1024,1024]{1,0:T(8,128)(2,1)S(1)}, bf16[1024,1024]{1,0:T(8,128)(2,1)}, u32[]{:S(2)}) copy-start(bf16[1024,1024]{1,0:T(8,128)(2,1)} %param.17) | copy-start | bytes 6291460
  6.5 3.2 %copy-start.13 = (bf16[1024,512]{1,0:T(8,128)(2,1)S(1)}, bf16[1024,512]{1,0:T(8,128)(2,1)}, u32[]{:S(2)}) copy-start(bf16[1024,512]{1,0:T(8,128)(2,1)} %param.16) | copy-start | bytes 3145732
  6.5 27.4 %all-gather.5.cloned.1.call-start = ((), (), s32[]{:S(2)}) async-start(), calls=%async_computation.3 | async-start | bytes 1310720 | tf_op jit(solution)/shard_map/all_gather | solution.py:74
  10.5 1.0 copy-start.3
  11.5 0.7 copy-start.10
  14.2 38.1 %all-gather.3.cloned.1.call-start = ((), (), s32[]{:S(2)}) async-start(), calls=%async_computation.2 | async-start | bytes 1310720 | tf_op jit(solution)/shard_map/all_gather | solution.py:75
  16.2 4.0 %copy-start.1 = (bf16[2,256,1024]{2,1,0:T(8,128)(2,1)S(1)}, bf16[2,256,1024]{2,1,0:T(8,128)(2,1)}, u32[]{:S(2)}) copy-start(bf16[2,256,1024]{2,1,0:T(8,128)(2,1)} %param.13) | copy-start | bytes 3145732
  16.2 4.0 %copy-start.8 = (f32[1024]{0:T(1024)S(1)}, f32[1024]{0:T(1024)}, u32[]{:S(2)}) copy-start(f32[1024]{0:T(1024)} %param.14) | copy-start | bytes 12292
  20.3 1.6 copy-start.2
  110.0 3.9 %copy-start.9 = (f32[1024]{0:T(1024)S(1)}, f32[1024]{0:T(1024)}, u32[]{:S(2)}) copy-start(f32[1024]{0:T(1024)} %param.19) | copy-start | bytes 12292
  112.9 1.0 copy-start.5
  114.2 7.6 %copy-start.11 = (f32[2,64]{1,0:T(2,128)S(1)}, f32[2,64]{1,0:T(2,128)}, u32[]{:S(2)}) copy-start(f32[2,64]{1,0:T(2,128)} %param.23) | copy-start | bytes 1540
  116.3 31.7 %all-to-all-start = ((bf16[2,256,1024]{2,0,1:T(2,128)(2,1)}), bf16[2,256,1024]{2,0,1:T(2,128)(2,1)S(1)}, u32[]{:S(2)}, u32[]{:S(2)}) async-start(bf16[2,256,1024]{2,0,1:T(2,128)(2,1)} %copy.73), calls=%async_computation | async-start | bytes 2097152 | tf_op jit(solution)/shard_map/all_to_all | solution.py:87
  148.0 1.2 copy-start.14
  148.3 1.7 copy-start.7
  149.9 1.0 copy-start.4
  184.3 29.7 %copy-start.6 = (bf16[512,1024]{1,0:T(8,128)(2,1)S(1)}, bf16[512,1024]{1,0:T(8,128)(2,1)}, u32[]{:S(2)}) copy-start(bf16[512,1024]{1,0:T(8,128)(2,1)} %copy-done.5) | copy-start | bytes 3145732
  184.3 29.7 %copy-start.12 = (bf16[1024,1024]{1,0:T(8,128)(2,1)S(1)}, bf16[1024,1024]{1,0:T(8,128)(2,1)}, u32[]{:S(2)}) copy-start(bf16[1024,1024]{1,0:T(8,128)(2,1)} %param.22) | copy-start | bytes 6291460
Sparse Core Ops, SparseCore 0:
  14.4 19.5 all-gather.4
  35.5 16.8 all-gather.2
where the time goes:
time: 224 us; the launch traced here: 223 us
  matrix products  54 us (24%)
  waiting for transfers between devices  47.3 us (21%)
  local copies, waits for them, and re-layouts  46.6 us (21%)
  blocking collectives  29.6 us (13%)
  other arithmetic  26.1 us (12%)
  between operations  13.8 us (6%)
  starting transfers between devices  5.56 us (2%)
    all_to_all x1, blocking collectives, body(): lax.all_to_all(time_att, 'frames', split_axis=0, concat_axis=1, tiled=True)  29.6 us
    dot_general x3, matrix products, attend(): jnp.einsum('nkgd,mkd->kgnm', grouped, key_heads, preferred_element_type=j...  23.1 us
    all_to_all x1, waiting for transfers between devices, body(): lax.all_to_all(normed_time.reshape(frames_here, rows_here, model_width),...  22.1 us
    dot_general x3, matrix products, attend(): jnp.einsum('kgnm,mkd->nkgd', weights, value_heads, preferred_element_type...  19.9 us
    reduce_sum x3, other arithmetic, attend(): totals = jnp.sum(expos, axis=-1)  18.8 us
    all_gather x1, waiting for transfers between devices, body(): lax.all_gather(values, 'band', axis=1, tiled=True)  18.4 us
    unnamed x33, local copies, waits for them, and re-layouts  13.1 us
    convert_element_type x3, local copies, waits for them, and re-layouts, project(): queries.reshape(row_count, -1).astype(jnp.bfloat16)  7.23 us
  transfers between devices with their start and end apart: 3, of which 3 were waited for; matrix products, arithmetic and copies ran while one was open for 7% of the time, Pallas kernels for 0%

commit v1 on v0

v1 whole, which is shorter than its diff:
```python
import functools

import jax
import jax.numpy as jnp
from jax import lax
from jax.experimental import pallas as pl
from jax.experimental.pallas import tpu as pltpu
from jax.sharding import PartitionSpec as P

EPS = 1e-06
LOG2E = 1.4426950408889634
BF16 = jnp.bfloat16
F32 = jnp.float32
LANES = 128
VMEM_LIMIT = 58 * 1024 * 1024


def dot(a, b):
    return jnp.dot(a, b, preferred_element_type=F32)


def dot_t(a, b):
    return lax.dot_general(a, b, (((1,), (1,)), ((), ())), preferred_element_type=F32)


def row_rms(x, gain):
    x = x.astype(F32)
    return x * lax.rsqrt(jnp.mean(x * x, axis=-1, keepdims=True) + EPS) * gain


def head_mask(width, head):
    shift = head.bit_length() - 1
    i = lax.broadcasted_iota(jnp.int32, (width, width), 0)
    j = lax.broadcasted_iota(jnp.int32, (width, width), 1)
    return jnp.where((i >> shift) == (j >> shift), 1.0, 0.0).astype(BF16)


def head_rms(x, gain, ones, head):
    width = ones.shape[0]
    parts = []
    for c in range(0, x.shape[1], width):
        v = x[:, c : c + width]
        sq = v * v
        hi = sq.astype(BF16)
        lo = (sq - hi.astype(F32)).astype(BF16)
        total = dot(hi, ones) + dot(lo, ones)
        parts.append(v * lax.rsqrt(total * (1.0 / head) + EPS) * gain[:, c : c + width])
    return parts


def twice(tile, head):
    lane = lax.broadcasted_iota(jnp.int32, tile.shape, 1)
    other = pltpu.roll(tile, head, 1)
    low = lane < head
    return jnp.where(low, tile, other), jnp.where(low, other, tile)


def store_queries(parts, q_ref, rows, head):
    scale = LOG2E * head**-0.5
    at = 0
    for part in parts:
        rounded = part.astype(BF16).astype(F32) * scale
        for t in range(0, part.shape[1], 2 * head):
            for one in twice(rounded[:, t : t + 2 * head], head):
                hi = one.astype(BF16).astype(F32)
                lane = lax.broadcasted_iota(jnp.int32, one.shape, 1)
                q_ref[rows, at : at + 2 * head] = jnp.where(lane < head, hi, one - hi).astype(BF16)
                at += 2 * head


def store_doubled(x, out_ref, rows, head):
    at = 0
    for t in range(0, x.shape[1], 2 * head):
        for one in twice(x[:, t : t + 2 * head].astype(F32), head):
            out_ref[rows, at : at + 2 * head] = one.astype(BF16)
            at += 2 * head


def softmax_out(scores, values):
    largest = jnp.max(scores, axis=-1, keepdims=True)
    expos = jnp.exp2(scores - largest)
    total = jnp.sum(expos, axis=-1, keepdims=True)
    return dot(expos.astype(BF16), values) / total


def merge_heads(out, rows, head):
    tiles = []
    for j in range(0, out.shape[0] // rows, 2):
        a = out[j * rows : (j + 1) * rows]
        b = out[(j + 1) * rows : (j + 2) * rows]
        lane = lax.broadcasted_iota(jnp.int32, a.shape, 1)
        tiles.append(jnp.where(lane < head, a, b))
    return jnp.concatenate(tiles, axis=1).astype(BF16)


def keyval_kernel(head, x_ref, norm_ref, w_ref, gain_ref, normed_ref, kv_ref):
    normed = row_rms(x_ref[...], norm_ref[...]).astype(BF16)
    normed_ref[...] = normed
    kv = dot(normed, w_ref[...])
    half = kv.shape[1] // 2
    ones = head_mask(min(256, half), head)
    parts = head_rms(kv[:, :half], gain_ref[...], ones, head)
    kv_ref[:, :half] = jnp.concatenate(parts, axis=1).astype(BF16)
    kv_ref[:, half:] = kv[:, half:].astype(BF16)


def query_kernel(head, x_ref, w_ref, gain_ref, q_ref):
    ones = head_mask(min(256, w_ref.shape[1]), head)
    q = dot(x_ref[...], w_ref[...])
    parts = head_rms(q, gain_ref[...], ones, head)
    store_queries(parts, q_ref, slice(None), head)


def space_kernel(head, first, pieces, *refs):
    (q_ref, x_ref, w_ref, norm_ref), refs = refs[:4], refs[4:]
    kv_refs, (stream_ref, timed_ref, k_buf, v_buf, att) = refs[:pieces], refs[pieces:]
    frames, rows = stream_ref.shape[0], stream_ref.shape[1]
    kv_heads = kv_refs[0].shape[2] // (2 * head)
    heads = q_ref.shape[2] // (2 * head)
    group = heads // kv_heads
    half = kv_heads * head
    wide = 2 * head

    def frame(f, carry):
        for i, ref in enumerate(kv_refs):
            n = ref.shape[1]
            store_doubled(ref[f, :, :half], k_buf, slice(i * n, (i + 1) * n), head)
            store_doubled(ref[f, :, half:], v_buf, slice(i * n, (i + 1) * n), head)

        def key_head(g, c):
            lanes = pl.ds(pl.multiple_of(g * wide, wide), wide)
            keys, values = k_buf[:, lanes], v_buf[:, lanes]
            for j in range(0, group, 2):
                outs = []
                for i in (j, j + 1):
                    at = pl.multiple_of((g * group + i) * wide, wide)
                    q = q_ref[f, first : first + rows, pl.ds(at, wide)]
                    outs.append(softmax_out(dot_t(q, keys), values))
                lane = lax.broadcasted_iota(jnp.int32, outs[0].shape, 1)
                at = pl.multiple_of(g * group * head + j * head, wide)
                att[:, pl.ds(at, wide)] = jnp.where(lane < head, outs[0], outs[1]).astype(BF16)
            return c

        lax.fori_loop(0, kv_heads, key_head, 0)
        update = dot(att[...], w_ref[...])
        stream = (x_ref[f, first : first + rows].astype(F32) + update).astype(BF16)
        stream_ref[f] = stream
        timed_ref[f] = row_rms(stream, norm_ref[...]).astype(BF16)
        return carry

    lax.fori_loop(0, frames, frame, 0)


def time_kernel(head, frames_here, spots, mix_ref, x_ref, wq_ref, wkv_ref, gq_ref, gk_ref, out_ref, q_buf, k_buf, v_buf):
    rows = x_ref.shape[0]
    half = wkv_ref.shape[1] // 2
    kv_heads = half // head
    group = wq_ref.shape[1] // head // kv_heads
    wide = 2 * head
    x = x_ref[...]
    ones = head_mask(min(256, half), head)
    kv = dot(x, wkv_ref[...])
    keys = jnp.concatenate(head_rms(kv[:, :half], gk_ref[...], ones, head), axis=1).astype(BF16)
    store_doubled(keys, k_buf, slice(None), head)
    store_doubled(kv[:, half:].astype(BF16), v_buf, slice(None), head)
    store_queries(head_rms(dot(x, wq_ref[...]), gq_ref[...], ones, head), q_buf, slice(None), head)

    def place(axis):
        n = lax.broadcasted_iota(jnp.int32, (rows, rows), axis)
        source = n // (frames_here * spots)
        frame = (source ^ mix_ref[0]) * frames_here + (n // spots) % frames_here
        return frame, n % spots

    (frame_q, spot_q), (frame_k, spot_k) = place(0), place(1)
    seen = (spot_q == spot_k) & (frame_q >= frame_k)

    def key_head(g, c):
        lanes = pl.ds(pl.multiple_of(g * wide, wide), wide)
        keys, values = k_buf[:, lanes], v_buf[:, lanes]
        for j in range(0, group, 2):
            outs = []
            for i in (j, j + 1):
                at = pl.multiple_of((g * group + i) * wide, wide)
                scores = dot_t(q_buf[:, pl.ds(at, wide)], keys)
                outs.append(softmax_out(jnp.where(seen, scores, -1e30), values))
            lane = lax.broadcasted_iota(jnp.int32, outs[0].shape, 1)
            at = pl.multiple_of(g * group * head + j * head, wide)
            out_ref[:, pl.ds(at, wide)] = jnp.where(lane < head, outs[0], outs[1]).astype(BF16)
        return c

    lax.fori_loop(0, kv_heads, key_head, 0)


def final_kernel(a_ref, x_ref, w_ref, out_ref):
    out_ref[...] = (x_ref[...].astype(F32) + dot(a_ref[...], w_ref[...])).astype(BF16)


def call(kernel, outs, flops, scratch=(), smem=()):
    single = not isinstance(outs, (list, tuple))
    shapes = [outs] if single else list(outs)

    def run(*args):
        moved = sum(a.size * a.dtype.itemsize for a in args) + sum(s.size * s.dtype.itemsize for s in shapes)
        vmem = pl.BlockSpec(memory_space=pltpu.VMEM)
        specs = [pl.BlockSpec(memory_space=pltpu.SMEM) if i in smem else vmem for i in range(len(args))]
        result = pl.pallas_call(
            kernel,
            out_shape=shapes,
            in_specs=specs,
            out_specs=[vmem] * len(shapes),
            scratch_shapes=list(scratch),
            compiler_params=pltpu.CompilerParams(vmem_limit_bytes=VMEM_LIMIT),
            cost_estimate=pl.CostEstimate(flops=int(flops), bytes_accessed=int(moved), transcendentals=0),
        )(*args)
        return result[0] if single else result

    return run


def shaped(*dims):
    return jax.ShapeDtypeStruct(dims, BF16)


def gather_all(x, axis, size):
    pieces = [x]
    step = size // 2
    while step:
        pieces += [lax.ppermute(p, axis, [(i, i ^ step) for i in range(size)]) for p in pieces]
        step //= 2
    return pieces


def make_body(mesh):
    frame_devices, band_devices = mesh.shape["frames"], mesh.shape["band"]

    def body(tokens, norm_space, query_space, keyval_space, out_space, qk_space, norm_time, query_time, keyval_time, out_time, qk_time):
        frames, rows, width = tokens.shape
        head = qk_space.shape[1]
        q_width, half = query_space.shape[1], keyval_space.shape[1] // 2
        heads, kv_heads = q_width // head, half // head
        flat = frames * rows
        gains = [jnp.tile(g[i], n)[None] for g in (qk_space, qk_time) for i, n in ((0, heads), (1, kv_heads))]

        normed, kv = call(functools.partial(keyval_kernel, head), [shaped(flat, width), shaped(flat, 2 * half)], 4 * flat * width * half)(
            tokens.reshape(flat, width), norm_space[None], keyval_space, gains[1]
        )
        all_kv = gather_all(kv.reshape(frames, rows, 2 * half), "band", band_devices)
        queries = call(functools.partial(query_kernel, head), shaped(flat, 2 * q_width), 2 * flat * width * q_width)(normed, query_space, gains[0])
        queries = queries.reshape(frames, rows, 2 * q_width)

        chunks = 2
        part = rows // chunks
        spots = part // frame_devices
        mix = jnp.zeros((1,), jnp.int32)
        keys = rows * band_devices
        outs = []
        for c in range(chunks):
            stream, timed = call(
                functools.partial(space_kernel, head, c * part, len(all_kv)),
                [shaped(frames, part, width), shaped(frames, part, width)],
                frames * part * (16 * keys * q_width + 2 * q_width * width),
                [pltpu.VMEM((keys, 2 * half), BF16), pltpu.VMEM((keys, 2 * half), BF16), pltpu.VMEM((part, q_width), BF16)],
            )(queries, tokens, out_space, norm_time[None], *all_kv)
            sent = timed.reshape(frames, frame_devices, spots, width).swapaxes(0, 1)
            moved = lax.all_to_all(sent, "frames", 0, 0)
            n = frame_devices * frames * spots
            att = call(
                functools.partial(time_kernel, head, frames, spots),
                shaped(n, q_width),
                2 * n * width * (q_width + 2 * half) + 16 * n * n * q_width,
                [pltpu.VMEM((n, 2 * q_width), BF16), pltpu.VMEM((n, 2 * half), BF16), pltpu.VMEM((n, 2 * half), BF16)],
                smem=(0,),
            )(mix, moved.reshape(n, width), query_time, keyval_time, gains[2], gains[3])
            back = lax.all_to_all(att.reshape(frame_devices, frames, spots, q_width), "frames", 0, 0)
            back = back.swapaxes(0, 1).reshape(frames * part, q_width)
            mixed = call(final_kernel, shaped(frames * part, width), 2 * frames * part * width * q_width)(
                back, stream.reshape(frames * part, width), out_time
            )
            outs.append(mixed.reshape(frames, part, width))
        return jnp.concatenate(outs, axis=1)

    return body


def solution(mesh):
    placed = (P("frames", "band", None),) + (P(),) * 10
    return jax.shard_map(make_body(mesh), mesh=mesh, in_specs=placed, out_specs=P("frames", "band", None), check_vma=False)
```

time: 224 us -> 142 us (0.63)
  Pallas kernels: 0 us -> 69.2 us
  matrix products: 54 us -> 0 us
  local copies, waits for them, and re-layouts: 46.6 us -> 9.9 us
  blocking collectives: 29.6 us -> 0 us
  other arithmetic: 26.1 us -> 2.08 us
  starting transfers between devices: 5.56 us -> 22.4 us
  between operations: 13.8 us -> 0.08 us
  waiting for transfers between devices: 47.3 us -> 37.6 us
    pallas_call x0 -> x8, Pallas kernels: none -> 69.2 us  [run(): pl.pallas_call(kernel, out_shape=shapes, in_specs=specs, out_specs=[vmem]...]
    dot_general x12 -> x0, matrix products: 54 us -> none  [the longest x3 23.1 us: attend(): jnp.einsum('nkgd,mkd->kgnm', grouped, key_heads, preferred_element_type=j...]
    all_to_all x1 -> x0, blocking collectives: 29.6 us -> none  [body(): lax.all_to_all(time_att, 'frames', split_axis=0, concat_axis=1, tiled=True)]
    all_gather x2 -> x0, waiting for transfers between devices: 25.1 us -> none  [the longest x1 18.4 us: body(): lax.all_gather(values, 'band', axis=1, tiled=True)]
    reduce_sum x6 -> x0, other arithmetic: 20.6 us -> none  [the longest x3 18.8 us: attend(): totals = jnp.sum(expos, axis=-1)]
    all_to_all x1 -> x4, starting transfers between devices: 5.52 us -> 19.4 us  [the longest x2 12.1 us: body(): moved = lax.all_to_all(sent, 'frames', 0, 0)]
    convert_element_type x5 -> x0, local copies, waits for them, and re-layouts: 13.5 us -> none  [the longest x3 7.23 us: project(): queries.reshape(row_count, -1).astype(jnp.bfloat16)]
    ppermute x0 -> x3, waiting for transfers between devices: none -> 12.1 us  [gather_all(): lax.ppermute(p, axis, [(i, i ^ step) for i in range(size)])]
  transfers between devices with their start and end apart: 3 -> 7, of which waited for: 3 -> 4; matrix products, arithmetic and copies ran while one was open for 7% -> 3% of each run, Pallas kernels for 0% -> 29%
where the time goes in v1:
time: 142 us; the launch traced here: 141 us
  Pallas kernels  69.2 us (49%)
  waiting for transfers between devices  37.6 us (26%)
  starting transfers between devices  22.4 us (16%)
  local copies, waits for them, and re-layouts  9.9 us (7%)
  other arithmetic  2.08 us (1%)
    pallas_call x8, Pallas kernels, run(): pl.pallas_call(kernel, out_shape=shapes, in_specs=specs, out_specs=[vmem]...  69.2 us
    all_to_all x2, waiting for transfers between devices, body(): lax.all_to_all(att.reshape(frame_devices, frames, spots, q_width), 'frame...  20.4 us
    ppermute x3, waiting for transfers between devices, gather_all(): lax.ppermute(p, axis, [(i, i ^ step) for i in range(size)])  12.1 us
    all_to_all x2, starting transfers between devices, body(): moved = lax.all_to_all(sent, 'frames', 0, 0)  12.1 us
    all_to_all x2, starting transfers between devices, body(): lax.all_to_all(att.reshape(frame_devices, frames, spots, q_width), 'frame...  7.31 us
    all_to_all x2, waiting for transfers between devices, body(): moved = lax.all_to_all(sent, 'frames', 0, 0)  5.08 us
    reshape x2, local copies, waits for them, and re-layouts, body(): sent = timed.reshape(frames, frame_devices, spots, width).swapaxes(0, 1)  3.77 us
    another operation x10, local copies, waits for them, and re-layouts, body(): jnp.tile(g[i], n)[None]  3.48 us
  transfers between devices with their start and end apart: 7, of which 4 were waited for; matrix products, arithmetic and copies ran while one was open for 3% of the time, Pallas kernels for 29%

profile of v1, /device:TPU:0, one launch (start us, length us, event | category | flops | bytes accessed | tf_op | source)
XLA Modules:
  0.0 141.2 jit_solution(14484576223684150376)
XLA Ops:
  0.0 0.8 slice_bitcast_fusion.2
  0.8 0.6 broadcast_in_dim_tile.12.gain_ref
  1.4 3.4 %shard_map.109 = (bf16[512,1024]{1,0:T(8,128)(2,1)}, bf16[512,512]{1,0:T(8,128)(2,1)}) custom-call(bf16[512,1024]{1,0:T(8,128)(2,1)} %bitcast.41, f32[1,1024]{1,0:T(1,128)} %bitcast.50, bf16[1024,512]{1,0:T(8,128)(2,1)} %w_ref.4, f32[1,256]{1,0:T(1,128)} %broadcast_in_dim_tile.12.gain_ref), custom_call_target="tpu_custom_call" | custom-call | flops 536870912 | bytes 3675136 | tf_op jit(solution)/shard_map/pallas_call | solution.py:206
  4.8 3.0 %collective-permute-start = (bf16[2,256,512]{2,1,0:T(8,128)(2,1)}, bf16[2,256,512]{2,1,0:T(8,128)(2,1)S(1)}, u32[]{:S(2)}, u32[]{:S(2)}) collective-permute-start(bf16[2,256,512]{2,1,0:T(8,128)(2,1)} %bitcast.51), channel_id=1, source_target_pairs={{0,2},{1,3},{2,0},{3,1},{4,6},{5,7},{6,4},{7,5},{8,10},{9,11},{10,... | collective-permute-start | bytes 1572872 | tf_op jit(solution)/shard_map/ppermute | solution.py:228
  7.8 0.0 collective-permute-start.1
  7.8 12.1 %collective-permute-done.refs_5_ = bf16[2,256,512]{2,1,0:T(8,128)(2,1)S(1)} collective-permute-done((bf16[2,256,512]{2,1,0:T(8,128)(2,1)}, bf16[2,256,512]{2,1,0:T(8,128)(2,1)S(1)}, u32[]{:S(2)}, u32[]{:S(2)}) %collective-permute-start) | collective-permute-done | bytes 524320 | tf_op jit(solution)/shard_map/ppermute | solution.py:228
  19.9 0.0 copy-start.4
  19.9 0.0 collective-permute-start.2
  19.9 0.8 broadcast_in_dim_tile.13.gain_ref
  20.7 6.0 %shard_map.110 = bf16[512,2048]{1,0:T(8,128)(2,1)} custom-call(bf16[512,1024]{1,0:T(8,128)(2,1)} %get-tuple-element.11.x_ref, bf16[1024,1024]{1,0:T(8,128)(2,1)} %w_ref.5, f32[1,1024]{1,0:T(1,128)} %broadcast_in_dim_tile.13.gain_ref), custom_call_target="tpu_custom_call" | custom-call | flops 1073741824 | bytes 5246976 | tf_op jit(solution)/shard_map/pallas_call | solution.py:206
  26.7 0.0 copy-done.4
  26.7 0.0 collective-permute-done.1.refs_6_
  26.7 0.0 copy-start.5
  26.7 0.0 collective-permute-done.2.refs_7_
  26.7 0.0 copy-start.6
  26.7 0.8 copy-done.5
  27.5 0.2 copy-done.6
  27.6 18.4 %shard_map.111 = (bf16[2,128,1024]{2,1,0:T(8,128)(2,1)}, bf16[2,128,1024]{2,1,0:T(8,128)(2,1)}) custom-call(bf16[2,256,2048]{2,1,0:T(8,128)(2,1)} %bitcast.35, bf16[2,256,1024]{2,1,0:T(8,128)(2,1)} %refs_1_.3, bf16[1024,1024]{1,0:T(8,128)(2,1)} %refs_2_.3, f32[1,1024]{1,0:T(1,128)} %bitcast.55, bf16[2,256,512]{2,1,0:T(8,128)(2,1)} %bitcast.53, ...), custom_call_target="tpu_custom_call" | custom-call | flops 4831838208 | bytes 8392704 | tf_op jit(solution)/shard_map/pallas_call | solution.py:206
  46.0 1.9 %copy.23 = bf16[2,8,16,1024]{3,2,0,1:T(8,128)(2,1)} copy(bf16[2,8,16,1024]{3,2,1,0:T(8,128)(2,1)} %bitcast.49) | data formatting | bytes 1048576 | tf_op jit(solution)/shard_map/reshape | solution.py:264
  47.9 6.1 %all-to-all-start = ((bf16[8,2,16,1024]{3,2,1,0:T(8,128)(2,1)}), bf16[8,2,16,1024]{3,2,1,0:T(8,128)(2,1)S(1)}, u32[]{:S(2)}, u32[]{:S(2)}) async-start(bf16[8,2,16,1024]{3,2,1,0:T(8,128)(2,1)} %bitcast.32), calls=%async_computation | async-start | bytes 1048576 | tf_op jit(solution)/shard_map/all_to_all | solution.py:265
  54.0 18.4 %shard_map.114 = (bf16[2,128,1024]{2,1,0:T(8,128)(2,1)}, bf16[2,128,1024]{2,1,0:T(8,128)(2,1)}) custom-call(bf16[2,256,2048]{2,1,0:T(8,128)(2,1)} %bitcast.36, bf16[2,256,1024]{2,1,0:T(8,128)(2,1)} %refs_1_.3, bf16[1024,1024]{1,0:T(8,128)(2,1)} %refs_2_.3, f32[1,1024]{1,0:T(1,128)} %bitcast.56, bf16[2,256,512]{2,1,0:T(8,128)(2,1)} %bitcast.54, ...), custom_call_target="tpu_custom_call" | custom-call | flops 4831838208 | bytes 8392704 | tf_op jit(solution)/shard_map/pallas_call | solution.py:206
  72.3 0.0 copy-start.3
  72.4 1.9 %copy.22 = bf16[2,8,16,1024]{3,2,0,1:T(8,128)(2,1)} copy(bf16[2,8,16,1024]{3,2,1,0:T(8,128)(2,1)} %bitcast.48) | data formatting | bytes 1048576 | tf_op jit(solution)/shard_map/reshape | solution.py:264
  74.2 0.0 all-to-all-done
  74.2 0.0 copy-start.1
  74.2 6.0 %all-to-all-start.2 = ((bf16[8,2,16,1024]{3,2,1,0:T(8,128)(2,1)}), bf16[8,2,16,1024]{3,2,1,0:T(8,128)(2,1)S(1)}, u32[]{:S(2)}, u32[]{:S(2)}) async-start(bf16[8,2,16,1024]{3,2,1,0:T(8,128)(2,1)} %bitcast.31), calls=%async_computation.2 | async-start | bytes 1048576 | tf_op jit(solution)/shard_map/all_to_all | solution.py:265
  80.3 0.0 copy-done.3
  80.3 0.7 broadcast_in_dim_tile.14.gq_ref
  80.9 0.7 broadcast_in_dim_tile.15.gk_ref
  81.6 0.0 copy-done.1
  81.6 8.1 %shard_map.112 = bf16[256,1024]{1,0:T(8,128)(2,1)} custom-call(s32[1]{0:T(128)} %constant.0.clone.1.mix_ref, bf16[256,1024]{1,0:T(8,128)(2,1)} %bitcast.44, bf16[1024,1024]{1,0:T(8,128)(2,1)} %wq_ref.3, bf16[1024,512]{1,0:T(8,128)(2,1)} %wkv_ref.3, f32[1,1024]{1,0:T(1,128)} %broadcast_in_dim_tile.14.gq_ref, f32[1,256]{1,0:T(1,128)} %broadcast_in_dim_tile.15.gk_ref), custom_call_target="tpu_custom_call" | custom-call | flops 1879048192 | bytes 4199428 | tf_op jit(solution)/shard_map/pallas_call | solution.py:206
  89.7 5.1 %all-to-all-done.2 = bf16[8,2,16,1024]{3,2,1,0:T(8,128)(2,1)S(1)} async-done(((bf16[8,2,16,1024]{3,2,1,0:T(8,128)(2,1)}), bf16[8,2,16,1024]{3,2,1,0:T(8,128)(2,1)S(1)}, u32[]{:S(2)}, u32[]{:S(2)}) %all-to-all-start.2) | async-done | bytes 524320 | tf_op jit(solution)/shard_map/all_to_all | solution.py:265
  94.7 0.0 copy-start.2
  94.7 3.7 %all-to-all-start.1 = ((bf16[8,2,16,1024]{3,2,1,0:T(8,128)(2,1)}), bf16[8,2,16,1024]{3,2,1,0:T(8,128)(2,1)S(1)}, u32[]{:S(2)}, u32[]{:S(2)}) async-start(bf16[8,2,16,1024]{3,2,1,0:T(8,128)(2,1)} %bitcast.46), calls=%async_computation.1 | async-start | bytes 1048576 | tf_op jit(solution)/shard_map/all_to_all | solution.py:274
  98.4 0.0 copy-done.2
  98.4 8.1 %shard_map.115 = bf16[256,1024]{1,0:T(8,128)(2,1)} custom-call(s32[1]{0:T(128)} %constant.0.clone.1.mix_ref, bf16[256,1024]{1,0:T(8,128)(2,1)} %bitcast.45, bf16[1024,1024]{1,0:T(8,128)(2,1)} %wq_ref.3, bf16[1024,512]{1,0:T(8,128)(2,1)} %wkv_ref.3, f32[1,1024]{1,0:T(1,128)} %broadcast_in_dim_tile.14.gq_ref, f32[1,256]{1,0:T(1,128)} %broadcast_in_dim_tile.15.gk_ref), custom_call_target="tpu_custom_call" | custom-call | flops 1879048192 | bytes 4199428 | tf_op jit(solution)/shard_map/pallas_call | solution.py:206
  106.5 6.5 %all-to-all-done.1 = bf16[8,2,16,1024]{3,2,1,0:T(8,128)(2,1)S(1)} async-done(((bf16[8,2,16,1024]{3,2,1,0:T(8,128)(2,1)}), bf16[8,2,16,1024]{3,2,1,0:T(8,128)(2,1)S(1)}, u32[]{:S(2)}, u32[]{:S(2)}) %all-to-all-start.1) | async-done | bytes 524320 | tf_op jit(solution)/shard_map/all_to_all | solution.py:274
  113.1 3.6 %all-to-all-start.3 = ((bf16[8,2,16,1024]{3,2,1,0:T(8,128)(2,1)}), bf16[8,2,16,1024]{3,2,1,0:T(8,128)(2,1)S(1)}, u32[]{:S(2)}, u32[]{:S(2)}) async-start(bf16[8,2,16,1024]{3,2,1,0:T(8,128)(2,1)} %bitcast.47), calls=%async_computation.3 | async-start | bytes 1048576 | tf_op jit(solution)/shard_map/all_to_all | solution.py:274
  116.7 0.8 copy.17
  117.5 13.8 %all-to-all-done.3 = bf16[8,2,16,1024]{3,2,1,0:T(8,128)(2,1)S(1)} async-done(((bf16[8,2,16,1024]{3,2,1,0:T(8,128)(2,1)}), bf16[8,2,16,1024]{3,2,1,0:T(8,128)(2,1)S(1)}, u32[]{:S(2)}, u32[]{:S(2)}) %all-to-all-start.3) | async-done | bytes 524320 | tf_op jit(solution)/shard_map/all_to_all | solution.py:274
  131.4 0.8 copy.19
  132.2 3.4 %shard_map.113 = bf16[256,1024]{1,0:T(8,128)(2,1)} custom-call(bf16[256,1024]{1,0:T(8,128)(2,1)} %bitcast.33, bf16[256,1024]{1,0:T(8,128)(2,1)} %bitcast.42, bf16[1024,1024]{1,0:T(8,128)(2,1)} %w_ref.7), custom_call_target="tpu_custom_call" | custom-call | flops 536870912 | bytes 3670016 | tf_op jit(solution)/shard_map/pallas_call | solution.py:206
  135.6 0.0 copy-start
  135.6 3.5 %shard_map.116 = bf16[256,1024]{1,0:T(8,128)(2,1)} custom-call(bf16[256,1024]{1,0:T(8,128)(2,1)} %bitcast.34, bf16[256,1024]{1,0:T(8,128)(2,1)} %bitcast.43, bf16[1024,1024]{1,0:T(8,128)(2,1)} %w_ref.7), custom_call_target="tpu_custom_call" | custom-call | flops 536870912 | bytes 3670016 | tf_op jit(solution)/shard_map/pallas_call | solution.py:206
  139.1 0.0 copy-done
  139.1 2.1 %pad_maximum_fusion = bf16[2,256,1024]{2,1,0:T(8,128)(2,1)} fusion(bf16[2,128,1024]{2,1,0:T(8,128)(2,1)} %bitcast.40, bf16[2,128,1024]{2,1,0:T(8,128)(2,1)S(1)} %bitcast.39), kind=kLoop, calls=%fused_computation | loop fusion | flops 2097152 | bytes 2097152 | tf_op jit(solution)/shard_map/concatenate | solution.py:280
  (5 shorter events, 0.0 us)
Async XLA Ops:
  4.8 15.1 %collective-permute-start = (bf16[2,256,512]{2,1,0:T(8,128)(2,1)}, bf16[2,256,512]{2,1,0:T(8,128)(2,1)S(1)}, u32[]{:S(2)}, u32[]{:S(2)}) collective-permute-start(bf16[2,256,512]{2,1,0:T(8,128)(2,1)} %bitcast.51), channel_id=1, source_target_pairs={{0,2},{1,3},{2,0},{3,1},{4,6},{5,7},{6,4},{7,5},{8,10},{9,11},{10,... | collective-permute-start | bytes 1572872 | tf_op jit(solution)/shard_map/ppermute | solution.py:228
  7.8 18.9 %collective-permute-start.1 = (bf16[2,256,512]{2,1,0:T(8,128)(2,1)}, bf16[2,256,512]{2,1,0:T(8,128)(2,1)S(1)}, u32[]{:S(2)}, u32[]{:S(2)}) collective-permute-start(bf16[2,256,512]{2,1,0:T(8,128)(2,1)} %bitcast.52), channel_id=1, source_target_pairs={{0,1},{1,0},{2,3},{3,2},{4,5},{5,4},{6,7},{7,6},{8,9},{9,8},{10,11... | collective-permute-start | bytes 1572872 | tf_op jit(solution)/shard_map/ppermute | solution.py:228
  19.9 6.7 %copy-start.4 = (bf16[2,256,512]{2,1,0:T(8,128)(2,1)}, bf16[2,256,512]{2,1,0:T(8,128)(2,1)S(1)}, u32[]{:S(2)}) copy-start(bf16[2,256,512]{2,1,0:T(8,128)(2,1)S(1)} %collective-permute-done.refs_5_) | copy-start | bytes 1572868
  19.9 6.8 %collective-permute-start.2 = (bf16[2,256,512]{2,1,0:T(8,128)(2,1)S(1)}, bf16[2,256,512]{2,1,0:T(8,128)(2,1)S(1)}, u32[]{:S(2)}, u32[]{:S(2)}) collective-permute-start(bf16[2,256,512]{2,1,0:T(8,128)(2,1)S(1)} %collective-permute-done.refs_5_), channel_id=1, source_target_pairs={{0,1},{1,0},{2,3},{3,2},{4,5},{5,4},{6,7},{7,6},{8,9},{9,8},{10,11... | collective-permute-start | bytes 1572872 | tf_op jit(solution)/shard_map/ppermute | solution.py:228
  26.7 0.8 copy-start.5
  26.7 1.0 copy-start.6
  47.9 26.4 %all-to-all-start = ((bf16[8,2,16,1024]{3,2,1,0:T(8,128)(2,1)}), bf16[8,2,16,1024]{3,2,1,0:T(8,128)(2,1)S(1)}, u32[]{:S(2)}, u32[]{:S(2)}) async-start(bf16[8,2,16,1024]{3,2,1,0:T(8,128)(2,1)} %bitcast.32), calls=%async_computation | async-start | bytes 1048576 | tf_op jit(solution)/shard_map/all_to_all | solution.py:265
  72.3 7.9 %copy-start.3 = (f32[2,64]{1,0:T(2,128)S(1)}, f32[2,64]{1,0:T(2,128)}, u32[]{:S(2)}) copy-start(f32[2,64]{1,0:T(2,128)} %param.21) | copy-start | bytes 1540
  74.2 7.4 %copy-start.1 = (bf16[8,2,16,1024]{3,2,1,0:T(8,128)(2,1)}, bf16[8,2,16,1024]{3,2,1,0:T(8,128)(2,1)S(1)}, u32[]{:S(2)}) copy-start(bf16[8,2,16,1024]{3,2,1,0:T(8,128)(2,1)S(1)} %all-to-all-done) | copy-start | bytes 1572868
  74.2 20.5 %all-to-all-start.2 = ((bf16[8,2,16,1024]{3,2,1,0:T(8,128)(2,1)}), bf16[8,2,16,1024]{3,2,1,0:T(8,128)(2,1)S(1)}, u32[]{:S(2)}, u32[]{:S(2)}) async-start(bf16[8,2,16,1024]{3,2,1,0:T(8,128)(2,1)} %bitcast.31), calls=%async_computation.2 | async-start | bytes 1048576 | tf_op jit(solution)/shard_map/all_to_all | solution.py:265
  94.7 3.7 %copy-start.2 = (bf16[8,2,16,1024]{3,2,1,0:T(8,128)(2,1)}, bf16[8,2,16,1024]{3,2,1,0:T(8,128)(2,1)S(1)}, u32[]{:S(2)}) copy-start(bf16[8,2,16,1024]{3,2,1,0:T(8,128)(2,1)S(1)} %all-to-all-done.2) | copy-start | bytes 1572868
  94.7 18.3 %all-to-all-start.1 = ((bf16[8,2,16,1024]{3,2,1,0:T(8,128)(2,1)}), bf16[8,2,16,1024]{3,2,1,0:T(8,128)(2,1)S(1)}, u32[]{:S(2)}, u32[]{:S(2)}) async-start(bf16[8,2,16,1024]{3,2,1,0:T(8,128)(2,1)} %bitcast.46), calls=%async_computation.1 | async-start | bytes 1048576 | tf_op jit(solution)/shard_map/all_to_all | solution.py:274
  113.1 18.3 %all-to-all-start.3 = ((bf16[8,2,16,1024]{3,2,1,0:T(8,128)(2,1)}), bf16[8,2,16,1024]{3,2,1,0:T(8,128)(2,1)S(1)}, u32[]{:S(2)}, u32[]{:S(2)}) async-start(bf16[8,2,16,1024]{3,2,1,0:T(8,128)(2,1)} %bitcast.47), calls=%async_computation.3 | async-start | bytes 1048576 | tf_op jit(solution)/shard_map/all_to_all | solution.py:274
  135.6 3.5 %copy-start = (bf16[256,1024]{1,0:T(8,128)(2,1)S(1)}, bf16[256,1024]{1,0:T(8,128)(2,1)}, u32[]{:S(2)}) copy-start(bf16[256,1024]{1,0:T(8,128)(2,1)} %shard_map.113) | copy-start | bytes 1572868

commit v2 on v0

v2 whole, which is shorter than its diff:
```python
import functools

import jax
import jax.numpy as jnp
from jax import lax
from jax.experimental import pallas as pl
from jax.experimental.pallas import tpu as pltpu
from jax.sharding import PartitionSpec as P


EPS = 1e-06
LOG2E = 1.4426950408889634
BF16 = jnp.bfloat16
F32 = jnp.float32


def dot(a, b):
    return jnp.dot(a, b, preferred_element_type=F32)


def row_rms(x, gain):
    x = x.astype(F32)
    return x * lax.rsqrt(jnp.mean(x * x, axis=-1, keepdims=True) + EPS) * gain


def column(row):
    n = row.shape[1]
    i = lax.broadcasted_iota(jnp.int32, (n, n), 0)
    j = lax.broadcasted_iota(jnp.int32, (n, n), 1)
    return jnp.sum(jnp.where(i == j, row, 0.0), axis=1, keepdims=True)


def feature_rms(x, gain):
    n = gain.shape[0]
    y = x.reshape(x.shape[0] // n, n, x.shape[1])
    total = jnp.sum(y * y, axis=1, keepdims=True)
    return (y * lax.rsqrt(total * (1.0 / n) + EPS) * gain[None]).reshape(x.shape)


def at(start, size):
    return pl.ds(pl.multiple_of(start, size), size)


def padded(q, odd):
    zero = jnp.zeros_like(q)
    return jnp.concatenate([zero, q] if odd else [q, zero], axis=0)


def query_columns(q_ref, lead, g, group, head, odd):
    heads = [q_ref[(*lead, at((g * group + i) * head, head), slice(None))] for i in range(group)]
    return jnp.concatenate([padded(q, odd) for q in heads], axis=1)


def keyval_kernel(x_ref, norm_ref, w_ref, gain_ref, normed_ref, kv_ref):
    frames, rows = kv_ref.shape[0], x_ref.shape[0] // kv_ref.shape[0]
    half = w_ref.shape[1] // 2
    gain = column(gain_ref[1:2, :])
    for f in range(frames):
        part = slice(f * rows, (f + 1) * rows)
        normed = row_rms(x_ref[part], norm_ref[...]).astype(BF16)
        normed_ref[part] = normed
        kv = dot(normed, w_ref[...]).T
        kv_ref[f, :rows] = feature_rms(kv[:half], gain).T.astype(BF16)
        kv_ref[f, rows:] = kv[half:].astype(BF16)


def over_key_heads(frames, kv_heads, score, finish, bufs):
    pairs = kv_heads // 2
    total = frames * pairs

    def split(step):
        return step // pairs, (step % pairs) * 2

    score(0, 0, False, bufs[0])

    def step(n, carry):
        f, g = split(n)
        f_next, g_next = split(jnp.minimum(n + 1, total - 1))
        score(f, g + 1, True, bufs[1])
        finish(f, g, bufs[0])
        score(f_next, g_next, False, bufs[0])
        finish(f, g + 1, bufs[1])
        return carry

    lax.fori_loop(0, total, step, 0)


def near_kernel(head, chunks, pieces, x_ref, w_ref, gain_ref, *refs):
    kv_refs, refs = refs[:pieces], refs[pieces:]
    (q_refs, o_refs, ml_refs), (q_buf, s0, s1) = (refs[i * chunks : (i + 1) * chunks] for i in range(3)), refs[3 * chunks :]
    frames, rows = kv_refs[0].shape[0], x_ref.shape[0] // kv_refs[0].shape[0]
    half = kv_refs[0].shape[2]
    heads, kv_heads = w_ref.shape[1] // head, half // head
    group, part, wide = heads // kv_heads, rows // chunks, 2 * head
    gain = column(gain_ref[0:1, :])
    for f in range(frames):
        q = dot(x_ref[f * rows : (f + 1) * rows], w_ref[...]).T
        q = (feature_rms(q, gain).astype(BF16).astype(F32) * head**-0.5).astype(BF16)
        q_buf[f] = q
        for c in range(chunks):
            q_refs[c][f] = q[:, c * part : (c + 1) * part]

    def score(f, g, odd, buf):
        keys = jnp.concatenate([ref[f, :rows, at((g // 2) * wide, wide)] for ref in kv_refs], axis=0)
        buf[...] = dot(keys, query_columns(q_buf, (f,), g, group, head, odd))

    def finish(f, g, buf):
        s = buf[...]
        largest = jnp.max(s, axis=0, keepdims=True)
        e = jnp.exp2((s - largest) * LOG2E)
        total = jnp.sum(e, axis=0, keepdims=True)
        values = jnp.concatenate([ref[f, at(rows + g * head, head), :] for ref in kv_refs], axis=1)
        out = dot(values, e.astype(BF16))
        for i in range(group):
            h = g * group + i
            for c in range(chunks):
                lanes = slice(i * rows + c * part, i * rows + (c + 1) * part)
                o_refs[c][f, at(h * head, head), :] = out[:, lanes]
                ml_refs[c][f, pl.ds(h, 1), :] = largest[:, lanes]
                ml_refs[c][f, pl.ds(heads + h, 1), :] = total[:, lanes]

    over_key_heads(frames, kv_heads, score, finish, (s0, s1))


def far_kernel(head, spots, pieces, q_ref, o_ref, ml_ref, x_ref, norm_ref, w_hbm, *refs):
    kv_refs, (stream_ref, timed_ref, att, s0, s1, w_ref, sem) = refs[:pieces], refs[pieces:]
    copy = pltpu.make_async_copy(w_hbm, w_ref, sem)
    copy.start()
    frames, rows, part = q_ref.shape[0], kv_refs[0].shape[1] - kv_refs[0].shape[2], q_ref.shape[2]
    half = kv_refs[0].shape[2]
    heads, kv_heads = q_ref.shape[1] // head, half // head
    group, wide = heads // kv_heads, 2 * head

    def score(f, g, odd, buf):
        keys = jnp.concatenate([ref[f, :rows, at((g // 2) * wide, wide)] for ref in kv_refs], axis=0)
        buf[...] = dot(keys, query_columns(q_ref, (f,), g, group, head, odd))

    def finish(f, g, buf):
        s = buf[...]
        before = jnp.concatenate([ml_ref[f, pl.ds(g * group + i, 1), :] for i in range(group)], axis=1)
        total = jnp.concatenate([ml_ref[f, pl.ds(heads + g * group + i, 1), :] for i in range(group)], axis=1)
        out = jnp.concatenate([o_ref[f, at((g * group + i) * head, head), :] for i in range(group)], axis=1)
        largest = jnp.maximum(before, jnp.max(s, axis=0, keepdims=True))
        scale = jnp.exp2((before - largest) * LOG2E)
        e = jnp.exp2((s - largest) * LOG2E)
        total = total * scale + jnp.sum(e, axis=0, keepdims=True)
        values = jnp.concatenate([ref[f, at(rows + g * head, head), :] for ref in kv_refs], axis=1)
        out = ((out * scale + dot(values, e.astype(BF16))) / total).astype(BF16)
        for i in range(group):
            att[f, at((g * group + i) * head, head), :] = out[:, i * part : (i + 1) * part]

    over_key_heads(frames, kv_heads, score, finish, (s0, s1))
    copy.wait()
    for f in range(frames):
        update = dot(att[f].T, w_ref[...])
        stream = (x_ref[f].astype(F32) + update).astype(BF16)
        timed = row_rms(stream, norm_ref[...]).astype(BF16)
        if spots:
            for d in range(part // spots):
                stream_ref[d, f] = stream[d * spots : (d + 1) * spots]
                timed_ref[d, f] = timed[d * spots : (d + 1) * spots]
        else:
            stream_ref[f] = stream
            timed_ref[f] = timed


def time_kernel(head, spots, x_ref, wkv_ref, wq_hbm, gain_ref, out_ref, wq_ref, q_buf, k_buf, v_buf, bias, att, sem):
    copy = pltpu.make_async_copy(wq_hbm, wq_ref, sem)
    copy.start()
    rows = x_ref.shape[0]
    half = wkv_ref.shape[1] // 2
    kv_heads = half // head
    group, wide = wq_ref.shape[1] // head // kv_heads, 2 * head
    x = x_ref[...]
    kv = dot(x, wkv_ref[...]).T
    k_buf[...] = feature_rms(kv[:half], column(gain_ref[1:2, :])).T.astype(BF16)
    v_buf[...] = kv[half:].astype(BF16)

    def place(axis):
        n = lax.broadcasted_iota(jnp.int32, (rows, rows), axis)
        return n // spots, n % spots

    (frame_k, spot_k), (frame_q, spot_q) = place(0), place(1)
    bias[...] = jnp.where((spot_q == spot_k) & (frame_q >= frame_k), 0.0, -1e30)
    copy.wait()
    q = feature_rms(dot(x, wq_ref[...]).T, column(gain_ref[0:1, :]))
    q_buf[...] = (q.astype(BF16).astype(F32) * head**-0.5).astype(BF16)
    for g in range(kv_heads):
        keys = k_buf[:, (g // 2) * wide : (g // 2 + 1) * wide]
        s = dot(keys, query_columns(q_buf, (), g, group, head, g % 2 == 1))
        s = jnp.concatenate([s[:, i * rows : (i + 1) * rows] + bias[...] for i in range(group)], axis=1)
        largest = jnp.max(s, axis=0, keepdims=True)
        e = jnp.exp2((s - largest) * LOG2E)
        total = jnp.sum(e, axis=0, keepdims=True)
        out = (dot(v_buf[g * head : (g + 1) * head], e.astype(BF16)) / total).astype(BF16)
        for i in range(group):
            h = g * group + i
            att[h * head : (h + 1) * head] = out[:, i * rows : (i + 1) * rows]
    out_ref[...] = att[...].T


def final_kernel(spots, a_ref, x_ref, w_ref, *refs):
    out_ref = refs[-1]
    mixed = (x_ref[...].astype(F32) + dot(a_ref[...], w_ref[...])).astype(BF16)
    frames, part = out_ref.shape[0], out_ref.shape[1]
    for f in range(frames):
        if spots:
            for d in range(part // spots):
                first = (d * frames + f) * spots
                out_ref[f, d * spots : (d + 1) * spots] = mixed[first : first + spots]
        else:
            out_ref[f] = mixed[f * part : (f + 1) * part]


def call(kernel, args, outs, flops, scratch=(), anywhere=(), blocks={}, out_blocks={}, alias={}):
    moved = sum(a.size * a.dtype.itemsize for a in args) + sum(s.size * s.dtype.itemsize for s in outs)

    def spec(shape, block):
        if block is None:
            return pl.BlockSpec(shape, lambda i: (0,) * len(shape))
        return pl.BlockSpec(*block)

    in_specs = [pl.BlockSpec(memory_space=pl.ANY) if i in anywhere else spec(a.shape, blocks.get(i)) for i, a in enumerate(args)]
    return pl.pallas_call(
        kernel,
        grid=(1,),
        out_shape=outs,
        in_specs=in_specs,
        out_specs=[spec(s.shape, out_blocks.get(i)) for i, s in enumerate(outs)],
        scratch_shapes=list(scratch),
        input_output_aliases=alias,
        compiler_params=pltpu.CompilerParams(vmem_limit_bytes=56 * 1024 * 1024),
        cost_estimate=pl.CostEstimate(flops=int(flops), bytes_accessed=int(moved), transcendentals=0),
    )(*args)


def shaped(*dims, dtype=BF16):
    return jax.ShapeDtypeStruct(dims, dtype)


def permuted(x, axis, size, bit):
    return lax.ppermute(x, axis, [(i, i ^ bit) for i in range(size)])


def make_body(mesh):
    frame_devices, band_devices = mesh.shape["frames"], mesh.shape["band"]
    chunks = 2

    def body(tokens, norm_space, query_space, keyval_space, out_space, qk_space, norm_time, query_time, keyval_time, out_time, qk_time):
        frames, rows, width = tokens.shape
        head = qk_space.shape[1]
        q_width, half = query_space.shape[1], keyval_space.shape[1] // 2
        heads = q_width // head
        flat, part = frames * rows, rows // chunks
        spots = part // frame_devices
        aligned = spots if spots % 16 == 0 else 0
        norm_space, norm_time = norm_space[None], norm_time[None]

        normed, kv = call(
            keyval_kernel,
            (tokens.reshape(flat, width), norm_space, keyval_space, qk_space),
            [shaped(flat, width), shaped(frames, rows + half, half)],
            4 * flat * width * half,
        )
        top = band_devices // 2
        far = [permuted(kv, "band", band_devices, top)]
        near, bit = [kv], top // 2
        while bit:
            near += [permuted(p, "band", band_devices, bit) for p in near]
            far += [permuted(p, "band", band_devices, bit) for p in far]
            bit //= 2

        near_keys = rows * len(near)
        outs = call(
            functools.partial(near_kernel, head, chunks, len(near)),
            (normed, query_space, qk_space, *near),
            [shaped(frames, q_width, part)] * chunks
            + [shaped(frames, q_width, part, dtype=F32)] * chunks
            + [shaped(frames, 2 * heads, part, dtype=F32)] * chunks,
            2 * flat * width * q_width + 8 * flat * near_keys * q_width,
            [pltpu.VMEM((frames, q_width, rows), BF16)] + [pltpu.VMEM((near_keys, rows * (q_width // half)), F32)] * 2,
        )
        far_keys = rows * len(far)
        mixed = None
        for c in range(chunks):
            piece = (frame_devices, frames, spots, width)
            layout = piece if aligned else (frames, part, width)
            stream, timed = call(
                functools.partial(far_kernel, head, aligned, len(far)),
                (outs[c], outs[chunks + c], outs[2 * chunks + c], tokens, norm_time, out_space, *far),
                [shaped(*layout), shaped(*layout)],
                frames * part * (8 * far_keys * q_width + 2 * q_width * width),
                [pltpu.VMEM((frames, q_width, part), BF16)]
                + [pltpu.VMEM((far_keys, part * (q_width // half)), F32)] * 2
                + [pltpu.VMEM((q_width, width), BF16), pltpu.SemaphoreType.DMA],
                anywhere=(5,),
                blocks={3: ((frames, part, width), lambda i, c=c: (0, c, 0))},
            )
            if not aligned:
                timed = timed.reshape(frames, frame_devices, spots, width).swapaxes(0, 1)
            moved = lax.all_to_all(timed, "frames", 0, 0)
            n = frame_devices * frames * spots
            (att,) = call(
                functools.partial(time_kernel, head, spots),
                (moved.reshape(n, width), keyval_time, query_time, qk_time),
                [shaped(n, q_width)],
                2 * n * width * (q_width + 2 * half) + 16 * n * n * q_width,
                [
                    pltpu.VMEM((width, q_width), BF16),
                    pltpu.VMEM((q_width, n), BF16),
                    pltpu.VMEM((n, half), BF16),
                    pltpu.VMEM((half, n), BF16),
                    pltpu.VMEM((n, n), F32),
                    pltpu.VMEM((q_width, n), BF16),
                    pltpu.SemaphoreType.DMA,
                ],
                anywhere=(2,),
            )
            back = lax.all_to_all(att.reshape(frame_devices, frames, spots, q_width), "frames", 0, 0)
            if not aligned:
                back = back.swapaxes(0, 1)
            args = (back.reshape(n, q_width), stream.reshape(n, width), out_time)
            (mixed,) = call(
                functools.partial(final_kernel, aligned),
                args if mixed is None else (*args, mixed),
                [shaped(frames, rows, width)],
                2 * n * width * q_width,
                anywhere=(3,),
                out_blocks={0: ((frames, part, width), lambda i, c=c: (0, c, 0))},
                alias={} if mixed is None else {3: 0},
            )
        return mixed

    return body


def solution(mesh):
    placed = (P("frames", "band", None),) + (P(),) * 10
    body = make_body(mesh)

    return jax.shard_map(body, mesh=mesh, in_specs=placed, out_specs=P("frames", "band", None), check_vma=False)
```

time: 224 us -> 120 us (0.54)
  matrix products: 54 us -> 0 us
  Pallas kernels: 0 us -> 48.9 us
  local copies, waits for them, and re-layouts: 46.6 us -> 2.43 us
  blocking collectives: 29.6 us -> 0 us
  other arithmetic: 26.1 us -> 0 us
  starting transfers between devices: 5.56 us -> 20 us
  between operations: 13.8 us -> 0.09 us
    dot_general x12 -> x0, matrix products: 54 us -> none  [the longest x3 23.1 us: attend(): jnp.einsum('nkgd,mkd->kgnm', grouped, key_heads, preferred_element_type=j...]
    pallas_call x0 -> x8, Pallas kernels: none -> 48.9 us  [call(): pl.pallas_call(kernel, grid=(1,), out_shape=outs, in_specs=in_specs, out_...]
    all_to_all x1 -> x0, blocking collectives: 29.6 us -> none  [body(): lax.all_to_all(time_att, 'frames', split_axis=0, concat_axis=1, tiled=True)]
    all_gather x2 -> x0, waiting for transfers between devices: 25.1 us -> none  [the longest x1 18.4 us: body(): lax.all_gather(values, 'band', axis=1, tiled=True)]
    reduce_sum x6 -> x0, other arithmetic: 20.6 us -> none  [the longest x3 18.8 us: attend(): totals = jnp.sum(expos, axis=-1)]
    convert_element_type x5 -> x0, local copies, waits for them, and re-layouts: 13.5 us -> none  [the longest x3 7.23 us: project(): queries.reshape(row_count, -1).astype(jnp.bfloat16)]
    all_to_all x1 -> x4, waiting for transfers between devices: 22.1 us -> 35.4 us  [the longest x2 19.3 us: body(): lax.all_to_all(att.reshape(frame_devices, frames, spots, q_width), 'frame...]
    ppermute x0 -> x3, waiting for transfers between devices: none -> 12.1 us  [permuted(): return lax.ppermute(x, axis, [(i, i ^ bit) for i in range(size)])]
  transfers between devices with their start and end apart: 3 -> 7, of which waited for: 3 -> 5; matrix products, arithmetic and copies ran while one was open for 7% -> 0% of each run, Pallas kernels for 0% -> 29%
where the time goes in v2:
time: 120 us; the launch traced here: 119 us
  Pallas kernels  48.9 us (41%)
  waiting for transfers between devices  47.5 us (40%)
  starting transfers between devices  20 us (17%)
  local copies, waits for them, and re-layouts  2.43 us (2%)
    pallas_call x8, Pallas kernels, call(): pl.pallas_call(kernel, grid=(1,), out_shape=outs, in_specs=in_specs, out_...  48.9 us
    all_to_all x2, waiting for transfers between devices, body(): lax.all_to_all(att.reshape(frame_devices, frames, spots, q_width), 'frame...  19.3 us
    all_to_all x2, waiting for transfers between devices, body(): moved = lax.all_to_all(timed, 'frames', 0, 0)  16.1 us
    ppermute x3, waiting for transfers between devices, permuted(): return lax.ppermute(x, axis, [(i, i ^ bit) for i in range(size)])  12.1 us
    all_to_all x2, starting transfers between devices, body(): moved = lax.all_to_all(timed, 'frames', 0, 0)  9.72 us
    all_to_all x2, starting transfers between devices, body(): lax.all_to_all(att.reshape(frame_devices, frames, spots, q_width), 'frame...  7.31 us
    ppermute x3, starting transfers between devices, permuted(): return lax.ppermute(x, axis, [(i, i ^ bit) for i in range(size)])  2.98 us
    unnamed x14, local copies, waits for them, and re-layouts  2.43 us
  transfers between devices with their start and end apart: 7, of which 5 were waited for; matrix products, arithmetic and copies ran while one was open for 0% of the time, Pallas kernels for 29%

profile of v2, /device:TPU:0, one launch (start us, length us, event | category | flops | bytes accessed | tf_op | source)
XLA Modules:
  0.0 119.0 jit_solution(5581639194918517909)
XLA Ops:
  0.0 3.4 %shard_map.109 = (bf16[512,1024]{1,0:T(8,128)(2,1)}, bf16[2,512,256]{2,1,0:T(8,128)(2,1)}) custom-call(bf16[512,1024]{1,0:T(8,128)(2,1)} %bitcast.13, f32[1,1024]{1,0:T(1,128)} %bitcast.20, bf16[1024,512]{1,0:T(8,128)(2,1)} %w_ref.4, f32[2,64]{1,0:T(2,128)} %gain_ref.5), custom_call_target="tpu_custom_call" | custom-call | flops 536870912 | bytes 3674624 | tf_op jit(solution)/shard_map/pallas_call | solution.py:224
  3.4 3.0 %collective-permute-start.1 = (bf16[2,512,256]{2,1,0:T(8,128)(2,1)}, bf16[2,512,256]{2,1,0:T(8,128)(2,1)S(1)}, u32[]{:S(2)}, u32[]{:S(2)}) collective-permute-start(bf16[2,512,256]{2,1,0:T(8,128)(2,1)} %get-tuple-element.18.refs_0_), channel_id=1, source_target_pairs={{0,2},{1,3},{2,0},{3,1},{4,6},{5,7},{6,4},{7,5},{8,10},{9,11},{10,... | collective-permute-start | bytes 1572872 | tf_op jit(solution)/shard_map/ppermute | solution.py:242
  6.4 0.0 collective-permute-start
  6.4 12.1 %collective-permute-done.1.refs_0_ = bf16[2,512,256]{2,1,0:T(8,128)(2,1)S(1)} collective-permute-done((bf16[2,512,256]{2,1,0:T(8,128)(2,1)}, bf16[2,512,256]{2,1,0:T(8,128)(2,1)S(1)}, u32[]{:S(2)}, u32[]{:S(2)}) %collective-permute-start.1) | collective-permute-done | bytes 524320 | tf_op jit(solution)/shard_map/ppermute | solution.py:242
  18.5 0.0 copy-start.4
  18.5 0.0 collective-permute-start.2
  18.5 0.0 collective-permute-done.refs_1_
  18.5 0.0 copy-start.6
  18.5 0.8 copy-done.6
  19.4 11.2 %shard_map.110 = (bf16[2,1024,128]{2,1,0:T(8,128)(2,1)}, bf16[2,1024,128]{2,1,0:T(8,128)(2,1)}, f32[2,1024,128]{2,1,0:T(8,128)}, f32[2,1024,128]{2,1,0:T(8,128)}...) custom-call(bf16[512,1024]{1,0:T(8,128)(2,1)} %get-tuple-element.17.x_ref, bf16[1024,1024]{1,0:T(8,128)(2,1)} %w_ref.5, ...), custom_call_target="tpu_custom_call" | custom-call | flops 3221225472 | bytes 7406080 | tf_op jit(solution)/shard_map/pallas_call | solution.py:224
  30.6 0.0 copy-done.4
  30.6 0.0 collective-permute-done.2.refs_1_
  30.6 0.0 copy-start.5
  30.6 0.8 copy-done.5
  31.4 7.2 %shard_map.113 = (bf16[8,2,16,1024]{3,2,1,0:T(8,128)(2,1)}, bf16[8,2,16,1024]{3,2,1,0:T(8,128)(2,1)}) custom-call(bf16[2,1024,128]{2,1,0:T(8,128)(2,1)} %get-tuple-element.24.q_ref, f32[2,1024,128]{2,1,0:T(8,128)} %get-tuple-element.25.o_ref, f32[2,32,128]{2,1,0:T(8,128)} %get-tuple-element.26.ml_ref, bf16[2,256,1024]{2,1,0:T(8,128)(2,1)} %x_ref.3, ...), custom_call_target="tpu_custom_call" | custom-call | flops 1610612736 | bytes 6852608 | tf_op jit(solution)/shard_map/pallas_call | solution.py:224
  38.6 6.1 %all-to-all-start.2 = ((bf16[8,2,16,1024]{3,2,1,0:T(8,128)(2,1)}), bf16[8,2,16,1024]{3,2,1,0:T(8,128)(2,1)S(1)}, u32[]{:S(2)}, u32[]{:S(2)}) async-start(bf16[8,2,16,1024]{3,2,1,0:T(8,128)(2,1)} %get-tuple-element.27), calls=%async_computation.2 | async-start | bytes 1048576 | tf_op jit(solution)/shard_map/all_to_all | solution.py:301
  44.7 7.2 %shard_map.111 = (bf16[8,2,16,1024]{3,2,1,0:T(8,128)(2,1)}, bf16[8,2,16,1024]{3,2,1,0:T(8,128)(2,1)}) custom-call(bf16[2,1024,128]{2,1,0:T(8,128)(2,1)} %get-tuple-element.19.q_ref, f32[2,1024,128]{2,1,0:T(8,128)} %get-tuple-element.20.o_ref, f32[2,32,128]{2,1,0:T(8,128)} %get-tuple-element.21.ml_ref, bf16[2,256,1024]{2,1,0:T(8,128)(2,1)} %x_ref.3, ...), custom_call_target="tpu_custom_call" | custom-call | flops 1610612736 | bytes 6852608 | tf_op jit(solution)/shard_map/pallas_call | solution.py:224
  51.9 7.9 %all-to-all-done.2 = bf16[8,2,16,1024]{3,2,1,0:T(8,128)(2,1)S(1)} async-done(((bf16[8,2,16,1024]{3,2,1,0:T(8,128)(2,1)}), bf16[8,2,16,1024]{3,2,1,0:T(8,128)(2,1)S(1)}, u32[]{:S(2)}, u32[]{:S(2)}) %all-to-all-start.2) | async-done | bytes 524320 | tf_op jit(solution)/shard_map/all_to_all | solution.py:301
  59.8 0.0 copy-start.2
  59.8 3.6 %all-to-all-start = ((bf16[8,2,16,1024]{3,2,1,0:T(8,128)(2,1)}), bf16[8,2,16,1024]{3,2,1,0:T(8,128)(2,1)S(1)}, u32[]{:S(2)}, u32[]{:S(2)}) async-start(bf16[8,2,16,1024]{3,2,1,0:T(8,128)(2,1)} %get-tuple-element.22), calls=%async_computation | async-start | bytes 1048576 | tf_op jit(solution)/shard_map/all_to_all | solution.py:301
  63.4 0.0 copy-done.2
  63.4 6.5 %shard_map.114 = bf16[256,1024]{1,0:T(8,128)(2,1)} custom-call(bf16[256,1024]{1,0:T(8,128)(2,1)} %bitcast.15, bf16[1024,512]{1,0:T(8,128)(2,1)} %wkv_ref.3, bf16[1024,1024]{1,0:T(8,128)(2,1)} %wq_hbm.3, f32[2,64]{1,0:T(2,128)} %gain_ref.7), custom_call_target="tpu_custom_call" | custom-call | flops 1879048192 | bytes 4194816 | tf_op jit(solution)/shard_map/pallas_call | solution.py:224
  69.9 8.2 %all-to-all-done = bf16[8,2,16,1024]{3,2,1,0:T(8,128)(2,1)S(1)} async-done(((bf16[8,2,16,1024]{3,2,1,0:T(8,128)(2,1)}), bf16[8,2,16,1024]{3,2,1,0:T(8,128)(2,1)S(1)}, u32[]{:S(2)}, u32[]{:S(2)}) %all-to-all-start) | async-done | bytes 524320 | tf_op jit(solution)/shard_map/all_to_all | solution.py:301
  78.1 0.0 copy-start.3
  78.1 3.7 %all-to-all-start.3 = ((bf16[8,2,16,1024]{3,2,1,0:T(8,128)(2,1)}), bf16[8,2,16,1024]{3,2,1,0:T(8,128)(2,1)S(1)}, u32[]{:S(2)}, u32[]{:S(2)}) async-start(bf16[8,2,16,1024]{3,2,1,0:T(8,128)(2,1)} %bitcast.18), calls=%async_computation.3 | async-start | bytes 1048576 | tf_op jit(solution)/shard_map/all_to_all | solution.py:319
  81.8 0.0 copy-done.3
  81.8 6.5 %shard_map.112 = bf16[256,1024]{1,0:T(8,128)(2,1)} custom-call(bf16[256,1024]{1,0:T(8,128)(2,1)} %bitcast.16, bf16[1024,512]{1,0:T(8,128)(2,1)} %wkv_ref.3, bf16[1024,1024]{1,0:T(8,128)(2,1)} %wq_hbm.3, f32[2,64]{1,0:T(2,128)} %gain_ref.7), custom_call_target="tpu_custom_call" | custom-call | flops 1879048192 | bytes 4194816 | tf_op jit(solution)/shard_map/pallas_call | solution.py:224
  88.3 8.1 %all-to-all-done.3 = bf16[8,2,16,1024]{3,2,1,0:T(8,128)(2,1)S(1)} async-done(((bf16[8,2,16,1024]{3,2,1,0:T(8,128)(2,1)}), bf16[8,2,16,1024]{3,2,1,0:T(8,128)(2,1)S(1)}, u32[]{:S(2)}, u32[]{:S(2)}) %all-to-all-start.3) | async-done | bytes 524320 | tf_op jit(solution)/shard_map/all_to_all | solution.py:319
  96.4 0.0 copy-start.1
  96.4 3.6 %all-to-all-start.1 = ((bf16[8,2,16,1024]{3,2,1,0:T(8,128)(2,1)}), bf16[8,2,16,1024]{3,2,1,0:T(8,128)(2,1)S(1)}, u32[]{:S(2)}, u32[]{:S(2)}) async-start(bf16[8,2,16,1024]{3,2,1,0:T(8,128)(2,1)} %bitcast.17), calls=%async_computation.1 | async-start | bytes 1048576 | tf_op jit(solution)/shard_map/all_to_all | solution.py:319
  100.1 0.0 copy-done.1
  100.1 3.4 %shard_map.115.refs_0_ = bf16[2,256,1024]{2,1,0:T(8,128)(2,1)} custom-call(bf16[256,1024]{1,0:T(8,128)(2,1)} %bitcast.12, bf16[256,1024]{1,0:T(8,128)(2,1)} %bitcast.19, bf16[1024,1024]{1,0:T(8,128)(2,1)} %w_ref.7), custom_call_target="tpu_custom_call" | custom-call | flops 536870912 | bytes 4194304 | tf_op jit(solution)/shard_map/pallas_call | solution.py:224
  103.5 11.2 %all-to-all-done.1 = bf16[8,2,16,1024]{3,2,1,0:T(8,128)(2,1)S(1)} async-done(((bf16[8,2,16,1024]{3,2,1,0:T(8,128)(2,1)}), bf16[8,2,16,1024]{3,2,1,0:T(8,128)(2,1)S(1)}, u32[]{:S(2)}, u32[]{:S(2)}) %all-to-all-start.1) | async-done | bytes 524320 | tf_op jit(solution)/shard_map/all_to_all | solution.py:319
  114.7 0.0 copy-start
  114.7 0.8 copy-done
  115.5 3.4 %shard_map.116 = bf16[2,256,1024]{2,1,0:T(8,128)(2,1)} custom-call(bf16[256,1024]{1,0:T(8,128)(2,1)} %bitcast.11, bf16[256,1024]{1,0:T(8,128)(2,1)} %bitcast.14, bf16[1024,1024]{1,0:T(8,128)(2,1)} %w_ref.7, bf16[2,256,1024]{2,1,0:T(8,128)(2,1)} %shard_map.115.refs_0_), custom_call_target="tpu_custom_call", output_to_operand_aliasing={{}: (3, {})} | custom-call | flops 536870912 | bytes 5242880 | tf_op jit(solution)/shard_map/pallas_call | solution.py:224
Async XLA Ops:
  3.4 15.1 %collective-permute-start.1 = (bf16[2,512,256]{2,1,0:T(8,128)(2,1)}, bf16[2,512,256]{2,1,0:T(8,128)(2,1)S(1)}, u32[]{:S(2)}, u32[]{:S(2)}) collective-permute-start(bf16[2,512,256]{2,1,0:T(8,128)(2,1)} %get-tuple-element.18.refs_0_), channel_id=1, source_target_pairs={{0,2},{1,3},{2,0},{3,1},{4,6},{5,7},{6,4},{7,5},{8,10},{9,11},{10,... | collective-permute-start | bytes 1572872 | tf_op jit(solution)/shard_map/ppermute | solution.py:242
  6.4 12.1 %collective-permute-start = (bf16[2,512,256]{2,1,0:T(8,128)(2,1)}, bf16[2,512,256]{2,1,0:T(8,128)(2,1)S(1)}, u32[]{:S(2)}, u32[]{:S(2)}) collective-permute-start(bf16[2,512,256]{2,1,0:T(8,128)(2,1)} %get-tuple-element.18.refs_0_), channel_id=1, source_target_pairs={{0,1},{1,0},{2,3},{3,2},{4,5},{5,4},{6,7},{7,6},{8,9},{9,8},{10,11... | collective-permute-start | bytes 1572872 | tf_op jit(solution)/shard_map/ppermute | solution.py:242
  18.5 12.1 %copy-start.4 = (bf16[2,512,256]{2,1,0:T(8,128)(2,1)}, bf16[2,512,256]{2,1,0:T(8,128)(2,1)S(1)}, u32[]{:S(2)}) copy-start(bf16[2,512,256]{2,1,0:T(8,128)(2,1)S(1)} %collective-permute-done.1.refs_0_) | copy-start | bytes 1572868
  18.5 12.1 %collective-permute-start.2 = (bf16[2,512,256]{2,1,0:T(8,128)(2,1)S(1)}, bf16[2,512,256]{2,1,0:T(8,128)(2,1)S(1)}, u32[]{:S(2)}, u32[]{:S(2)}) collective-permute-start(bf16[2,512,256]{2,1,0:T(8,128)(2,1)S(1)} %collective-permute-done.1.refs_0_), channel_id=1, source_target_pairs={{0,1},{1,0},{2,3},{3,2},{4,5},{5,4},{6,7},{7,6},{8,9},{9,8},{10,11... | collective-permute-start | bytes 1572872 | tf_op jit(solution)/shard_map/ppermute | solution.py:242
  18.5 0.8 copy-start.6
  30.6 0.8 copy-start.5
  38.6 21.2 %all-to-all-start.2 = ((bf16[8,2,16,1024]{3,2,1,0:T(8,128)(2,1)}), bf16[8,2,16,1024]{3,2,1,0:T(8,128)(2,1)S(1)}, u32[]{:S(2)}, u32[]{:S(2)}) async-start(bf16[8,2,16,1024]{3,2,1,0:T(8,128)(2,1)} %get-tuple-element.27), calls=%async_computation.2 | async-start | bytes 1048576 | tf_op jit(solution)/shard_map/all_to_all | solution.py:301
  59.8 3.6 %copy-start.2 = (bf16[8,2,16,1024]{3,2,1,0:T(8,128)(2,1)}, bf16[8,2,16,1024]{3,2,1,0:T(8,128)(2,1)S(1)}, u32[]{:S(2)}) copy-start(bf16[8,2,16,1024]{3,2,1,0:T(8,128)(2,1)S(1)} %all-to-all-done.2) | copy-start | bytes 1572868
  59.8 18.3 %all-to-all-start = ((bf16[8,2,16,1024]{3,2,1,0:T(8,128)(2,1)}), bf16[8,2,16,1024]{3,2,1,0:T(8,128)(2,1)S(1)}, u32[]{:S(2)}, u32[]{:S(2)}) async-start(bf16[8,2,16,1024]{3,2,1,0:T(8,128)(2,1)} %get-tuple-element.22), calls=%async_computation | async-start | bytes 1048576 | tf_op jit(solution)/shard_map/all_to_all | solution.py:301
  78.1 3.7 %copy-start.3 = (bf16[8,2,16,1024]{3,2,1,0:T(8,128)(2,1)}, bf16[8,2,16,1024]{3,2,1,0:T(8,128)(2,1)S(1)}, u32[]{:S(2)}) copy-start(bf16[8,2,16,1024]{3,2,1,0:T(8,128)(2,1)S(1)} %all-to-all-done) | copy-start | bytes 1572868
  78.1 18.3 %all-to-all-start.3 = ((bf16[8,2,16,1024]{3,2,1,0:T(8,128)(2,1)}), bf16[8,2,16,1024]{3,2,1,0:T(8,128)(2,1)S(1)}, u32[]{:S(2)}, u32[]{:S(2)}) async-start(bf16[8,2,16,1024]{3,2,1,0:T(8,128)(2,1)} %bitcast.18), calls=%async_computation.3 | async-start | bytes 1048576 | tf_op jit(solution)/shard_map/all_to_all | solution.py:319
  96.4 3.6 %copy-start.1 = (bf16[8,2,16,1024]{3,2,1,0:T(8,128)(2,1)}, bf16[8,2,16,1024]{3,2,1,0:T(8,128)(2,1)S(1)}, u32[]{:S(2)}) copy-start(bf16[8,2,16,1024]{3,2,1,0:T(8,128)(2,1)S(1)} %all-to-all-done.3) | copy-start | bytes 1572868
  96.4 18.3 %all-to-all-start.1 = ((bf16[8,2,16,1024]{3,2,1,0:T(8,128)(2,1)}), bf16[8,2,16,1024]{3,2,1,0:T(8,128)(2,1)S(1)}, u32[]{:S(2)}, u32[]{:S(2)}) async-start(bf16[8,2,16,1024]{3,2,1,0:T(8,128)(2,1)} %bitcast.17), calls=%async_computation.1 | async-start | bytes 1048576 | tf_op jit(solution)/shard_map/all_to_all | solution.py:319
  114.7 0.8 copy-start

commit v3 on v2

--- a/solution.py
+++ b/solution.py
@@ -1,4 +1,5 @@
 import functools
+import math
 
 import jax
 import jax.numpy as jnp
@@ -51,7 +52,7 @@
     return jnp.concatenate([padded(q, odd) for q in heads], axis=1)
 
 
-def keyval_kernel(x_ref, norm_ref, w_ref, gain_ref, normed_ref, kv_ref):
+def keyval_kernel(me_ref, x_ref, norm_ref, w_ref, gain_ref, normed_ref, kv_ref):
     frames, rows = kv_ref.shape[0], x_ref.shape[0] // kv_ref.shape[0]
     half = w_ref.shape[1] // 2
     gain = column(gain_ref[1:2, :])
@@ -122,12 +123,11 @@
     over_key_heads(frames, kv_heads, score, finish, (s0, s1))
 
 
-def far_kernel(head, spots, pieces, q_ref, o_ref, ml_ref, x_ref, norm_ref, w_hbm, *refs):
-    kv_refs, (stream_ref, timed_ref, att, s0, s1, w_ref, sem) = refs[:pieces], refs[pieces:]
-    copy = pltpu.make_async_copy(w_hbm, w_ref, sem)
-    copy.start()
-    frames, rows, part = q_ref.shape[0], kv_refs[0].shape[1] - kv_refs[0].shape[2], q_ref.shape[2]
-    half = kv_refs[0].shape[2]
+def far_kernel(head, first, spots, pieces, me_ref, q_ref, o_ref, ml_ref, x_ref, norm_ref, w_ref, *refs):
+    kv_refs, stream_ref, refs = refs[:pieces], refs[pieces], refs[pieces + 1 :]
+    timed_refs, (att, s0, s1, timed_buf) = refs[:-4], refs[-4:]
+    frames, part, half = q_ref.shape[0], q_ref.shape[2], kv_refs[0].shape[2]
+    rows = kv_refs[0].shape[1] - half
     heads, kv_heads = q_ref.shape[1] // head, half // head
     group, wide = heads // kv_heads, 2 * head
 
@@ -150,39 +150,41 @@
             att[f, at((g * group + i) * head, head), :] = out[:, i * part : (i + 1) * part]
 
     over_key_heads(frames, kv_heads, score, finish, (s0, s1))
-    copy.wait()
     for f in range(frames):
         update = dot(att[f].T, w_ref[...])
-        stream = (x_ref[f].astype(F32) + update).astype(BF16)
+        stream = (x_ref[f, first : first + part].astype(F32) + update).astype(BF16)
         timed = row_rms(stream, norm_ref[...]).astype(BF16)
-        if spots:
-            for d in range(part // spots):
-                stream_ref[d, f] = stream[d * spots : (d + 1) * spots]
-                timed_ref[d, f] = timed[d * spots : (d + 1) * spots]
+        stream_ref[f] = stream
+        if not spots:
+            timed_refs[0][f] = timed
+        elif len(timed_refs) == 1:
+            for k in range(part // spots):
+                timed_refs[0][(k * frames + f) * spots : (k * frames + f + 1) * spots] = timed[k * spots : (k + 1) * spots]
         else:
-            stream_ref[f] = stream
-            timed_ref[f] = timed
-
-
-def time_kernel(head, spots, x_ref, wkv_ref, wq_hbm, gain_ref, out_ref, wq_ref, q_buf, k_buf, v_buf, bias, att, sem):
-    copy = pltpu.make_async_copy(wq_hbm, wq_ref, sem)
-    copy.start()
-    rows = x_ref.shape[0]
+            timed_buf[...] = timed
+            for k, ref in enumerate(timed_refs):
+                ref[f * spots : (f + 1) * spots] = timed_buf[at((me_ref[0] ^ k) * spots, spots), :]
+
+
+def time_kernel(head, frames_here, spots, pieces, me_ref, gain_ref, wkv_ref, wq_ref, *refs):
+    x_refs, out_refs, (q_buf, k_buf, v_buf, bias, att) = refs[:pieces], refs[pieces : 2 * pieces], refs[2 * pieces :]
+    x = jnp.concatenate([ref[...] for ref in x_refs], axis=0)
+    rows = x.shape[0]
+    step = rows // pieces
     half = wkv_ref.shape[1] // 2
     kv_heads = half // head
     group, wide = wq_ref.shape[1] // head // kv_heads, 2 * head
-    x = x_ref[...]
+
+    def place(axis):
+        n = lax.broadcasted_iota(jnp.int32, (rows, rows), axis)
+        source = n // (frames_here * spots)
+        return (source ^ me_ref[0]) * frames_here + (n // spots) % frames_here, n % spots
+
+    (frame_k, spot_k), (frame_q, spot_q) = place(0), place(1)
+    bias[...] = jnp.where((spot_q == spot_k) & (frame_q >= frame_k), 0.0, -1e30)
     kv = dot(x, wkv_ref[...]).T
     k_buf[...] = feature_rms(kv[:half], column(gain_ref[1:2, :])).T.astype(BF16)
     v_buf[...] = kv[half:].astype(BF16)
-
-    def place(axis):
-        n = lax.broadcasted_iota(jnp.int32, (rows, rows), axis)
-        return n // spots, n % spots
-
-    (frame_k, spot_k), (frame_q, spot_q) = place(0), place(1)
-    bias[...] = jnp.where((spot_q == spot_k) & (frame_q >= frame_k), 0.0, -1e30)
-    copy.wait()
     q = feature_rms(dot(x, wq_ref[...]).T, column(gain_ref[0:1, :]))
     q_buf[...] = (q.astype(BF16).astype(F32) * head**-0.5).astype(BF16)
     for g in range(kv_heads):
@@ -196,42 +198,56 @@
         for i in range(group):
             h = g * group + i
             att[h * head : (h + 1) * head] = out[:, i * rows : (i + 1) * rows]
-    out_ref[...] = att[...].T
-
-
-def final_kernel(spots, a_ref, x_ref, w_ref, *refs):
-    out_ref = refs[-1]
-    mixed = (x_ref[...].astype(F32) + dot(a_ref[...], w_ref[...])).astype(BF16)
-    frames, part = out_ref.shape[0], out_ref.shape[1]
+    out = att[...].T
+    for i, ref in enumerate(out_refs):
+        ref[...] = out[i * step : (i + 1) * step]
+
+
+def final_kernel(first, spots, pieces, me_ref, x_ref, w_ref, *refs):
+    a_refs, (out_hbm, a_buf, out_buf, sem) = refs[:pieces], refs[-4:]
+    frames, part = x_ref.shape[0], x_ref.shape[1]
+    copies = []
     for f in range(frames):
-        if spots:
-            for d in range(part // spots):
-                first = (d * frames + f) * spots
-                out_ref[f, d * spots : (d + 1) * spots] = mixed[first : first + spots]
+        if not spots:
+            a_buf[...] = a_refs[0][f]
         else:
-            out_ref[f] = mixed[f * part : (f + 1) * part]
-
-
-def call(kernel, args, outs, flops, scratch=(), anywhere=(), blocks={}, out_blocks={}, alias={}):
-    moved = sum(a.size * a.dtype.itemsize for a in args) + sum(s.size * s.dtype.itemsize for s in outs)
-
-    def spec(shape, block):
-        if block is None:
-            return pl.BlockSpec(shape, lambda i: (0,) * len(shape))
-        return pl.BlockSpec(*block)
-
-    in_specs = [pl.BlockSpec(memory_space=pl.ANY) if i in anywhere else spec(a.shape, blocks.get(i)) for i, a in enumerate(args)]
+            for k in range(part // spots):
+                start = f * spots if pieces > 1 else (k * frames + f) * spots
+                a_buf[at((me_ref[0] ^ k) * spots, spots), :] = a_refs[k if pieces > 1 else 0][start : start + spots]
+        out_buf[f] = (x_ref[f].astype(F32) + dot(a_buf[...], w_ref[...])).astype(BF16)
+        copies.append(pltpu.make_async_copy(out_buf.at[f], out_hbm.at[f, pl.ds(first, part)], sem.at[f]))
+        copies[-1].start()
+    for copy in copies:
+        copy.wait()
+
+
+def size_of(arrays):
+    return sum(a.size * a.dtype.itemsize for a in arrays)
+
+
+def call(kernel, args, outs, flops, scratch=(), anywhere=(), out_anywhere=False, alias={}, smem=(), room=None):
+    vmem = pl.BlockSpec(memory_space=pltpu.VMEM)
+    in_specs = [vmem] * len(args)
+    for i in anywhere:
+        in_specs[i] = pl.BlockSpec(memory_space=pl.ANY)
+    for i in smem:
+        in_specs[i] = pl.BlockSpec(memory_space=pltpu.SMEM)
+    if room is None:
+        kept = sum(math.prod(s.shape) * jnp.dtype(s.dtype).itemsize for s in scratch if s.dtype in (BF16, F32))
+        room = kept + size_of(a for i, a in enumerate(args) if i not in anywhere) + size_of(outs) + (6 << 20)
     return pl.pallas_call(
         kernel,
-        grid=(1,),
         out_shape=outs,
         in_specs=in_specs,
-        out_specs=[spec(s.shape, out_blocks.get(i)) for i, s in enumerate(outs)],
+        out_specs=[pl.BlockSpec(memory_space=pl.ANY) if out_anywhere else vmem] * len(outs),
         scratch_shapes=list(scratch),
         input_output_aliases=alias,
-        compiler_params=pltpu.CompilerParams(vmem_limit_bytes=56 * 1024 * 1024),
-        cost_estimate=pl.CostEstimate(flops=int(flops), bytes_accessed=int(moved), transcendentals=0),
+        compiler_params=pltpu.CompilerParams(vmem_limit_bytes=room),
+        cost_estimate=pl.CostEstimate(flops=int(flops), bytes_accessed=int(size_of(args) + size_of(outs)), transcendentals=0),
     )(*args)
+
+
+PIECES = (lambda n: n, lambda n: n)
 
 
 def shaped(*dims, dtype=BF16):
@@ -255,12 +271,15 @@
         spots = part // frame_devices
         aligned = spots if spots % 16 == 0 else 0
         norm_space, norm_time = norm_space[None], norm_time[None]
+        zero = jnp.zeros((1,), jnp.int32)
+        index = lax.axis_index("frames").astype(jnp.int32).reshape(1)
 
         normed, kv = call(
             keyval_kernel,
-            (tokens.reshape(flat, width), norm_space, keyval_space, qk_space),
+            (index, tokens.reshape(flat, width), norm_space, keyval_space, qk_space),
             [shaped(flat, width), shaped(frames, rows + half, half)],
             4 * flat * width * half,
+            smem=(0,),
         )
         top = band_devices // 2
         far = [permuted(kv, "band", band_devices, top)]
@@ -281,53 +300,63 @@
             [pltpu.VMEM((frames, q_width, rows), BF16)] + [pltpu.VMEM((near_keys, rows * (q_width // half)), F32)] * 2,
         )
         far_keys = rows * len(far)
-        mixed = None
+        n = frame_devices * frames * spots
+
+        def exchange(xs):
+            if len(xs) > 1:
+                return [xs[0]] + [permuted(x, "frames", frame_devices, k) for k, x in enumerate(xs) if k]
+            return [lax.all_to_all(xs[0].reshape(frame_devices, frames, spots, -1), "frames", 0, 0).reshape(n, -1)]
+
+        streams, sent = [], []
         for c in range(chunks):
-            piece = (frame_devices, frames, spots, width)
-            layout = piece if aligned else (frames, part, width)
-            stream, timed = call(
-                functools.partial(far_kernel, head, aligned, len(far)),
-                (outs[c], outs[chunks + c], outs[2 * chunks + c], tokens, norm_time, out_space, *far),
-                [shaped(*layout), shaped(*layout)],
+            pieces = PIECES[c](frame_devices) if aligned else 1
+            stream, *timed = call(
+                functools.partial(far_kernel, head, c * part, aligned, len(far)),
+                (index if pieces > 1 else zero, outs[c], outs[chunks + c], outs[2 * chunks + c], tokens, norm_time, out_space, *far),
+                [shaped(frames, part, width)] + ([shaped(n // pieces, width)] * pieces if aligned else [shaped(frames, part, width)]),
                 frames * part * (8 * far_keys * q_width + 2 * q_width * width),
                 [pltpu.VMEM((frames, q_width, part), BF16)]
                 + [pltpu.VMEM((far_keys, part * (q_width // half)), F32)] * 2
-                + [pltpu.VMEM((q_width, width), BF16), pltpu.SemaphoreType.DMA],
-                anywhere=(5,),
-                blocks={3: ((frames, part, width), lambda i, c=c: (0, c, 0))},
+                + [pltpu.VMEM((part, width), BF16)],
+                smem=(0,),
             )
             if not aligned:
-                timed = timed.reshape(frames, frame_devices, spots, width).swapaxes(0, 1)
-            moved = lax.all_to_all(timed, "frames", 0, 0)
-            n = frame_devices * frames * spots
-            (att,) = call(
-                functools.partial(time_kernel, head, spots),
-                (moved.reshape(n, width), keyval_time, query_time, qk_time),
-                [shaped(n, q_width)],
+                timed = [timed[0].reshape(frames, frame_devices, spots, width).swapaxes(0, 1)]
+            moved = exchange(timed)
+            streams.append(stream)
+            sent.append(moved)
+        mixed = None
+        for c in range(chunks):
+            pieces = len(sent[c])
+            me = index if pieces > 1 else zero
+            atts = call(
+                functools.partial(time_kernel, head, frames, spots, pieces),
+                (me, qk_time, keyval_time, query_time, *sent[c]),
+                [shaped(n // pieces, q_width)] * pieces,
                 2 * n * width * (q_width + 2 * half) + 16 * n * n * q_width,
                 [
-                    pltpu.VMEM((width, q_width), BF16),
                     pltpu.VMEM((q_width, n), BF16),
                     pltpu.VMEM((n, half), BF16),
                     pltpu.VMEM((half, n), BF16),
                     pltpu.VMEM((n, n), F32),
                     pltpu.VMEM((q_width, n), BF16),
-                    pltpu.SemaphoreType.DMA,
                 ],
-                anywhere=(2,),
+                smem=(0,),
             )
-            back = lax.all_to_all(att.reshape(frame_devices, frames, spots, q_width), "frames", 0, 0)
+            back = exchange(atts)
             if not aligned:
-                back = back.swapaxes(0, 1)
-            args = (back.reshape(n, q_width), stream.reshape(n, width), out_time)
+                back = [back[0].reshape(frame_devices, frames, spots, q_width).swapaxes(0, 1).reshape(frames, part, q_width)]
+            args = (me, streams[c], out_time, *back)
             (mixed,) = call(
-                functools.partial(final_kernel, aligned),
+                functools.partial(final_kernel, c * part, aligned, pieces),
                 args if mixed is None else (*args, mixed),
                 [shaped(frames, rows, width)],
                 2 * n * width * q_width,
-                anywhere=(3,),
-                out_blocks={0: ((frames, part, width), lambda i, c=c: (0, c, 0))},
-                alias={} if mixed is None else {3: 0},
+                [pltpu.VMEM((part, q_width), BF16), pltpu.VMEM((frames, part, width), BF16), pltpu.SemaphoreType.DMA((frames,))],
+                anywhere=() if mixed is None else (3 + pieces,),
+                out_anywhere=True,
+                alias={} if mixed is None else {3 + pieces: 0},
+                smem=(0,),
             )
         return mixed
 

time: 120 us -> 97.1 us (0.81)
  waiting for transfers between devices: 47.5 us -> 20.2 us
  starting transfers between devices: 20 us -> 45.1 us
  Pallas kernels: 48.9 us -> 27.3 us
  local copies, waits for them, and re-layouts: 2.43 us -> 3.87 us
    ppermute x3 -> x31, starting transfers between devices: 2.98 us -> 45.1 us  [permuted(): return lax.ppermute(x, axis, [(i, i ^ bit) for i in range(size)])]
    all_to_all x4 -> x0, waiting for transfers between devices: 35.4 us -> none  [the longest x2 19.3 us: body(): lax.all_to_all(att.reshape(frame_devices, frames, spots, q_width), 'frame...]
    pallas_call x8, Pallas kernels: 48.9 us -> 27.3 us  [call(): pl.pallas_call(kernel, out_shape=outs, in_specs=in_specs, out_specs=[pl.B...]
    all_to_all x4 -> x0, starting transfers between devices: 17 us -> none  [the longest x2 9.72 us: body(): moved = lax.all_to_all(timed, 'frames', 0, 0)]
    ppermute x3 -> x31, waiting for transfers between devices: 12.1 us -> 20.2 us  [permuted(): return lax.ppermute(x, axis, [(i, i ^ bit) for i in range(size)])]
    unnamed x14 -> x26, local copies, waits for them, and re-layouts: 2.43 us -> 3.87 us
  transfers between devices with their start and end apart: 7 -> 31, of which waited for: 5 -> 6; matrix products, arithmetic and copies ran while one was open for 0% -> 0% of each run, Pallas kernels for 29% -> 21%
where the time goes in v3:
time: 97.1 us; the launch traced here: 96.9 us
  starting transfers between devices  45.1 us (46%)
  Pallas kernels  27.3 us (28%)
  waiting for transfers between devices  20.2 us (21%)
  local copies, waits for them, and re-layouts  3.87 us (4%)
    ppermute x31, starting transfers between devices, permuted(): return lax.ppermute(x, axis, [(i, i ^ bit) for i in range(size)])  45.1 us
    pallas_call x8, Pallas kernels, call(): pl.pallas_call(kernel, out_shape=outs, in_specs=in_specs, out_specs=[pl.B...  27.3 us
    ppermute x31, waiting for transfers between devices, permuted(): return lax.ppermute(x, axis, [(i, i ^ bit) for i in range(size)])  20.2 us
    unnamed x26, local copies, waits for them, and re-layouts  3.87 us
  transfers between devices with their start and end apart: 31, of which 6 were waited for; matrix products, arithmetic and copies ran while one was open for 0% of the time, Pallas kernels for 21%

profile of v3, /device:TPU:0, one launch (start us, length us, event | category | flops | bytes accessed | tf_op | source)
XLA Modules:
  0.0 96.9 jit_solution(7698025312968883900)
XLA Ops:
  0.0 1.2 %copy-done.1 = bf16[1024,512]{1,0:T(8,128)(2,1)S(1)} copy-done((bf16[1024,512]{1,0:T(8,128)(2,1)S(1)}, bf16[1024,512]{1,0:T(8,128)(2,1)}, u32[]{:S(2)}) %copy-start.1) | copy-done | bytes 1048600
  1.2 1.2 %copy-done.2 = bf16[2,256,1024]{2,1,0:T(8,128)(2,1)S(1)} copy-done((bf16[2,256,1024]{2,1,0:T(8,128)(2,1)S(1)}, bf16[2,256,1024]{2,1,0:T(8,128)(2,1)}, u32[]{:S(2)}) %copy-start.2) | copy-done | bytes 1048600
  2.5 0.7 copy-done.4
  3.2 0.7 copy-done.5
  3.8 1.1 %shard_map.109 = (bf16[512,1024]{1,0:T(8,128)(2,1)S(1)}, bf16[2,512,256]{2,1,0:T(8,128)(2,1)S(1)}) custom-call(s32[1]{0:T(128)} %bitcast.me_ref, bf16[512,1024]{1,0:T(8,128)(2,1)S(1)} %bitcast.4, f32[1,1024]{1,0:T(1,128)S(1)} %bitcast.5, bf16[1024,512]{1,0:T(8,128)(2,1)S(1)} %copy-done.1, f32[2,64]{1,0:T(2,128)S(1)} %copy-done.5), custom_call_target="tpu_custom_call" | custom-call | flops 536870912 | bytes 3674628 | tf_op jit(solution)/shard_map/pallas_call | solution.py:238
  4.9 3.0 %collective-permute-start.1 = (bf16[2,512,256]{2,1,0:T(8,128)(2,1)S(1)}, bf16[2,512,256]{2,1,0:T(8,128)(2,1)S(1)}, u32[]{:S(2)}, u32[]{:S(2)}) collective-permute-start(bf16[2,512,256]{2,1,0:T(8,128)(2,1)S(1)} %get-tuple-element.48.refs_0_), channel_id=1, source_target_pairs={{0,2},{1,3},{2,0},{3,1},{4,6},{5,7},{6,4},{7,5},{8,10},{9,11},{10,... | collective-permute-start | bytes 1572872 | tf_op jit(solution)/shard_map/ppermute | solution.py:258
  7.9 0.0 collective-permute-start
  7.9 11.9 %collective-permute-done.1.refs_0_ = bf16[2,512,256]{2,1,0:T(8,128)(2,1)S(1)} collective-permute-done((bf16[2,512,256]{2,1,0:T(8,128)(2,1)S(1)}, bf16[2,512,256]{2,1,0:T(8,128)(2,1)S(1)}, u32[]{:S(2)}, u32[]{:S(2)}) %collective-permute-start.1) | collective-permute-done | bytes 524320 | tf_op jit(solution)/shard_map/ppermute | solution.py:258
  19.9 0.0 collective-permute-start.2
  19.9 0.0 collective-permute-done.refs_1_
  19.9 0.0 copy-start.3
  19.9 0.0 copy-start.8
  19.9 0.0 copy-start.11
  19.9 7.9 %shard_map.110 = (bf16[2,1024,128]{2,1,0:T(8,128)(2,1)S(1)}, bf16[2,1024,128]{2,1,0:T(8,128)(2,1)S(1)}, f32[2,1024,128]{2,1,0:T(8,128)S(1)}, f32[2,1024,128]{2,1...) custom-call(bf16[512,1024]{1,0:T(8,128)(2,1)S(1)} %get-tuple-element.47.x_ref, ...), custom_call_target="tpu_custom_call" | custom-call | flops 3221225472 | bytes 7406080 | tf_op jit(solution)/shard_map/pallas_call | solution.py:238
  27.8 4.6 %shard_map.113 = (bf16[2,128,1024]{2,1,0:T(8,128)(2,1)S(1)}, bf16[32,1024]{1,0:T(8,128)(2,1)S(1)}, bf16[32,1024]{1,0:T(8,128)(2,1)S(1)}, bf16[32,1024]{1,0:T(8,1...) custom-call(s32[1]{0:T(128)} %bitcast.me_ref, ...), custom_call_target="tpu_custom_call" | custom-call | flops 1610612736 | bytes 6852612 | tf_op jit(solution)/shard_map/pallas_call | solution.py:238
  32.5 1.8 %collective-permute-start.17 = (bf16[32,1024]{1,0:T(8,128)(2,1)S(1)}, bf16[32,1024]{1,0:T(8,128)(2,1)S(1)}, u32[]{:S(2)}, u32[]{:S(2)}) collective-permute-start(bf16[32,1024]{1,0:T(8,128)(2,1)S(1)} %get-tuple-element.74), channel_id=1, source_target_pairs={{0,4},{4,0},{8,12},{12,8},{16,20},{20,16},{24,28},{28,24},{1,5},{5... | collective-permute-start | bytes 196616 | tf_op jit(solution)/shard_map/ppermute | solution.py:258
  34.3 1.6 %collective-permute-start.18 = (bf16[32,1024]{1,0:T(8,128)(2,1)S(1)}, bf16[32,1024]{1,0:T(8,128)(2,1)S(1)}, u32[]{:S(2)}, u32[]{:S(2)}) collective-permute-start(bf16[32,1024]{1,0:T(8,128)(2,1)S(1)} %get-tuple-element.75), channel_id=1, source_target_pairs={{0,8},{4,12},{8,0},{12,4},{16,24},{20,28},{24,16},{28,20},{1,9},{5... | collective-permute-start | bytes 196616 | tf_op jit(solution)/shard_map/ppermute | solution.py:258
  35.9 0.2 collective-permute-start.19
  36.0 2.8 %collective-permute-start.20 = (bf16[32,1024]{1,0:T(8,128)(2,1)S(1)}, bf16[32,1024]{1,0:T(8,128)(2,1)S(1)}, u32[]{:S(2)}, u32[]{:S(2)}) collective-permute-start(bf16[32,1024]{1,0:T(8,128)(2,1)S(1)} %get-tuple-element.77), channel_id=1, source_target_pairs={{0,16},{4,20},{8,24},{12,28},{16,0},{20,4},{24,8},{28,12},{1,17},{... | collective-permute-start | bytes 196616 | tf_op jit(solution)/shard_map/ppermute | solution.py:258
  38.8 1.3 %collective-permute-start.21 = (bf16[32,1024]{1,0:T(8,128)(2,1)S(1)}, bf16[32,1024]{1,0:T(8,128)(2,1)S(1)}, u32[]{:S(2)}, u32[]{:S(2)}) collective-permute-start(bf16[32,1024]{1,0:T(8,128)(2,1)S(1)} %get-tuple-element.78), channel_id=1, source_target_pairs={{0,20},{4,16},{8,28},{12,24},{16,4},{20,0},{24,12},{28,8},{1,21},{... | collective-permute-start | bytes 196616 | tf_op jit(solution)/shard_map/ppermute | solution.py:258
  40.1 4.7 %shard_map.111 = (bf16[2,128,1024]{2,1,0:T(8,128)(2,1)S(1)}, bf16[32,1024]{1,0:T(8,128)(2,1)S(1)}, bf16[32,1024]{1,0:T(8,128)(2,1)S(1)}, bf16[32,1024]{1,0:T(8,1...) custom-call(s32[1]{0:T(128)} %bitcast.me_ref, ...), custom_call_target="tpu_custom_call" | custom-call | flops 1610612736 | bytes 6852612 | tf_op jit(solution)/shard_map/pallas_call | solution.py:238
  44.9 3.7 %collective-permute-start.22 = (bf16[32,1024]{1,0:T(8,128)(2,1)S(1)}, bf16[32,1024]{1,0:T(8,128)(2,1)S(1)}, u32[]{:S(2)}, u32[]{:S(2)}) collective-permute-start(bf16[32,1024]{1,0:T(8,128)(2,1)S(1)} %get-tuple-element.79), channel_id=1, source_target_pairs={{0,24},{4,28},{8,16},{12,20},{16,8},{20,12},{24,0},{28,4},{1,25},{... | collective-permute-start | bytes 196616 | tf_op jit(solution)/shard_map/ppermute | solution.py:258
  48.6 0.0 collective-permute-done.18.refs_2_
  48.6 0.0 collective-permute-start.23
  48.6 1.7 %collective-permute-start.3 = (bf16[32,1024]{1,0:T(8,128)(2,1)S(1)}, bf16[32,1024]{1,0:T(8,128)(2,1)S(1)}, u32[]{:S(2)}, u32[]{:S(2)}) collective-permute-start(bf16[32,1024]{1,0:T(8,128)(2,1)S(1)} %get-tuple-element.54), channel_id=1, source_target_pairs={{0,4},{4,0},{8,12},{12,8},{16,20},{20,16},{24,28},{28,24},{1,5},{5... | collective-permute-start | bytes 196616 | tf_op jit(solution)/shard_map/ppermute | solution.py:258
  50.3 0.0 collective-permute-start.4
  50.3 0.0 collective-permute-done.21.refs_5_
  50.3 1.9 %collective-permute-start.5 = (bf16[32,1024]{1,0:T(8,128)(2,1)S(1)}, bf16[32,1024]{1,0:T(8,128)(2,1)S(1)}, u32[]{:S(2)}, u32[]{:S(2)}) collective-permute-start(bf16[32,1024]{1,0:T(8,128)(2,1)S(1)} %get-tuple-element.56), channel_id=1, source_target_pairs={{0,12},{4,8},{8,4},{12,0},{16,28},{20,24},{24,20},{28,16},{1,13},{... | collective-permute-start | bytes 196616 | tf_op jit(solution)/shard_map/ppermute | solution.py:258
  52.1 0.0 collective-permute-done.22.refs_6_
  52.1 2.4 %collective-permute-start.6 = (bf16[32,1024]{1,0:T(8,128)(2,1)S(1)}, bf16[32,1024]{1,0:T(8,128)(2,1)S(1)}, u32[]{:S(2)}, u32[]{:S(2)}) collective-permute-start(bf16[32,1024]{1,0:T(8,128)(2,1)S(1)} %get-tuple-element.57), channel_id=1, source_target_pairs={{0,16},{4,20},{8,24},{12,28},{16,0},{20,4},{24,8},{28,12},{1,17},{... | collective-permute-start | bytes 196616 | tf_op jit(solution)/shard_map/ppermute | solution.py:258
  54.5 1.3 %collective-permute-done.23.refs_7_ = bf16[32,1024]{1,0:T(8,128)(2,1)S(1)} collective-permute-done((bf16[32,1024]{1,0:T(8,128)(2,1)S(1)}, bf16[32,1024]{1,0:T(8,128)(2,1)S(1)}, u32[]{:S(2)}, u32[]{:S(2)}) %collective-permute-start.23) | collective-permute-done | bytes 65568 | tf_op jit(solution)/shard_map/ppermute | solution.py:258
  55.8 0.3 collective-permute-start.7
  56.1 0.0 collective-permute-done.3.refs_1_
  56.1 3.6 %collective-permute-start.8 = (bf16[32,1024]{1,0:T(8,128)(2,1)S(1)}, bf16[32,1024]{1,0:T(8,128)(2,1)S(1)}, u32[]{:S(2)}, u32[]{:S(2)}) collective-permute-start(bf16[32,1024]{1,0:T(8,128)(2,1)S(1)} %get-tuple-element.59), channel_id=1, source_target_pairs={{0,24},{4,28},{8,16},{12,20},{16,8},{20,12},{24,0},{28,4},{1,25},{... | collective-permute-start | bytes 196616 | tf_op jit(solution)/shard_map/ppermute | solution.py:258
  59.7 0.3 collective-permute-start.9
  60.0 3.1 %shard_map.114 = (bf16[32,1024]{1,0:T(8,128)(2,1)S(1)}, bf16[32,1024]{1,0:T(8,128)(2,1)S(1)}, bf16[32,1024]{1,0:T(8,128)(2,1)S(1)}, bf16[32,1024]{1,0:T(8,128)(2...) custom-call(s32[1]{0:T(128)} %bitcast.me_ref, ...), custom_call_target="tpu_custom_call" | custom-call | flops 1879048192 | bytes 4194820 | tf_op jit(solution)/shard_map/pallas_call | solution.py:238
  63.1 1.5 %collective-permute-start.24 = (bf16[32,1024]{1,0:T(8,128)(2,1)S(1)}, bf16[32,1024]{1,0:T(8,128)(2,1)S(1)}, u32[]{:S(2)}, u32[]{:S(2)}) collective-permute-start(bf16[32,1024]{1,0:T(8,128)(2,1)S(1)} %get-tuple-element.82), channel_id=1, source_target_pairs={{0,4},{4,0},{8,12},{12,8},{16,20},{20,16},{24,28},{28,24},{1,5},{5... | collective-permute-start | bytes 196616 | tf_op jit(solution)/shard_map/ppermute | solution.py:258
  64.6 0.1 collective-permute-done.7.refs_5_
  64.7 1.9 %collective-permute-start.26 = (bf16[32,1024]{1,0:T(8,128)(2,1)S(1)}, bf16[32,1024]{1,0:T(8,128)(2,1)S(1)}, u32[]{:S(2)}, u32[]{:S(2)}) collective-permute-start(bf16[32,1024]{1,0:T(8,128)(2,1)S(1)} %get-tuple-element.84), channel_id=1, source_target_pairs={{0,12},{4,8},{8,4},{12,0},{16,28},{20,24},{24,20},{28,16},{1,13},{... | collective-permute-start | bytes 196616 | tf_op jit(solution)/shard_map/ppermute | solution.py:258
  66.6 0.0 collective-permute-done.8.refs_6_
  66.6 2.2 %collective-permute-start.27 = (bf16[32,1024]{1,0:T(8,128)(2,1)S(1)}, bf16[32,1024]{1,0:T(8,128)(2,1)S(1)}, u32[]{:S(2)}, u32[]{:S(2)}) collective-permute-start(bf16[32,1024]{1,0:T(8,128)(2,1)S(1)} %get-tuple-element.85), channel_id=1, source_target_pairs={{0,16},{4,20},{8,24},{12,28},{16,0},{20,4},{24,8},{28,12},{1,17},{... | collective-permute-start | bytes 196616 | tf_op jit(solution)/shard_map/ppermute | solution.py:258
  68.8 0.0 collective-permute-done.9.refs_7_
  68.8 1.6 %collective-permute-start.28 = (bf16[32,1024]{1,0:T(8,128)(2,1)S(1)}, bf16[32,1024]{1,0:T(8,128)(2,1)S(1)}, u32[]{:S(2)}, u32[]{:S(2)}) collective-permute-start(bf16[32,1024]{1,0:T(8,128)(2,1)S(1)} %get-tuple-element.86), channel_id=1, source_target_pairs={{0,20},{4,16},{8,28},{12,24},{16,4},{20,0},{24,12},{28,8},{1,21},{... | collective-permute-start | bytes 196616 | tf_op jit(solution)/shard_map/ppermute | solution.py:258
  70.4 3.0 %shard_map.112 = (bf16[32,1024]{1,0:T(8,128)(2,1)S(1)}, bf16[32,1024]{1,0:T(8,128)(2,1)S(1)}, bf16[32,1024]{1,0:T(8,128)(2,1)S(1)}, bf16[32,1024]{1,0:T(8,128)(2...) custom-call(s32[1]{0:T(128)} %bitcast.me_ref, ...), custom_call_target="tpu_custom_call" | custom-call | flops 1879048192 | bytes 4194820 | tf_op jit(solution)/shard_map/pallas_call | solution.py:238
  73.5 0.0 collective-permute-done.24.refs_1_
  73.5 3.7 %collective-permute-start.29 = (bf16[32,1024]{1,0:T(8,128)(2,1)S(1)}, bf16[32,1024]{1,0:T(8,128)(2,1)S(1)}, u32[]{:S(2)}, u32[]{:S(2)}) collective-permute-start(bf16[32,1024]{1,0:T(8,128)(2,1)S(1)} %get-tuple-element.87), channel_id=1, source_target_pairs={{0,24},{4,28},{8,16},{12,20},{16,8},{20,12},{24,0},{28,4},{1,25},{... | collective-permute-start | bytes 196616 | tf_op jit(solution)/shard_map/ppermute | solution.py:258
  77.2 0.0 collective-permute-done.25.refs_2_
  77.2 0.3 collective-permute-start.30
  77.4 0.0 collective-permute-done.26.refs_3_
  77.4 1.4 %collective-permute-start.10 = (bf16[32,1024]{1,0:T(8,128)(2,1)S(1)}, bf16[32,1024]{1,0:T(8,128)(2,1)S(1)}, u32[]{:S(2)}, u32[]{:S(2)}) collective-permute-start(bf16[32,1024]{1,0:T(8,128)(2,1)S(1)} %get-tuple-element.62), channel_id=1, source_target_pairs={{0,4},{4,0},{8,12},{12,8},{16,20},{20,16},{24,28},{28,24},{1,5},{5... | collective-permute-start | bytes 196616 | tf_op jit(solution)/shard_map/ppermute | solution.py:258
  78.8 0.0 collective-permute-done.27.refs_4_
  78.9 2.1 %collective-permute-start.12 = (bf16[32,1024]{1,0:T(8,128)(2,1)S(1)}, bf16[32,1024]{1,0:T(8,128)(2,1)S(1)}, u32[]{:S(2)}, u32[]{:S(2)}) collective-permute-start(bf16[32,1024]{1,0:T(8,128)(2,1)S(1)} %get-tuple-element.64), channel_id=1, source_target_pairs={{0,12},{4,8},{8,4},{12,0},{16,28},{20,24},{24,20},{28,16},{1,13},{... | collective-permute-start | bytes 196616 | tf_op jit(solution)/shard_map/ppermute | solution.py:258
  80.9 0.0 collective-permute-done.29.refs_6_
  80.9 2.2 %collective-permute-start.13 = (bf16[32,1024]{1,0:T(8,128)(2,1)S(1)}, bf16[32,1024]{1,0:T(8,128)(2,1)S(1)}, u32[]{:S(2)}, u32[]{:S(2)}) collective-permute-start(bf16[32,1024]{1,0:T(8,128)(2,1)S(1)} %get-tuple-element.65), channel_id=1, source_target_pairs={{0,16},{4,20},{8,24},{12,28},{16,0},{20,4},{24,8},{28,12},{1,17},{... | collective-permute-start | bytes 196616 | tf_op jit(solution)/shard_map/ppermute | solution.py:258
  83.1 1.8 %collective-permute-done.30.refs_7_ = bf16[32,1024]{1,0:T(8,128)(2,1)S(1)} collective-permute-done((bf16[32,1024]{1,0:T(8,128)(2,1)S(1)}, bf16[32,1024]{1,0:T(8,128)(2,1)S(1)}, u32[]{:S(2)}, u32[]{:S(2)}) %collective-permute-start.30) | collective-permute-done | bytes 65568 | tf_op jit(solution)/shard_map/ppermute | solution.py:258
  84.9 3.5 %collective-permute-start.15 = (bf16[32,1024]{1,0:T(8,128)(2,1)S(1)}, bf16[32,1024]{1,0:T(8,128)(2,1)S(1)}, u32[]{:S(2)}, u32[]{:S(2)}) collective-permute-start(bf16[32,1024]{1,0:T(8,128)(2,1)S(1)} %get-tuple-element.67), channel_id=1, source_target_pairs={{0,24},{4,28},{8,16},{12,20},{16,8},{20,12},{24,0},{28,4},{1,25},{... | collective-permute-start | bytes 196616 | tf_op jit(solution)/shard_map/ppermute | solution.py:258
  88.3 0.0 collective-permute-done.11.refs_2_
  88.3 0.4 collective-permute-start.16
  88.7 1.5 %shard_map.115.refs_8_ = bf16[2,256,1024]{2,1,0:T(8,128)(2,1)} custom-call(s32[1]{0:T(128)} %bitcast.me_ref, bf16[2,128,1024]{2,1,0:T(8,128)(2,1)S(1)} %get-tuple-element.72.x_ref, bf16[1024,1024]{1,0:T(8,128)(2,1)S(1)} %copy-done, bf16[32,1024]{1,0:T(8,128)(2,1)S(1)} %get-tuple-element.81.refs_0_, bf16[32,1024]{1,0:T(8,128)(2,1)S(1)} %collective-permute-done.24.refs_1_, ...), custom_call_target="tpu_custom_call" | custom-call | flops 536870912 | bytes 4194308 | tf_op jit(solution)/shard_map/pallas_call | solution.py:238
  90.2 0.0 collective-permute-done.13.refs_4_
  90.2 1.7 %collective-permute-done.14.refs_5_ = bf16[32,1024]{1,0:T(8,128)(2,1)S(1)} collective-permute-done((bf16[32,1024]{1,0:T(8,128)(2,1)S(1)}, bf16[32,1024]{1,0:T(8,128)(2,1)S(1)}, u32[]{:S(2)}, u32[]{:S(2)}) %collective-permute-start.14) | collective-permute-done | bytes 65568 | tf_op jit(solution)/shard_map/ppermute | solution.py:258
  91.9 0.0 collective-permute-done.15.refs_6_
  91.9 3.4 %collective-permute-done.16.refs_7_ = bf16[32,1024]{1,0:T(8,128)(2,1)S(1)} collective-permute-done((bf16[32,1024]{1,0:T(8,128)(2,1)S(1)}, bf16[32,1024]{1,0:T(8,128)(2,1)S(1)}, u32[]{:S(2)}, u32[]{:S(2)}) %collective-permute-start.16) | collective-permute-done | bytes 65568 | tf_op jit(solution)/shard_map/ppermute | solution.py:258
  95.3 1.5 %shard_map.116 = bf16[2,256,1024]{2,1,0:T(8,128)(2,1)} custom-call(s32[1]{0:T(128)} %bitcast.me_ref, bf16[2,128,1024]{2,1,0:T(8,128)(2,1)S(1)} %get-tuple-element.52.x_ref, bf16[1024,1024]{1,0:T(8,128)(2,1)S(1)} %copy-done, bf16[32,1024]{1,0:T(8,128)(2,1)S(1)} %get-tuple-element.61.refs_0_, ...), custom_call_target="tpu_custom_call", output_to_operand_aliasing={{}: (11, {})} | custom-call | flops 536870912 | bytes 5242884 | tf_op jit(solution)/shard_map/pallas_call | solution.py:238
  (32 shorter events, 0.1 us)
Async XLA Ops:
  0.0 19.9 %copy-start.6 = (f32[2,64]{1,0:T(2,128)S(1)}, f32[2,64]{1,0:T(2,128)}, u32[]{:S(2)}) copy-start(f32[2,64]{1,0:T(2,128)} %gain_ref.5) | copy-start | bytes 1540
  0.0 1.2 %copy-start.1 = (bf16[1024,512]{1,0:T(8,128)(2,1)S(1)}, bf16[1024,512]{1,0:T(8,128)(2,1)}, u32[]{:S(2)}) copy-start(bf16[1024,512]{1,0:T(8,128)(2,1)} %w_ref.6) | copy-start | bytes 3145732
  1.2 1.2 %copy-start.2 = (bf16[2,256,1024]{2,1,0:T(8,128)(2,1)S(1)}, bf16[2,256,1024]{2,1,0:T(8,128)(2,1)}, u32[]{:S(2)}) copy-start(bf16[2,256,1024]{2,1,0:T(8,128)(2,1)} %x_ref.3) | copy-start | bytes 3145732
  2.5 0.7 copy-start.4
  3.2 0.7 copy-start.5
  3.8 16.0 %copy-start.7 = (bf16[1024,1024]{1,0:T(8,128)(2,1)S(1)}, bf16[1024,1024]{1,0:T(8,128)(2,1)}, u32[]{:S(2)}) copy-start(bf16[1024,1024]{1,0:T(8,128)(2,1)} %w_ref.7) | copy-start | bytes 6291460
  4.9 15.0 %collective-permute-start.1 = (bf16[2,512,256]{2,1,0:T(8,128)(2,1)S(1)}, bf16[2,512,256]{2,1,0:T(8,128)(2,1)S(1)}, u32[]{:S(2)}, u32[]{:S(2)}) collective-permute-start(bf16[2,512,256]{2,1,0:T(8,128)(2,1)S(1)} %get-tuple-element.48.refs_0_), channel_id=1, source_target_pairs={{0,2},{1,3},{2,0},{3,1},{4,6},{5,7},{6,4},{7,5},{8,10},{9,11},{10,... | collective-permute-start | bytes 1572872 | tf_op jit(solution)/shard_map/ppermute | solution.py:258
  7.9 11.9 %collective-permute-start = (bf16[2,512,256]{2,1,0:T(8,128)(2,1)S(1)}, bf16[2,512,256]{2,1,0:T(8,128)(2,1)S(1)}, u32[]{:S(2)}, u32[]{:S(2)}) collective-permute-start(bf16[2,512,256]{2,1,0:T(8,128)(2,1)S(1)} %get-tuple-element.48.refs_0_), channel_id=1, source_target_pairs={{0,1},{1,0},{2,3},{3,2},{4,5},{5,4},{6,7},{7,6},{8,9},{9,8},{10,11... | collective-permute-start | bytes 1572872 | tf_op jit(solution)/shard_map/ppermute | solution.py:258
  19.9 7.9 %collective-permute-start.2 = (bf16[2,512,256]{2,1,0:T(8,128)(2,1)S(1)}, bf16[2,512,256]{2,1,0:T(8,128)(2,1)S(1)}, u32[]{:S(2)}, u32[]{:S(2)}) collective-permute-start(bf16[2,512,256]{2,1,0:T(8,128)(2,1)S(1)} %collective-permute-done.1.refs_0_), channel_id=1, source_target_pairs={{0,1},{1,0},{2,3},{3,2},{4,5},{5,4},{6,7},{7,6},{8,9},{9,8},{10,11... | collective-permute-start | bytes 1572872 | tf_op jit(solution)/shard_map/ppermute | solution.py:258
  19.9 7.9 %copy-start.3 = (bf16[2,256,1024]{2,1,0:T(8,128)(2,1)S(1)}, bf16[2,256,1024]{2,1,0:T(8,128)(2,1)}, u32[]{:S(2)}) copy-start(bf16[2,256,1024]{2,1,0:T(8,128)(2,1)} %x_ref.3) | copy-start | bytes 3145732
  19.9 7.9 %copy-start.8 = (bf16[1024,1024]{1,0:T(8,128)(2,1)S(1)}, bf16[1024,1024]{1,0:T(8,128)(2,1)}, u32[]{:S(2)}) copy-start(bf16[1024,1024]{1,0:T(8,128)(2,1)} %w_ref.9) | copy-start | bytes 6291460
  19.9 7.9 %copy-start.11 = (f32[1024]{0:T(1024)S(1)}, f32[1024]{0:T(1024)}, u32[]{:S(2)}) copy-start(f32[1024]{0:T(1024)} %param.17) | copy-start | bytes 12292
  32.5 12.4 %collective-permute-start.17 = (bf16[32,1024]{1,0:T(8,128)(2,1)S(1)}, bf16[32,1024]{1,0:T(8,128)(2,1)S(1)}, u32[]{:S(2)}, u32[]{:S(2)}) collective-permute-start(bf16[32,1024]{1,0:T(8,128)(2,1)S(1)} %get-tuple-element.74), channel_id=1, source_target_pairs={{0,4},{4,0},{8,12},{12,8},{16,20},{20,16},{24,28},{28,24},{1,5},{5... | collective-permute-start | bytes 196616 | tf_op jit(solution)/shard_map/ppermute | solution.py:258
  34.3 14.3 %collective-permute-start.18 = (bf16[32,1024]{1,0:T(8,128)(2,1)S(1)}, bf16[32,1024]{1,0:T(8,128)(2,1)S(1)}, u32[]{:S(2)}, u32[]{:S(2)}) collective-permute-start(bf16[32,1024]{1,0:T(8,128)(2,1)S(1)} %get-tuple-element.75), channel_id=1, source_target_pairs={{0,8},{4,12},{8,0},{12,4},{16,24},{20,28},{24,16},{28,20},{1,9},{5... | collective-permute-start | bytes 196616 | tf_op jit(solution)/shard_map/ppermute | solution.py:258
  35.9 12.8 %collective-permute-start.19 = (bf16[32,1024]{1,0:T(8,128)(2,1)S(1)}, bf16[32,1024]{1,0:T(8,128)(2,1)S(1)}, u32[]{:S(2)}, u32[]{:S(2)}) collective-permute-start(bf16[32,1024]{1,0:T(8,128)(2,1)S(1)} %get-tuple-element.76), channel_id=1, source_target_pairs={{0,12},{4,8},{8,4},{12,0},{16,28},{20,24},{24,20},{28,16},{1,13},{... | collective-permute-start | bytes 196616 | tf_op jit(solution)/shard_map/ppermute | solution.py:258
  36.0 14.2 %collective-permute-start.20 = (bf16[32,1024]{1,0:T(8,128)(2,1)S(1)}, bf16[32,1024]{1,0:T(8,128)(2,1)S(1)}, u32[]{:S(2)}, u32[]{:S(2)}) collective-permute-start(bf16[32,1024]{1,0:T(8,128)(2,1)S(1)} %get-tuple-element.77), channel_id=1, source_target_pairs={{0,16},{4,20},{8,24},{12,28},{16,0},{20,4},{24,8},{28,12},{1,17},{... | collective-permute-start | bytes 196616 | tf_op jit(solution)/shard_map/ppermute | solution.py:258
  38.8 11.4 %collective-permute-start.21 = (bf16[32,1024]{1,0:T(8,128)(2,1)S(1)}, bf16[32,1024]{1,0:T(8,128)(2,1)S(1)}, u32[]{:S(2)}, u32[]{:S(2)}) collective-permute-start(bf16[32,1024]{1,0:T(8,128)(2,1)S(1)} %get-tuple-element.78), channel_id=1, source_target_pairs={{0,20},{4,16},{8,28},{12,24},{16,4},{20,0},{24,12},{28,8},{1,21},{... | collective-permute-start | bytes 196616 | tf_op jit(solution)/shard_map/ppermute | solution.py:258
  40.1 19.8 %copy-start.9 = (bf16[1024,1024]{1,0:T(8,128)(2,1)S(1)}, bf16[1024,1024]{1,0:T(8,128)(2,1)}, u32[]{:S(2)}) copy-start(bf16[1024,1024]{1,0:T(8,128)(2,1)} %wq_ref.3) | copy-start | bytes 6291460
  40.1 19.8 %copy-start.10 = (bf16[1024,512]{1,0:T(8,128)(2,1)S(1)}, bf16[1024,512]{1,0:T(8,128)(2,1)}, u32[]{:S(2)}) copy-start(bf16[1024,512]{1,0:T(8,128)(2,1)} %wkv_ref.3) | copy-start | bytes 3145732
  40.1 19.8 %copy-start.12 = (f32[2,64]{1,0:T(2,128)S(1)}, f32[2,64]{1,0:T(2,128)}, u32[]{:S(2)}) copy-start(f32[2,64]{1,0:T(2,128)} %gain_ref.7) | copy-start | bytes 1540
  44.9 7.2 %collective-permute-start.22 = (bf16[32,1024]{1,0:T(8,128)(2,1)S(1)}, bf16[32,1024]{1,0:T(8,128)(2,1)S(1)}, u32[]{:S(2)}, u32[]{:S(2)}) collective-permute-start(bf16[32,1024]{1,0:T(8,128)(2,1)S(1)} %get-tuple-element.79), channel_id=1, source_target_pairs={{0,24},{4,28},{8,16},{12,20},{16,8},{20,12},{24,0},{28,4},{1,25},{... | collective-permute-start | bytes 196616 | tf_op jit(solution)/shard_map/ppermute | solution.py:258
  48.6 7.2 %collective-permute-start.23 = (bf16[32,1024]{1,0:T(8,128)(2,1)S(1)}, bf16[32,1024]{1,0:T(8,128)(2,1)S(1)}, u32[]{:S(2)}, u32[]{:S(2)}) collective-permute-start(bf16[32,1024]{1,0:T(8,128)(2,1)S(1)} %get-tuple-element.80), channel_id=1, source_target_pairs={{0,28},{4,24},{8,20},{12,16},{16,12},{20,8},{24,4},{28,0},{1,29},{... | collective-permute-start | bytes 196616 | tf_op jit(solution)/shard_map/ppermute | solution.py:258
  48.6 7.5 %collective-permute-start.3 = (bf16[32,1024]{1,0:T(8,128)(2,1)S(1)}, bf16[32,1024]{1,0:T(8,128)(2,1)S(1)}, u32[]{:S(2)}, u32[]{:S(2)}) collective-permute-start(bf16[32,1024]{1,0:T(8,128)(2,1)S(1)} %get-tuple-element.54), channel_id=1, source_target_pairs={{0,4},{4,0},{8,12},{12,8},{16,20},{20,16},{24,28},{28,24},{1,5},{5... | collective-permute-start | bytes 196616 | tf_op jit(solution)/shard_map/ppermute | solution.py:258
  50.3 9.5 %collective-permute-start.4 = (bf16[32,1024]{1,0:T(8,128)(2,1)S(1)}, bf16[32,1024]{1,0:T(8,128)(2,1)S(1)}, u32[]{:S(2)}, u32[]{:S(2)}) collective-permute-start(bf16[32,1024]{1,0:T(8,128)(2,1)S(1)} %get-tuple-element.55), channel_id=1, source_target_pairs={{0,8},{4,12},{8,0},{12,4},{16,24},{20,28},{24,16},{28,20},{1,9},{5... | collective-permute-start | bytes 196616 | tf_op jit(solution)/shard_map/ppermute | solution.py:258
  50.3 12.8 %collective-permute-start.5 = (bf16[32,1024]{1,0:T(8,128)(2,1)S(1)}, bf16[32,1024]{1,0:T(8,128)(2,1)S(1)}, u32[]{:S(2)}, u32[]{:S(2)}) collective-permute-start(bf16[32,1024]{1,0:T(8,128)(2,1)S(1)} %get-tuple-element.56), channel_id=1, source_target_pairs={{0,12},{4,8},{8,4},{12,0},{16,28},{20,24},{24,20},{28,16},{1,13},{... | collective-permute-start | bytes 196616 | tf_op jit(solution)/shard_map/ppermute | solution.py:258
  52.1 12.4 %collective-permute-start.6 = (bf16[32,1024]{1,0:T(8,128)(2,1)S(1)}, bf16[32,1024]{1,0:T(8,128)(2,1)S(1)}, u32[]{:S(2)}, u32[]{:S(2)}) collective-permute-start(bf16[32,1024]{1,0:T(8,128)(2,1)S(1)} %get-tuple-element.57), channel_id=1, source_target_pairs={{0,16},{4,20},{8,24},{12,28},{16,0},{20,4},{24,8},{28,12},{1,17},{... | collective-permute-start | bytes 196616 | tf_op jit(solution)/shard_map/ppermute | solution.py:258
  55.8 8.9 %collective-permute-start.7 = (bf16[32,1024]{1,0:T(8,128)(2,1)S(1)}, bf16[32,1024]{1,0:T(8,128)(2,1)S(1)}, u32[]{:S(2)}, u32[]{:S(2)}) collective-permute-start(bf16[32,1024]{1,0:T(8,128)(2,1)S(1)} %get-tuple-element.58), channel_id=1, source_target_pairs={{0,20},{4,16},{8,28},{12,24},{16,4},{20,0},{24,12},{28,8},{1,21},{... | collective-permute-start | bytes 196616 | tf_op jit(solution)/shard_map/ppermute | solution.py:258
  56.1 10.5 %collective-permute-start.8 = (bf16[32,1024]{1,0:T(8,128)(2,1)S(1)}, bf16[32,1024]{1,0:T(8,128)(2,1)S(1)}, u32[]{:S(2)}, u32[]{:S(2)}) collective-permute-start(bf16[32,1024]{1,0:T(8,128)(2,1)S(1)} %get-tuple-element.59), channel_id=1, source_target_pairs={{0,24},{4,28},{8,16},{12,20},{16,8},{20,12},{24,0},{28,4},{1,25},{... | collective-permute-start | bytes 196616 | tf_op jit(solution)/shard_map/ppermute | solution.py:258
  59.7 9.1 %collective-permute-start.9 = (bf16[32,1024]{1,0:T(8,128)(2,1)S(1)}, bf16[32,1024]{1,0:T(8,128)(2,1)S(1)}, u32[]{:S(2)}, u32[]{:S(2)}) collective-permute-start(bf16[32,1024]{1,0:T(8,128)(2,1)S(1)} %get-tuple-element.60), channel_id=1, source_target_pairs={{0,28},{4,24},{8,20},{12,16},{16,12},{20,8},{24,4},{28,0},{1,29},{... | collective-permute-start | bytes 196616 | tf_op jit(solution)/shard_map/ppermute | solution.py:258
  63.1 10.4 %collective-permute-start.24 = (bf16[32,1024]{1,0:T(8,128)(2,1)S(1)}, bf16[32,1024]{1,0:T(8,128)(2,1)S(1)}, u32[]{:S(2)}, u32[]{:S(2)}) collective-permute-start(bf16[32,1024]{1,0:T(8,128)(2,1)S(1)} %get-tuple-element.82), channel_id=1, source_target_pairs={{0,4},{4,0},{8,12},{12,8},{16,20},{20,16},{24,28},{28,24},{1,5},{5... | collective-permute-start | bytes 196616 | tf_op jit(solution)/shard_map/ppermute | solution.py:258
  64.6 12.6 %collective-permute-start.25 = (bf16[32,1024]{1,0:T(8,128)(2,1)S(1)}, bf16[32,1024]{1,0:T(8,128)(2,1)S(1)}, u32[]{:S(2)}, u32[]{:S(2)}) collective-permute-start(bf16[32,1024]{1,0:T(8,128)(2,1)S(1)} %get-tuple-element.83), channel_id=1, source_target_pairs={{0,8},{4,12},{8,0},{12,4},{16,24},{20,28},{24,16},{28,20},{1,9},{5... | collective-permute-start | bytes 196616 | tf_op jit(solution)/shard_map/ppermute | solution.py:258
  64.7 12.7 %collective-permute-start.26 = (bf16[32,1024]{1,0:T(8,128)(2,1)S(1)}, bf16[32,1024]{1,0:T(8,128)(2,1)S(1)}, u32[]{:S(2)}, u32[]{:S(2)}) collective-permute-start(bf16[32,1024]{1,0:T(8,128)(2,1)S(1)} %get-tuple-element.84), channel_id=1, source_target_pairs={{0,12},{4,8},{8,4},{12,0},{16,28},{20,24},{24,20},{28,16},{1,13},{... | collective-permute-start | bytes 196616 | tf_op jit(solution)/shard_map/ppermute | solution.py:258
  66.6 12.2 %collective-permute-start.27 = (bf16[32,1024]{1,0:T(8,128)(2,1)S(1)}, bf16[32,1024]{1,0:T(8,128)(2,1)S(1)}, u32[]{:S(2)}, u32[]{:S(2)}) collective-permute-start(bf16[32,1024]{1,0:T(8,128)(2,1)S(1)} %get-tuple-element.85), channel_id=1, source_target_pairs={{0,16},{4,20},{8,24},{12,28},{16,0},{20,4},{24,8},{28,12},{1,17},{... | collective-permute-start | bytes 196616 | tf_op jit(solution)/shard_map/ppermute | solution.py:258
  68.8 10.0 %collective-permute-start.28 = (bf16[32,1024]{1,0:T(8,128)(2,1)S(1)}, bf16[32,1024]{1,0:T(8,128)(2,1)S(1)}, u32[]{:S(2)}, u32[]{:S(2)}) collective-permute-start(bf16[32,1024]{1,0:T(8,128)(2,1)S(1)} %get-tuple-element.86), channel_id=1, source_target_pairs={{0,20},{4,16},{8,28},{12,24},{16,4},{20,0},{24,12},{28,8},{1,21},{... | collective-permute-start | bytes 196616 | tf_op jit(solution)/shard_map/ppermute | solution.py:258
  70.4 18.3 %copy-start = (bf16[1024,1024]{1,0:T(8,128)(2,1)S(1)}, bf16[1024,1024]{1,0:T(8,128)(2,1)}, u32[]{:S(2)}) copy-start(bf16[1024,1024]{1,0:T(8,128)(2,1)} %w_ref.11) | copy-start | bytes 6291460
  73.5 7.4 %collective-permute-start.29 = (bf16[32,1024]{1,0:T(8,128)(2,1)S(1)}, bf16[32,1024]{1,0:T(8,128)(2,1)S(1)}, u32[]{:S(2)}, u32[]{:S(2)}) collective-permute-start(bf16[32,1024]{1,0:T(8,128)(2,1)S(1)} %get-tuple-element.87), channel_id=1, source_target_pairs={{0,24},{4,28},{8,16},{12,20},{16,8},{20,12},{24,0},{28,4},{1,25},{... | collective-permute-start | bytes 196616 | tf_op jit(solution)/shard_map/ppermute | solution.py:258
  77.2 7.7 %collective-permute-start.30 = (bf16[32,1024]{1,0:T(8,128)(2,1)S(1)}, bf16[32,1024]{1,0:T(8,128)(2,1)S(1)}, u32[]{:S(2)}, u32[]{:S(2)}) collective-permute-start(bf16[32,1024]{1,0:T(8,128)(2,1)S(1)} %get-tuple-element.88), channel_id=1, source_target_pairs={{0,28},{4,24},{8,20},{12,16},{16,12},{20,8},{24,4},{28,0},{1,29},{... | collective-permute-start | bytes 196616 | tf_op jit(solution)/shard_map/ppermute | solution.py:258
  77.4 7.4 %collective-permute-start.10 = (bf16[32,1024]{1,0:T(8,128)(2,1)S(1)}, bf16[32,1024]{1,0:T(8,128)(2,1)S(1)}, u32[]{:S(2)}, u32[]{:S(2)}) collective-permute-start(bf16[32,1024]{1,0:T(8,128)(2,1)S(1)} %get-tuple-element.62), channel_id=1, source_target_pairs={{0,4},{4,0},{8,12},{12,8},{16,20},{20,16},{24,28},{28,24},{1,5},{5... | collective-permute-start | bytes 196616 | tf_op jit(solution)/shard_map/ppermute | solution.py:258
  78.8 9.5 %collective-permute-start.11 = (bf16[32,1024]{1,0:T(8,128)(2,1)S(1)}, bf16[32,1024]{1,0:T(8,128)(2,1)S(1)}, u32[]{:S(2)}, u32[]{:S(2)}) collective-permute-start(bf16[32,1024]{1,0:T(8,128)(2,1)S(1)} %get-tuple-element.63), channel_id=1, source_target_pairs={{0,8},{4,12},{8,0},{12,4},{16,24},{20,28},{24,16},{28,20},{1,9},{5... | collective-permute-start | bytes 196616 | tf_op jit(solution)/shard_map/ppermute | solution.py:258
  78.9 11.3 %collective-permute-start.12 = (bf16[32,1024]{1,0:T(8,128)(2,1)S(1)}, bf16[32,1024]{1,0:T(8,128)(2,1)S(1)}, u32[]{:S(2)}, u32[]{:S(2)}) collective-permute-start(bf16[32,1024]{1,0:T(8,128)(2,1)S(1)} %get-tuple-element.64), channel_id=1, source_target_pairs={{0,12},{4,8},{8,4},{12,0},{16,28},{20,24},{24,20},{28,16},{1,13},{... | collective-permute-start | bytes 196616 | tf_op jit(solution)/shard_map/ppermute | solution.py:258
  80.9 9.3 %collective-permute-start.13 = (bf16[32,1024]{1,0:T(8,128)(2,1)S(1)}, bf16[32,1024]{1,0:T(8,128)(2,1)S(1)}, u32[]{:S(2)}, u32[]{:S(2)}) collective-permute-start(bf16[32,1024]{1,0:T(8,128)(2,1)S(1)} %get-tuple-element.65), channel_id=1, source_target_pairs={{0,16},{4,20},{8,24},{12,28},{16,0},{20,4},{24,8},{28,12},{1,17},{... | collective-permute-start | bytes 196616 | tf_op jit(solution)/shard_map/ppermute | solution.py:258
  84.9 7.0 %collective-permute-start.14 = (bf16[32,1024]{1,0:T(8,128)(2,1)S(1)}, bf16[32,1024]{1,0:T(8,128)(2,1)S(1)}, u32[]{:S(2)}, u32[]{:S(2)}) collective-permute-start(bf16[32,1024]{1,0:T(8,128)(2,1)S(1)} %get-tuple-element.66), channel_id=1, source_target_pairs={{0,20},{4,16},{8,28},{12,24},{16,4},{20,0},{24,12},{28,8},{1,21},{... | collective-permute-start | bytes 196616 | tf_op jit(solution)/shard_map/ppermute | solution.py:258
  84.9 7.0 %collective-permute-start.15 = (bf16[32,1024]{1,0:T(8,128)(2,1)S(1)}, bf16[32,1024]{1,0:T(8,128)(2,1)S(1)}, u32[]{:S(2)}, u32[]{:S(2)}) collective-permute-start(bf16[32,1024]{1,0:T(8,128)(2,1)S(1)} %get-tuple-element.67), channel_id=1, source_target_pairs={{0,24},{4,28},{8,16},{12,20},{16,8},{20,12},{24,0},{28,4},{1,25},{... | collective-permute-start | bytes 196616 | tf_op jit(solution)/shard_map/ppermute | solution.py:258
  88.3 7.0 %collective-permute-start.16 = (bf16[32,1024]{1,0:T(8,128)(2,1)S(1)}, bf16[32,1024]{1,0:T(8,128)(2,1)S(1)}, u32[]{:S(2)}, u32[]{:S(2)}) collective-permute-start(bf16[32,1024]{1,0:T(8,128)(2,1)S(1)} %get-tuple-element.68), channel_id=1, source_target_pairs={{0,28},{4,24},{8,20},{12,16},{16,12},{20,8},{24,4},{28,0},{1,29},{... | collective-permute-start | bytes 196616 | tf_op jit(solution)/shard_map/ppermute | solution.py:258

commit v4 on v3

v4 whole, which is shorter than its diff:
```python
import functools
import math

import jax
import jax.numpy as jnp
from jax import lax
from jax.experimental import pallas as pl
from jax.experimental.pallas import tpu as pltpu
from jax.sharding import PartitionSpec as P


EPS = 1e-06
LOG2E = 1.4426950408889634
BF16 = jnp.bfloat16
F32 = jnp.float32


def dot(a, b):
    return jnp.dot(a, b, preferred_element_type=F32)


def row_rms(x, gain):
    x = x.astype(F32)
    return x * lax.rsqrt(jnp.mean(x * x, axis=-1, keepdims=True) + EPS) * gain


def column(row):
    n = row.shape[1]
    i = lax.broadcasted_iota(jnp.int32, (n, n), 0)
    j = lax.broadcasted_iota(jnp.int32, (n, n), 1)
    return jnp.sum(jnp.where(i == j, row, 0.0), axis=1, keepdims=True)


def feature_rms(x, gain):
    n = gain.shape[0]
    y = x.reshape(x.shape[0] // n, n, x.shape[1])
    total = jnp.sum(y * y, axis=1, keepdims=True)
    return (y * lax.rsqrt(total * (1.0 / n) + EPS) * gain[None]).reshape(x.shape)


def at(start, size):
    return pl.ds(pl.multiple_of(start, size), size)


def padded(q, odd):
    zero = jnp.zeros_like(q)
    return jnp.concatenate([zero, q] if odd else [q, zero], axis=0)


def query_columns(q_ref, lead, g, group, head, odd, lanes=slice(None)):
    heads = [q_ref[(*lead, at((g * group + i) * head, head), lanes)] for i in range(group)]
    return jnp.concatenate([padded(q, odd) for q in heads], axis=1)


def keyval_kernel(me_ref, x_hbm, norm_hbm, w_hbm, gain_hbm, normed_ref, kv_ref, x_ref, norm_ref, w_ref, gain_ref, sems):
    frames, rows = x_hbm.shape[0], x_hbm.shape[1]
    half = w_ref.shape[1] // 2
    small = [pltpu.make_async_copy(norm_hbm, norm_ref, sems.at[frames]), pltpu.make_async_copy(gain_hbm, gain_ref, sems.at[frames + 1])]
    x_copies = [pltpu.make_async_copy(x_hbm.at[f], x_ref.at[f], sems.at[f]) for f in range(frames)]
    w_copy = pltpu.make_async_copy(w_hbm, w_ref, sems.at[frames + 2])
    for copy in (*small, x_copies[0], w_copy, *x_copies[1:]):
        copy.start()
    for copy in small:
        copy.wait()
    gain = column(gain_ref[1:2, :])
    for f in range(frames):
        x_copies[f].wait()
        part = slice(f * rows, (f + 1) * rows)
        normed = row_rms(x_ref[f], norm_ref[...]).astype(BF16)
        normed_ref[part] = normed
        if f == 0:
            w_copy.wait()
        kv = dot(normed, w_ref[...]).T
        kv_ref[f, :rows] = feature_rms(kv[:half], gain).T.astype(BF16)
        kv_ref[f, rows:] = kv[half:].astype(BF16)


def over_key_heads(frames, kv_heads, score, finish, bufs):
    pairs = kv_heads // 2
    total = frames * pairs

    def split(step):
        return step // pairs, (step % pairs) * 2

    score(0, 0, False, bufs[0])

    def step(n, carry):
        f, g = split(n)
        f_next, g_next = split(jnp.minimum(n + 1, total - 1))
        score(f, g + 1, True, bufs[1])
        finish(f, g, bufs[0])
        score(f_next, g_next, False, bufs[0])
        finish(f, g + 1, bufs[1])
        return carry

    lax.fori_loop(0, total, step, 0)


def near_kernel(head, pieces, x_ref, w_ref, gain_ref, *refs):
    kv_refs, refs = refs[:pieces], refs[pieces:]
    q_ref, o_ref, ml_ref, s0, s1 = refs
    frames, rows = kv_refs[0].shape[0], x_ref.shape[0] // kv_refs[0].shape[0]
    half = kv_refs[0].shape[2]
    heads, kv_heads = w_ref.shape[1] // head, half // head
    group, wide = heads // kv_heads, 2 * head
    gain = column(gain_ref[0:1, :])
    for f in range(frames):
        q = dot(x_ref[f * rows : (f + 1) * rows], w_ref[...]).T
        q_ref[f] = (feature_rms(q, gain).astype(BF16).astype(F32) * head**-0.5).astype(BF16)

    def score(f, g, odd, buf):
        keys = jnp.concatenate([ref[f, :rows, at((g // 2) * wide, wide)] for ref in kv_refs], axis=0)
        buf[...] = dot(keys, query_columns(q_ref, (f,), g, group, head, odd))

    def finish(f, g, buf):
        s = buf[...]
        largest = jnp.max(s, axis=0, keepdims=True)
        e = jnp.exp2((s - largest) * LOG2E)
        total = jnp.sum(e, axis=0, keepdims=True)
        values = jnp.concatenate([ref[f, at(rows + g * head, head), :] for ref in kv_refs], axis=1)
        out = dot(values, e.astype(BF16))
        for i in range(group):
            h = g * group + i
            lanes = slice(i * rows, (i + 1) * rows)
            o_ref[f, at(h * head, head), :] = out[:, lanes]
            ml_ref[f, g, i : i + 1, :] = largest[:, lanes]
            ml_ref[f, g, group + i : group + i + 1, :] = total[:, lanes]

    over_key_heads(frames, kv_heads, score, finish, (s0, s1))


def far_kernel(head, chunk, top, spots, pieces, me_ref, q_ref, o_ref, ml_ref, x_ref, norm_ref, w_ref, *refs):
    kv_refs, stream_ref, refs = refs[:pieces], refs[pieces], refs[pieces + 1 :]
    timed_refs, (att, s0, s1, timed_buf) = refs[:-4], refs[-4:]
    frames, part, half = stream_ref.shape[0], stream_ref.shape[1], kv_refs[0].shape[2]
    rows = kv_refs[0].shape[1] - half
    heads, kv_heads = q_ref.shape[1] // head, half // head
    group, wide = heads // kv_heads, 2 * head
    mine = slice(chunk * part, (chunk + 1) * part)

    def score(f, g, odd, buf):
        keys = jnp.concatenate([ref[f, :rows, at((g // 2) * wide, wide)] for ref in kv_refs], axis=0)
        buf[...] = dot(keys, query_columns(q_ref, (f,), g, group, head, odd, mine))

    def finish(f, g, buf):
        s = buf[...]
        ml = ml_ref[f, g, :, mine]
        before = jnp.concatenate([ml[i : i + 1] for i in range(group)], axis=1)
        total = jnp.concatenate([ml[group + i : group + i + 1] for i in range(group)], axis=1)
        out = jnp.concatenate([o_ref[f, at((g * group + i) * head, head), mine] for i in range(group)], axis=1)
        largest = jnp.maximum(before, jnp.max(s, axis=0, keepdims=True))
        scale = jnp.exp2((before - largest) * LOG2E)
        e = jnp.exp2((s - largest) * LOG2E)
        total = total * scale + jnp.sum(e, axis=0, keepdims=True)
        values = jnp.concatenate([ref[f, at(rows + g * head, head), :] for ref in kv_refs], axis=1)
        out = ((out * scale + dot(values, e.astype(BF16))) / total).astype(BF16)
        for i in range(group):
            att[f, at((g * group + i) * head, head), :] = out[:, i * part : (i + 1) * part]

    over_key_heads(frames, kv_heads, score, finish, (s0, s1))
    for f in range(frames):
        update = dot(att[f].T, w_ref[...])
        stream = (x_ref[f, mine].astype(F32) + update).astype(BF16)
        timed = row_rms(stream, norm_ref[...]).astype(BF16)
        stream_ref[f] = stream
        if not top:
            timed_refs[0][f] = timed
        else:
            timed_buf[...] = timed
            for k, ref in enumerate(timed_refs):
                ref[f * spots : (f + 1) * spots] = timed_buf[at(((me_ref[0] ^ k) % top) * spots, spots), :]


def in_groups(refs, frames, spots, groups):
    sub = spots // groups
    starts = [(p, f * spots + h * sub) for h in range(groups) for p in range(len(refs)) for f in range(frames)]
    return jnp.concatenate([refs[p][start : start + sub] for p, start in starts], axis=0)


def out_of_groups(x, refs, frames, spots, groups):
    sub = spots // groups
    n = 0
    for h in range(groups):
        for ref in refs:
            for f in range(frames):
                ref[f * spots + h * sub : f * spots + (h + 1) * sub] = x[n * sub : (n + 1) * sub]
                n += 1


def project(head, x, gain_ref, wkv_ref, wq_ref, q_ref, kv_ref):
    half = wkv_ref.shape[1] // 2
    kv = dot(x, wkv_ref[...]).T
    kv_ref[: x.shape[0]] = feature_rms(kv[:half], column(gain_ref[1:2, :])).T.astype(BF16)
    kv_ref[x.shape[0] :] = kv[half:].astype(BF16)
    q = feature_rms(dot(x, wq_ref[...]).T, column(gain_ref[0:1, :]))
    q_ref[...] = (q.astype(BF16).astype(F32) * head**-0.5).astype(BF16)


def attend_time(head, q_ref, kv_refs, bias, att, groups):
    count = q_ref.shape[1]
    kv_heads = (kv_refs[0].shape[0] - count) // head
    group, wide, cols = q_ref.shape[0] // head // kv_heads, 2 * head, count // groups
    for h in range(groups):
        lanes = slice(h * cols, (h + 1) * cols)
        for g in range(kv_heads):
            keys = jnp.concatenate([ref[lanes, (g // 2) * wide : (g // 2 + 1) * wide] for ref in kv_refs], axis=0)
            s = dot(keys, query_columns(q_ref, (), g, group, head, g % 2 == 1, lanes))
            s = jnp.concatenate([s[:, i * cols : (i + 1) * cols] + bias[...] for i in range(group)], axis=1)
            largest = jnp.max(s, axis=0, keepdims=True)
            e = jnp.exp2((s - largest) * LOG2E)
            total = jnp.sum(e, axis=0, keepdims=True)
            values = jnp.concatenate([ref[count + g * head : count + (g + 1) * head, lanes] for ref in kv_refs], axis=1)
            out = (dot(values, e.astype(BF16)) / total).astype(BF16)
            for i in range(group):
                att[(g * group + i) * head : (g * group + i + 1) * head, lanes] = out[:, i * cols : (i + 1) * cols]


def causal_bias(bias, frames, sub, me_ref):
    def place(axis):
        n = lax.broadcasted_iota(jnp.int32, bias.shape, axis)
        return (n // (frames * sub) ^ me_ref[0]) * frames + (n // sub) % frames, n % sub

    (frame_k, spot_k), (frame_q, spot_q) = place(0), place(1)
    bias[...] = jnp.where((spot_q == spot_k) & (frame_q >= frame_k), 0.0, -1e30)


def time_project_kernel(head, frames, spots, groups, pieces, gain_ref, wkv_ref, wq_ref, *refs):
    x_refs, (q_ref, kv_ref) = refs[:pieces], refs[pieces:]
    project(head, in_groups(x_refs, frames, spots, groups), gain_ref, wkv_ref, wq_ref, q_ref, kv_ref)


def time_attend_kernel(head, frames, spots, groups, pieces, me_ref, q_ref, kv_ref, kv_other, *refs):
    out_refs, (bias, att) = refs[:pieces], refs[pieces:]
    causal_bias(bias, frames, spots // groups, me_ref)
    attend_time(head, q_ref, (kv_ref, kv_other), bias, att, groups)
    out_of_groups(att[...].T, out_refs, frames, spots, groups)


def time_whole_kernel(head, frames, spots, me_ref, gain_ref, wkv_ref, wq_ref, x_ref, out_ref, q_buf, kv_buf, bias, att):
    causal_bias(bias, frames, spots, me_ref)
    project(head, x_ref[...], gain_ref, wkv_ref, wq_ref, q_buf, kv_buf)
    attend_time(head, q_buf, (kv_buf,), bias, att, 1)
    out_ref[...] = att[...].T


def final_kernel(chunk, top, spots, pieces, me_ref, w_ref, x_ref, *refs):
    a_refs, (out_hbm, a_buf, out_buf, sem) = refs[:pieces], refs[-4:]
    frames, part = x_ref.shape[0], x_ref.shape[1]
    copies = []
    for f in range(frames):
        if not top:
            a_buf[...] = a_refs[0][f]
        else:
            for k, ref in enumerate(a_refs):
                a_buf[at(((me_ref[0] ^ k) % top) * spots, spots), :] = ref[f * spots : (f + 1) * spots]
        out_buf[f] = (x_ref[f].astype(F32) + dot(a_buf[...], w_ref[...])).astype(BF16)
        copies.append(pltpu.make_async_copy(out_buf.at[f], out_hbm.at[f, pl.ds(chunk * part, part)], sem.at[f]))
        copies[-1].start()
    for copy in copies:
        copy.wait()


def size_of(arrays):
    return sum(a.size * a.dtype.itemsize for a in arrays)


def call(kernel, args, outs, flops, scratch=(), anywhere=(), out_anywhere=False, alias={}, smem=(), room=None):
    vmem = pl.BlockSpec(memory_space=pltpu.VMEM)
    in_specs = [vmem] * len(args)
    for i in anywhere:
        in_specs[i] = pl.BlockSpec(memory_space=pl.ANY)
    for i in smem:
        in_specs[i] = pl.BlockSpec(memory_space=pltpu.SMEM)
    if room is None:
        kept = sum(math.prod(s.shape) * jnp.dtype(s.dtype).itemsize for s in scratch if s.dtype in (BF16, F32))
        room = kept + size_of(a for i, a in enumerate(args) if i not in anywhere) + size_of(outs) + (6 << 20)
    return pl.pallas_call(
        kernel,
        out_shape=outs,
        in_specs=in_specs,
        out_specs=[pl.BlockSpec(memory_space=pl.ANY) if out_anywhere else vmem] * len(outs),
        scratch_shapes=list(scratch),
        input_output_aliases=alias,
        compiler_params=pltpu.CompilerParams(vmem_limit_bytes=room),
        cost_estimate=pl.CostEstimate(flops=int(flops), bytes_accessed=int(size_of(args) + size_of(outs)), transcendentals=0),
    )(*args)


FIRST_ROOM = 57 << 20


def shaped(*dims, dtype=BF16):
    return jax.ShapeDtypeStruct(dims, dtype)


def permuted(x, axis, size, bit):
    return lax.ppermute(x, axis, [(i, i ^ bit) for i in range(size)])


def make_body(mesh):
    frame_devices, band_devices = mesh.shape["frames"], mesh.shape["band"]
    chunks, groups = 2, 2

    def body(tokens, norm_space, query_space, keyval_space, out_space, qk_space, norm_time, query_time, keyval_time, out_time, qk_time):
        frames, rows, width = tokens.shape
        head = qk_space.shape[1]
        q_width, half = query_space.shape[1], keyval_space.shape[1] // 2
        flat, part = frames * rows, rows // chunks
        top = frame_devices // 2
        spots = part // top
        n = frames * part
        by_partner = spots % (16 * groups) == 0 and n == half
        top = top if by_partner else 0
        norm_space, norm_time = norm_space[None], norm_time[None]
        index = lax.axis_index("frames").astype(jnp.int32).reshape(1)
        me = index if by_partner else jnp.zeros((1,), jnp.int32)

        normed, kv = call(
            keyval_kernel,
            (index, tokens, norm_space, keyval_space, qk_space),
            [shaped(flat, width), shaped(frames, rows + half, half)],
            4 * flat * width * half,
            [
                pltpu.VMEM(tokens.shape, BF16),
                pltpu.VMEM((1, width), F32),
                pltpu.VMEM(keyval_space.shape, BF16),
                pltpu.VMEM(qk_space.shape, F32),
                pltpu.SemaphoreType.DMA((frames + 3,)),
            ],
            anywhere=(1, 2, 3, 4),
            smem=(0,),
            room=FIRST_ROOM,
        )
        bit = band_devices // 2
        far = [permuted(kv, "band", band_devices, bit)]
        near, bit = [kv], bit // 2
        while bit:
            near += [permuted(p, "band", band_devices, bit) for p in near]
            far += [permuted(p, "band", band_devices, bit) for p in far]
            bit //= 2

        near_keys, far_keys = rows * len(near), rows * len(far)
        state = call(
            functools.partial(near_kernel, head, len(near)),
            (normed, query_space, qk_space, *near),
            [shaped(frames, q_width, rows), shaped(frames, q_width, rows, dtype=F32), shaped(frames, half // head, 2 * q_width // half, rows, dtype=F32)],
            2 * flat * width * q_width + 8 * flat * near_keys * q_width,
            [pltpu.VMEM((near_keys, rows * (q_width // half)), F32)] * 2,
        )

        def far_part(c):
            outs = [shaped(frames * spots, width)] * top if by_partner else [shaped(frames, part, width)]
            return call(
                functools.partial(far_kernel, head, c, top, spots, len(far)),
                (me, *state, tokens, norm_time, out_space, *far),
                [shaped(frames, part, width)] + outs,
                frames * part * (8 * far_keys * q_width + 2 * q_width * width),
                [pltpu.VMEM((frames, q_width, part), BF16)]
                + [pltpu.VMEM((far_keys, part * (q_width // half)), F32)] * 2
                + [pltpu.VMEM((part, width), BF16)],
                smem=(0,),
            )

        def final_part(c, stream, atts, mixed):
            args = (me, out_time, stream, *atts)
            return call(
                functools.partial(final_kernel, c, top, spots, len(atts)),
                args if mixed is None else (*args, mixed),
                [shaped(frames, rows, width)],
                2 * n * width * q_width,
                [pltpu.VMEM((part, q_width), BF16), pltpu.VMEM((frames, part, width), BF16), pltpu.SemaphoreType.DMA((frames,))],
                anywhere=() if mixed is None else (len(args),),
                out_anywhere=True,
                alias={} if mixed is None else {len(args): 0},
                smem=(0,),
            )[0]

        if not by_partner:
            mixed = None
            for c in range(chunks):
                stream, timed = far_part(c)
                sent = timed.reshape(frames, frame_devices, -1, width).swapaxes(0, 1)
                moved = lax.all_to_all(sent, "frames", 0, 0).reshape(n, width)
                (att,) = call(
                    functools.partial(time_whole_kernel, head, frames, part // frame_devices),
                    (me, qk_time, keyval_time, query_time, moved),
                    [shaped(n, q_width)],
                    2 * n * width * (q_width + 2 * half) + 16 * n * n * q_width,
                    [pltpu.VMEM(s, t) for s, t in (((q_width, n), BF16), ((n + half, max(n, half)), BF16), ((n, n), F32), ((q_width, n), BF16))],
                    smem=(0,),
                )
                back = lax.all_to_all(att.reshape(frame_devices, frames, -1, q_width), "frames", 0, 0)
                back = back.swapaxes(0, 1).reshape(frames, part, q_width)
                mixed = final_part(c, stream, [back], mixed)
            return mixed

        def exchange(xs):
            return [permuted(x, "frames", frame_devices, k) if k else x for k, x in enumerate(xs)]

        sub = n // groups
        streams, moved, projected, back = [], [], [], []
        for c in range(chunks):
            stream, *timed = far_part(c)
            streams.append(stream)
            moved.append(exchange(timed))
        for c in range(chunks):
            q, kv_time = call(
                functools.partial(time_project_kernel, head, frames, spots, groups, top),
                (qk_time, keyval_time, query_time, *moved[c]),
                [shaped(q_width, n), shaped(n + half, half)],
                2 * n * width * (q_width + 2 * half),
            )
            projected.append((q, kv_time, permuted(kv_time, "frames", frame_devices, top)))
        for c in range(chunks):
            atts = call(
                functools.partial(time_attend_kernel, head, frames, spots, groups, top),
                (me, *projected[c]),
                [shaped(frames * spots, q_width)] * top,
                16 * n * 2 * sub * q_width,
                [pltpu.VMEM((2 * sub, sub), F32), pltpu.VMEM((q_width, n), BF16)],
                smem=(0,),
            )
            back.append(exchange(atts))
        mixed = None
        for c in range(chunks):
            mixed = final_part(c, streams[c], back[c], mixed)
        return mixed

    return body


def solution(mesh):
    placed = (P("frames", "band", None),) + (P(),) * 10
    body = make_body(mesh)

    return jax.shard_map(body, mesh=mesh, in_specs=placed, out_specs=P("frames", "band", None), check_vma=False)
```

time: 97.1 us -> 86.6 us (0.89)
  starting transfers between devices: 45.1 us -> 21.4 us
  waiting for transfers between devices: 20.2 us -> 30.8 us
  Pallas kernels: 27.3 us -> 31.6 us
  local copies, waits for them, and re-layouts: 3.87 us -> 2.3 us
    ppermute x31 -> x17, starting transfers between devices: 45.1 us -> 21.4 us  [permuted(): return lax.ppermute(x, axis, [(i, i ^ bit) for i in range(size)])]
    ppermute x31 -> x17, waiting for transfers between devices: 20.2 us -> 30.8 us  [permuted(): return lax.ppermute(x, axis, [(i, i ^ bit) for i in range(size)])]
    pallas_call x8 -> x10, Pallas kernels: 27.3 us -> 31.6 us  [call(): pl.pallas_call(kernel, out_shape=outs, in_specs=in_specs, out_specs=[pl.B...]
    unnamed x26 -> x22, local copies, waits for them, and re-layouts: 3.87 us -> 2.3 us
  transfers between devices with their start and end apart: 31 -> 17, of which waited for: 6 -> 8; matrix products, arithmetic and copies ran while one was open for 0% -> 0% of each run, Pallas kernels for 21% -> 25%
where the time goes in v4:
time: 86.6 us; the launch traced here: 86.4 us
  Pallas kernels  31.6 us (36%)
  waiting for transfers between devices  30.8 us (36%)
  starting transfers between devices  21.4 us (25%)
  local copies, waits for them, and re-layouts  2.3 us (3%)
    pallas_call x10, Pallas kernels, call(): pl.pallas_call(kernel, out_shape=outs, in_specs=in_specs, out_specs=[pl.B...  31.6 us
    ppermute x17, waiting for transfers between devices, permuted(): return lax.ppermute(x, axis, [(i, i ^ bit) for i in range(size)])  30.8 us
    ppermute x17, starting transfers between devices, permuted(): return lax.ppermute(x, axis, [(i, i ^ bit) for i in range(size)])  21.4 us
    unnamed x22, local copies, waits for them, and re-layouts  2.3 us
  transfers between devices with their start and end apart: 17, of which 8 were waited for; matrix products, arithmetic and copies ran while one was open for 0% of the time, Pallas kernels for 25%

profile of v4, /device:TPU:0, one launch (start us, length us, event | category | flops | bytes accessed | tf_op | source)
XLA Modules:
  0.0 86.4 jit_solution(15470331730688733786)
XLA Ops:
  0.0 0.0 copy-start.7
  0.0 0.0 copy-start.8
  0.0 3.8 %shard_map.109 = (bf16[512,1024]{1,0:T(8,128)(2,1)}, bf16[2,512,256]{2,1,0:T(8,128)(2,1)}) custom-call(s32[1]{0:T(128)} %bitcast.me_ref, bf16[2,256,1024]{2,1,0:T(8,128)(2,1)} %x_ref.3, f32[1,1024]{1,0:T(1,128)} %bitcast.5, bf16[1024,512]{1,0:T(8,128)(2,1)} %w_hbm.1, f32[2,64]{1,0:T(2,128)} %gain_ref.3), custom_call_target="tpu_custom_call" | custom-call | flops 536870912 | bytes 3674628 | tf_op jit(solution)/shard_map/pallas_call | solution.py:277
  3.8 3.0 %collective-permute-start.1 = (bf16[2,512,256]{2,1,0:T(8,128)(2,1)}, bf16[2,512,256]{2,1,0:T(8,128)(2,1)S(1)}, u32[]{:S(2)}, u32[]{:S(2)}) collective-permute-start(bf16[2,512,256]{2,1,0:T(8,128)(2,1)} %get-tuple-element.33.refs_0_), channel_id=1, source_target_pairs={{0,2},{1,3},{2,0},{3,1},{4,6},{5,7},{6,4},{7,5},{8,10},{9,11},{10,... | collective-permute-start | bytes 1572872 | tf_op jit(solution)/shard_map/ppermute | solution.py:297
  6.8 0.0 collective-permute-start
  6.8 12.1 %collective-permute-done.1.refs_0_ = bf16[2,512,256]{2,1,0:T(8,128)(2,1)S(1)} collective-permute-done((bf16[2,512,256]{2,1,0:T(8,128)(2,1)}, bf16[2,512,256]{2,1,0:T(8,128)(2,1)S(1)}, u32[]{:S(2)}, u32[]{:S(2)}) %collective-permute-start.1) | collective-permute-done | bytes 524320 | tf_op jit(solution)/shard_map/ppermute | solution.py:297
  19.0 0.0 collective-permute-start.2
  19.0 0.0 collective-permute-done.refs_1_
  19.0 0.0 copy-done.7
  19.0 0.0 copy-done.8
  19.0 0.0 copy-start.9
  19.0 1.2 %copy-done.9 = bf16[512,1024]{1,0:T(8,128)(2,1)S(1)} copy-done((bf16[512,1024]{1,0:T(8,128)(2,1)S(1)}, bf16[512,1024]{1,0:T(8,128)(2,1)}, u32[]{:S(2)}) %copy-start.9) | copy-done | bytes 1048600
  20.2 0.0 copy-start.10
  20.2 1.0 %copy-done.10 = bf16[2,512,256]{2,1,0:T(8,128)(2,1)S(1)} copy-done((bf16[2,512,256]{2,1,0:T(8,128)(2,1)S(1)}, bf16[2,512,256]{2,1,0:T(8,128)(2,1)}, u32[]{:S(2)}) %copy-start.10) | copy-done | bytes 524312
  21.3 0.0 copy-start
  21.3 0.0 copy-start.1
  21.3 7.7 %shard_map.110 = (bf16[2,1024,256]{2,1,0:T(8,128)(2,1)S(1)}, f32[2,1024,256]{2,1,0:T(8,128)S(1)}, f32[2,4,8,256]{3,2,1,0:T(8,128)S(1)}) custom-call(bf16[512,1024]{1,0:T(8,128)(2,1)S(1)} %copy-done.9, bf16[1024,1024]{1,0:T(8,128)(2,1)S(1)} %copy-done.8, f32[2,64]{1,0:T(2,128)S(1)} %copy-done.7, bf16[2,512,256]{2,1,0:T(8,128)(2,1)S(1)} %copy-done.10, ...), custom_call_target="tpu_custom_call" | custom-call | flops 3221225472 | bytes 7406080 | tf_op jit(solution)/shard_map/pallas_call | solution.py:277
  28.9 0.0 collective-permute-done.2.refs_1_
  29.0 0.0 copy-done
  29.0 0.0 copy-done.1
  29.0 0.0 copy-done.5
  29.0 4.5 %shard_map.114 = (bf16[2,128,1024]{2,1,0:T(8,128)(2,1)S(1)}, bf16[64,1024]{1,0:T(8,128)(2,1)S(1)}, bf16[64,1024]{1,0:T(8,128)(2,1)S(1)}, bf16[64,1024]{1,0:T(8,128)(2,1)S(1)}, bf16[64,1024]{1,0:T(8,128)(2,1)S(1)}) custom-call(s32[1]{0:T(128)} %bitcast.me_ref, bf16[2,1024,256]{2,1,0:T(8,128)(2,1)S(1)} %get-tuple-element.34.q_ref, ...), custom_call_target="tpu_custom_call" | custom-call | flops 1610612736 | bytes 8458244 | tf_op jit(solution)/shard_map/pallas_call | solution.py:277
  33.5 1.8 %collective-permute-start.10 = (bf16[64,1024]{1,0:T(8,128)(2,1)S(1)}, bf16[64,1024]{1,0:T(8,128)(2,1)S(1)}, u32[]{:S(2)}, u32[]{:S(2)}) collective-permute-start(bf16[64,1024]{1,0:T(8,128)(2,1)S(1)} %get-tuple-element.50), channel_id=1, source_target_pairs={{0,4},{4,0},{8,12},{12,8},{16,20},{20,16},{24,28},{28,24},{1,5},{5... | collective-permute-start | bytes 393224 | tf_op jit(solution)/shard_map/ppermute | solution.py:297
  35.3 1.6 %collective-permute-start.11 = (bf16[64,1024]{1,0:T(8,128)(2,1)S(1)}, bf16[64,1024]{1,0:T(8,128)(2,1)S(1)}, u32[]{:S(2)}, u32[]{:S(2)}) collective-permute-start(bf16[64,1024]{1,0:T(8,128)(2,1)S(1)} %get-tuple-element.51), channel_id=1, source_target_pairs={{0,8},{4,12},{8,0},{12,4},{16,24},{20,28},{24,16},{28,20},{1,9},{5... | collective-permute-start | bytes 393224 | tf_op jit(solution)/shard_map/ppermute | solution.py:297
  36.9 0.0 copy-start.2
  36.9 0.0 copy-start.4
  36.9 0.2 collective-permute-start.12
  37.1 4.6 %shard_map.111 = (bf16[2,128,1024]{2,1,0:T(8,128)(2,1)S(1)}, bf16[64,1024]{1,0:T(8,128)(2,1)S(1)}, bf16[64,1024]{1,0:T(8,128)(2,1)S(1)}, bf16[64,1024]{1,0:T(8,128)(2,1)S(1)}, bf16[64,1024]{1,0:T(8,128)(2,1)S(1)}) custom-call(s32[1]{0:T(128)} %bitcast.me_ref, bf16[2,1024,256]{2,1,0:T(8,128)(2,1)S(1)} %get-tuple-element.34.q_ref, ...), custom_call_target="tpu_custom_call" | custom-call | flops 1610612736 | bytes 8458244 | tf_op jit(solution)/shard_map/pallas_call | solution.py:277
  41.7 1.8 %collective-permute-start.3 = (bf16[64,1024]{1,0:T(8,128)(2,1)S(1)}, bf16[64,1024]{1,0:T(8,128)(2,1)S(1)}, u32[]{:S(2)}, u32[]{:S(2)}) collective-permute-start(bf16[64,1024]{1,0:T(8,128)(2,1)S(1)} %get-tuple-element.39), channel_id=1, source_target_pairs={{0,4},{4,0},{8,12},{12,8},{16,20},{20,16},{24,28},{28,24},{1,5},{5... | collective-permute-start | bytes 393224 | tf_op jit(solution)/shard_map/ppermute | solution.py:297
  43.5 1.6 %collective-permute-start.4 = (bf16[64,1024]{1,0:T(8,128)(2,1)S(1)}, bf16[64,1024]{1,0:T(8,128)(2,1)S(1)}, u32[]{:S(2)}, u32[]{:S(2)}) collective-permute-start(bf16[64,1024]{1,0:T(8,128)(2,1)S(1)} %get-tuple-element.40), channel_id=1, source_target_pairs={{0,8},{4,12},{8,0},{12,4},{16,24},{20,28},{24,16},{28,20},{1,9},{5... | collective-permute-start | bytes 393224 | tf_op jit(solution)/shard_map/ppermute | solution.py:297
  45.1 0.0 collective-permute-done.10.refs_1_
  45.1 0.2 collective-permute-start.5
  45.3 0.0 collective-permute-done.11.refs_2_
  45.3 0.0 collective-permute-done.12.refs_3_
  45.3 0.0 copy-done.2
  45.3 0.0 copy-done.4
  45.3 0.0 copy-done.6
  45.3 1.2 %shard_map.115 = (bf16[1024,256]{1,0:T(8,128)(2,1)S(1)}, bf16[512,256]{1,0:T(8,128)(2,1)S(1)}) custom-call(f32[2,64]{1,0:T(2,128)S(1)} %copy-done.6, bf16[1024,512]{1,0:T(8,128)(2,1)S(1)} %copy-done.4, bf16[1024,1024]{1,0:T(8,128)(2,1)S(1)} %copy-done.2, bf16[64,1024]{1,0:T(8,128)(2,1)S(1)} %get-tuple-element.49.refs_0_, ...), custom_call_target="tpu_custom_call" | custom-call | flops 805306368 | bytes 4456960 | tf_op jit(solution)/shard_map/pallas_call | solution.py:277
  46.5 2.9 %collective-permute-start.13 = (bf16[512,256]{1,0:T(8,128)(2,1)S(1)}, bf16[512,256]{1,0:T(8,128)(2,1)S(1)}, u32[]{:S(2)}, u32[]{:S(2)}) collective-permute-start(bf16[512,256]{1,0:T(8,128)(2,1)S(1)} %get-tuple-element.54.kv_ref), channel_id=1, source_target_pairs={{0,16},{4,20},{8,24},{12,28},{16,0},{20,4},{24,8},{28,12},{1,17},{... | collective-permute-start | bytes 786440 | tf_op jit(solution)/shard_map/ppermute | solution.py:297
  49.4 0.0 collective-permute-done.3.refs_1_
  49.4 3.2 %collective-permute-done.4.refs_2_ = bf16[64,1024]{1,0:T(8,128)(2,1)S(1)} collective-permute-done((bf16[64,1024]{1,0:T(8,128)(2,1)S(1)}, bf16[64,1024]{1,0:T(8,128)(2,1)S(1)}, u32[]{:S(2)}, u32[]{:S(2)}) %collective-permute-start.4) | collective-permute-done | bytes 131104 | tf_op jit(solution)/shard_map/ppermute | solution.py:297
  52.7 1.2 %collective-permute-done.5.refs_3_ = bf16[64,1024]{1,0:T(8,128)(2,1)S(1)} collective-permute-done((bf16[64,1024]{1,0:T(8,128)(2,1)S(1)}, bf16[64,1024]{1,0:T(8,128)(2,1)S(1)}, u32[]{:S(2)}, u32[]{:S(2)}) %collective-permute-start.5) | collective-permute-done | bytes 131104 | tf_op jit(solution)/shard_map/ppermute | solution.py:297
  53.9 1.2 %shard_map.112 = (bf16[1024,256]{1,0:T(8,128)(2,1)S(1)}, bf16[512,256]{1,0:T(8,128)(2,1)S(1)}) custom-call(f32[2,64]{1,0:T(2,128)S(1)} %copy-done.6, bf16[1024,512]{1,0:T(8,128)(2,1)S(1)} %copy-done.4, bf16[1024,1024]{1,0:T(8,128)(2,1)S(1)} %copy-done.2, bf16[64,1024]{1,0:T(8,128)(2,1)S(1)} %get-tuple-element.38.refs_0_, ...), custom_call_target="tpu_custom_call" | custom-call | flops 805306368 | bytes 4456960 | tf_op jit(solution)/shard_map/pallas_call | solution.py:277
  55.1 1.2 %collective-permute-start.6 = (bf16[512,256]{1,0:T(8,128)(2,1)S(1)}, bf16[512,256]{1,0:T(8,128)(2,1)S(1)}, u32[]{:S(2)}, u32[]{:S(2)}) collective-permute-start(bf16[512,256]{1,0:T(8,128)(2,1)S(1)} %get-tuple-element.43.kv_ref), channel_id=1, source_target_pairs={{0,16},{4,20},{8,24},{12,28},{16,0},{20,4},{24,8},{28,12},{1,17},{... | collective-permute-start | bytes 786440 | tf_op jit(solution)/shard_map/ppermute | solution.py:297
  56.3 11.3 %collective-permute-done.13.kv_other = bf16[512,256]{1,0:T(8,128)(2,1)S(1)} collective-permute-done((bf16[512,256]{1,0:T(8,128)(2,1)S(1)}, bf16[512,256]{1,0:T(8,128)(2,1)S(1)}, u32[]{:S(2)}, u32[]{:S(2)}) %collective-permute-start.13) | collective-permute-done | bytes 262176 | tf_op jit(solution)/shard_map/ppermute | solution.py:297
  67.5 2.8 %shard_map.116 = (bf16[64,1024]{1,0:T(8,128)(2,1)S(1)}, bf16[64,1024]{1,0:T(8,128)(2,1)S(1)}, bf16[64,1024]{1,0:T(8,128)(2,1)S(1)}, bf16[64,1024]{1,0:T(8,128)(2,1)S(1)}) custom-call(s32[1]{0:T(128)} %bitcast.me_ref, bf16[1024,256]{1,0:T(8,128)(2,1)S(1)} %get-tuple-element.53.q_ref, bf16[512,256]{1,0:T(8,128)(2,1)S(1)} %get-tuple-element.54.kv_ref, ...), custom_call_target="tpu_custom_call" | custom-call | flops 1073741824 | bytes 1572868 | tf_op jit(solution)/shard_map/pallas_call | solution.py:277
  70.3 0.0 copy-start.3
  70.3 2.2 %collective-permute-start.14 = (bf16[64,1024]{1,0:T(8,128)(2,1)S(1)}, bf16[64,1024]{1,0:T(8,128)(2,1)S(1)}, u32[]{:S(2)}, u32[]{:S(2)}) collective-permute-start(bf16[64,1024]{1,0:T(8,128)(2,1)S(1)} %get-tuple-element.56), channel_id=1, source_target_pairs={{0,4},{4,0},{8,12},{12,8},{16,20},{20,16},{24,28},{28,24},{1,5},{5... | collective-permute-start | bytes 393224 | tf_op jit(solution)/shard_map/ppermute | solution.py:297
  72.5 0.0 collective-permute-start.15
  72.5 1.5 %collective-permute-start.16 = (bf16[64,1024]{1,0:T(8,128)(2,1)S(1)}, bf16[64,1024]{1,0:T(8,128)(2,1)S(1)}, u32[]{:S(2)}, u32[]{:S(2)}) collective-permute-start(bf16[64,1024]{1,0:T(8,128)(2,1)S(1)} %get-tuple-element.58), channel_id=1, source_target_pairs={{0,12},{4,8},{8,4},{12,0},{16,28},{20,24},{24,20},{28,16},{1,13},{... | collective-permute-start | bytes 393224 | tf_op jit(solution)/shard_map/ppermute | solution.py:297
  74.0 0.0 collective-permute-done.6.kv_other
  74.0 2.8 %shard_map.113 = (bf16[64,1024]{1,0:T(8,128)(2,1)S(1)}, bf16[64,1024]{1,0:T(8,128)(2,1)S(1)}, bf16[64,1024]{1,0:T(8,128)(2,1)S(1)}, bf16[64,1024]{1,0:T(8,128)(2,1)S(1)}) custom-call(s32[1]{0:T(128)} %bitcast.me_ref, bf16[1024,256]{1,0:T(8,128)(2,1)S(1)} %get-tuple-element.42.q_ref, bf16[512,256]{1,0:T(8,128)(2,1)S(1)} %get-tuple-element.43.kv_ref, ...), custom_call_target="tpu_custom_call" | custom-call | flops 1073741824 | bytes 1572868 | tf_op jit(solution)/shard_map/pallas_call | solution.py:277
  76.8 2.0 %collective-permute-start.7 = (bf16[64,1024]{1,0:T(8,128)(2,1)S(1)}, bf16[64,1024]{1,0:T(8,128)(2,1)S(1)}, u32[]{:S(2)}, u32[]{:S(2)}) collective-permute-start(bf16[64,1024]{1,0:T(8,128)(2,1)S(1)} %get-tuple-element.45), channel_id=1, source_target_pairs={{0,4},{4,0},{8,12},{12,8},{16,20},{20,16},{24,28},{28,24},{1,5},{5... | collective-permute-start | bytes 393224 | tf_op jit(solution)/shard_map/ppermute | solution.py:297
  78.8 0.0 collective-permute-start.8
  78.8 0.1 collective-permute-done.14.refs_1_
  78.9 1.5 %collective-permute-start.9 = (bf16[64,1024]{1,0:T(8,128)(2,1)S(1)}, bf16[64,1024]{1,0:T(8,128)(2,1)S(1)}, u32[]{:S(2)}, u32[]{:S(2)}) collective-permute-start(bf16[64,1024]{1,0:T(8,128)(2,1)S(1)} %get-tuple-element.47), channel_id=1, source_target_pairs={{0,12},{4,8},{8,4},{12,0},{16,28},{20,24},{24,20},{28,16},{1,13},{... | collective-permute-start | bytes 393224 | tf_op jit(solution)/shard_map/ppermute | solution.py:297
  80.4 0.0 collective-permute-done.15.refs_2_
  80.4 0.0 collective-permute-done.16.refs_3_
  80.4 0.0 copy-done.3
  80.4 1.5 %shard_map.117.refs_4_ = bf16[2,256,1024]{2,1,0:T(8,128)(2,1)} custom-call(s32[1]{0:T(128)} %bitcast.me_ref, bf16[1024,1024]{1,0:T(8,128)(2,1)S(1)} %copy-done.3, bf16[2,128,1024]{2,1,0:T(8,128)(2,1)S(1)} %get-tuple-element.48.x_ref, bf16[64,1024]{1,0:T(8,128)(2,1)S(1)} %get-tuple-element.55.refs_0_, bf16[64,1024]{1,0:T(8,128)(2,1)S(1)} %collective-permute-done.14.refs_1_, ...), custom_call_target="tpu_custom_call" | custom-call | flops 536870912 | bytes 4194308 | tf_op jit(solution)/shard_map/pallas_call | solution.py:277
  81.9 0.7 collective-permute-done.7.refs_1_
  82.6 1.2 %collective-permute-done.8.refs_2_ = bf16[64,1024]{1,0:T(8,128)(2,1)S(1)} collective-permute-done((bf16[64,1024]{1,0:T(8,128)(2,1)S(1)}, bf16[64,1024]{1,0:T(8,128)(2,1)S(1)}, u32[]{:S(2)}, u32[]{:S(2)}) %collective-permute-start.8) | collective-permute-done | bytes 131104 | tf_op jit(solution)/shard_map/ppermute | solution.py:297
  83.8 1.0 %collective-permute-done.9.refs_3_ = bf16[64,1024]{1,0:T(8,128)(2,1)S(1)} collective-permute-done((bf16[64,1024]{1,0:T(8,128)(2,1)S(1)}, bf16[64,1024]{1,0:T(8,128)(2,1)S(1)}, u32[]{:S(2)}, u32[]{:S(2)}) %collective-permute-start.9) | collective-permute-done | bytes 131104 | tf_op jit(solution)/shard_map/ppermute | solution.py:297
  84.8 1.5 %shard_map.118 = bf16[2,256,1024]{2,1,0:T(8,128)(2,1)} custom-call(s32[1]{0:T(128)} %bitcast.me_ref, bf16[1024,1024]{1,0:T(8,128)(2,1)S(1)} %copy-done.3, bf16[2,128,1024]{2,1,0:T(8,128)(2,1)S(1)} %get-tuple-element.37.x_ref, bf16[64,1024]{1,0:T(8,128)(2,1)S(1)} %get-tuple-element.44.refs_0_, ...), custom_call_target="tpu_custom_call", output_to_operand_aliasing={{}: (7, {})} | custom-call | flops 536870912 | bytes 5242884 | tf_op jit(solution)/shard_map/pallas_call | solution.py:277
  (2 shorter events, 0.0 us)
Async XLA Ops:
  0.0 19.0 %copy-start.7 = (f32[2,64]{1,0:T(2,128)S(1)}, f32[2,64]{1,0:T(2,128)}, u32[]{:S(2)}) copy-start(f32[2,64]{1,0:T(2,128)} %gain_ref.3) | copy-start | bytes 1540
  0.0 19.0 %copy-start.8 = (bf16[1024,1024]{1,0:T(8,128)(2,1)S(1)}, bf16[1024,1024]{1,0:T(8,128)(2,1)}, u32[]{:S(2)}) copy-start(bf16[1024,1024]{1,0:T(8,128)(2,1)} %w_ref.5) | copy-start | bytes 6291460
  3.8 15.2 %collective-permute-start.1 = (bf16[2,512,256]{2,1,0:T(8,128)(2,1)}, bf16[2,512,256]{2,1,0:T(8,128)(2,1)S(1)}, u32[]{:S(2)}, u32[]{:S(2)}) collective-permute-start(bf16[2,512,256]{2,1,0:T(8,128)(2,1)} %get-tuple-element.33.refs_0_), channel_id=1, source_target_pairs={{0,2},{1,3},{2,0},{3,1},{4,6},{5,7},{6,4},{7,5},{8,10},{9,11},{10,... | collective-permute-start | bytes 1572872 | tf_op jit(solution)/shard_map/ppermute | solution.py:297
  6.8 12.1 %collective-permute-start = (bf16[2,512,256]{2,1,0:T(8,128)(2,1)}, bf16[2,512,256]{2,1,0:T(8,128)(2,1)S(1)}, u32[]{:S(2)}, u32[]{:S(2)}) collective-permute-start(bf16[2,512,256]{2,1,0:T(8,128)(2,1)} %get-tuple-element.33.refs_0_), channel_id=1, source_target_pairs={{0,1},{1,0},{2,3},{3,2},{4,5},{5,4},{6,7},{7,6},{8,9},{9,8},{10,11... | collective-permute-start | bytes 1572872 | tf_op jit(solution)/shard_map/ppermute | solution.py:297
  19.0 10.0 %collective-permute-start.2 = (bf16[2,512,256]{2,1,0:T(8,128)(2,1)S(1)}, bf16[2,512,256]{2,1,0:T(8,128)(2,1)S(1)}, u32[]{:S(2)}, u32[]{:S(2)}) collective-permute-start(bf16[2,512,256]{2,1,0:T(8,128)(2,1)S(1)} %collective-permute-done.1.refs_0_), channel_id=1, source_target_pairs={{0,1},{1,0},{2,3},{3,2},{4,5},{5,4},{6,7},{7,6},{8,9},{9,8},{10,11... | collective-permute-start | bytes 1572872 | tf_op jit(solution)/shard_map/ppermute | solution.py:297
  19.0 1.2 %copy-start.9 = (bf16[512,1024]{1,0:T(8,128)(2,1)S(1)}, bf16[512,1024]{1,0:T(8,128)(2,1)}, u32[]{:S(2)}) copy-start(bf16[512,1024]{1,0:T(8,128)(2,1)} %get-tuple-element.32.x_ref) | copy-start | bytes 3145732
  20.2 1.0 %copy-start.10 = (bf16[2,512,256]{2,1,0:T(8,128)(2,1)S(1)}, bf16[2,512,256]{2,1,0:T(8,128)(2,1)}, u32[]{:S(2)}) copy-start(bf16[2,512,256]{2,1,0:T(8,128)(2,1)} %get-tuple-element.33.refs_0_) | copy-start | bytes 1572868
  21.3 7.7 %copy-start = (bf16[2,256,1024]{2,1,0:T(8,128)(2,1)S(1)}, bf16[2,256,1024]{2,1,0:T(8,128)(2,1)}, u32[]{:S(2)}) copy-start(bf16[2,256,1024]{2,1,0:T(8,128)(2,1)} %x_ref.3) | copy-start | bytes 3145732
  21.3 7.7 %copy-start.1 = (bf16[1024,1024]{1,0:T(8,128)(2,1)S(1)}, bf16[1024,1024]{1,0:T(8,128)(2,1)}, u32[]{:S(2)}) copy-start(bf16[1024,1024]{1,0:T(8,128)(2,1)} %w_ref.7) | copy-start | bytes 6291460
  21.3 7.7 %copy-start.5 = (f32[1024]{0:T(1024)S(1)}, f32[1024]{0:T(1024)}, u32[]{:S(2)}) copy-start(f32[1024]{0:T(1024)} %param.17) | copy-start | bytes 12292
  33.5 11.6 %collective-permute-start.10 = (bf16[64,1024]{1,0:T(8,128)(2,1)S(1)}, bf16[64,1024]{1,0:T(8,128)(2,1)S(1)}, u32[]{:S(2)}, u32[]{:S(2)}) collective-permute-start(bf16[64,1024]{1,0:T(8,128)(2,1)S(1)} %get-tuple-element.50), channel_id=1, source_target_pairs={{0,4},{4,0},{8,12},{12,8},{16,20},{20,16},{24,28},{28,24},{1,5},{5... | collective-permute-start | bytes 393224 | tf_op jit(solution)/shard_map/ppermute | solution.py:297
  35.3 9.9 %collective-permute-start.11 = (bf16[64,1024]{1,0:T(8,128)(2,1)S(1)}, bf16[64,1024]{1,0:T(8,128)(2,1)S(1)}, u32[]{:S(2)}, u32[]{:S(2)}) collective-permute-start(bf16[64,1024]{1,0:T(8,128)(2,1)S(1)} %get-tuple-element.51), channel_id=1, source_target_pairs={{0,8},{4,12},{8,0},{12,4},{16,24},{20,28},{24,16},{28,20},{1,9},{5... | collective-permute-start | bytes 393224 | tf_op jit(solution)/shard_map/ppermute | solution.py:297
  36.9 8.4 %copy-start.2 = (bf16[1024,1024]{1,0:T(8,128)(2,1)S(1)}, bf16[1024,1024]{1,0:T(8,128)(2,1)}, u32[]{:S(2)}) copy-start(bf16[1024,1024]{1,0:T(8,128)(2,1)} %wq_ref.3) | copy-start | bytes 6291460
  36.9 8.4 %copy-start.4 = (bf16[1024,512]{1,0:T(8,128)(2,1)S(1)}, bf16[1024,512]{1,0:T(8,128)(2,1)}, u32[]{:S(2)}) copy-start(bf16[1024,512]{1,0:T(8,128)(2,1)} %wkv_ref.3) | copy-start | bytes 3145732
  36.9 8.4 %copy-start.6 = (f32[2,64]{1,0:T(2,128)S(1)}, f32[2,64]{1,0:T(2,128)}, u32[]{:S(2)}) copy-start(f32[2,64]{1,0:T(2,128)} %gain_ref.5) | copy-start | bytes 1540
  36.9 8.4 %collective-permute-start.12 = (bf16[64,1024]{1,0:T(8,128)(2,1)S(1)}, bf16[64,1024]{1,0:T(8,128)(2,1)S(1)}, u32[]{:S(2)}, u32[]{:S(2)}) collective-permute-start(bf16[64,1024]{1,0:T(8,128)(2,1)S(1)} %get-tuple-element.52), channel_id=1, source_target_pairs={{0,12},{4,8},{8,4},{12,0},{16,28},{20,24},{24,20},{28,16},{1,13},{... | collective-permute-start | bytes 393224 | tf_op jit(solution)/shard_map/ppermute | solution.py:297
  41.7 7.7 %collective-permute-start.3 = (bf16[64,1024]{1,0:T(8,128)(2,1)S(1)}, bf16[64,1024]{1,0:T(8,128)(2,1)S(1)}, u32[]{:S(2)}, u32[]{:S(2)}) collective-permute-start(bf16[64,1024]{1,0:T(8,128)(2,1)S(1)} %get-tuple-element.39), channel_id=1, source_target_pairs={{0,4},{4,0},{8,12},{12,8},{16,20},{20,16},{24,28},{28,24},{1,5},{5... | collective-permute-start | bytes 393224 | tf_op jit(solution)/shard_map/ppermute | solution.py:297
  43.5 9.1 %collective-permute-start.4 = (bf16[64,1024]{1,0:T(8,128)(2,1)S(1)}, bf16[64,1024]{1,0:T(8,128)(2,1)S(1)}, u32[]{:S(2)}, u32[]{:S(2)}) collective-permute-start(bf16[64,1024]{1,0:T(8,128)(2,1)S(1)} %get-tuple-element.40), channel_id=1, source_target_pairs={{0,8},{4,12},{8,0},{12,4},{16,24},{20,28},{24,16},{28,20},{1,9},{5... | collective-permute-start | bytes 393224 | tf_op jit(solution)/shard_map/ppermute | solution.py:297
  45.1 8.8 %collective-permute-start.5 = (bf16[64,1024]{1,0:T(8,128)(2,1)S(1)}, bf16[64,1024]{1,0:T(8,128)(2,1)S(1)}, u32[]{:S(2)}, u32[]{:S(2)}) collective-permute-start(bf16[64,1024]{1,0:T(8,128)(2,1)S(1)} %get-tuple-element.41), channel_id=1, source_target_pairs={{0,12},{4,8},{8,4},{12,0},{16,28},{20,24},{24,20},{28,16},{1,13},{... | collective-permute-start | bytes 393224 | tf_op jit(solution)/shard_map/ppermute | solution.py:297
  46.5 21.0 %collective-permute-start.13 = (bf16[512,256]{1,0:T(8,128)(2,1)S(1)}, bf16[512,256]{1,0:T(8,128)(2,1)S(1)}, u32[]{:S(2)}, u32[]{:S(2)}) collective-permute-start(bf16[512,256]{1,0:T(8,128)(2,1)S(1)} %get-tuple-element.54.kv_ref), channel_id=1, source_target_pairs={{0,16},{4,20},{8,24},{12,28},{16,0},{20,4},{24,8},{28,12},{1,17},{... | collective-permute-start | bytes 786440 | tf_op jit(solution)/shard_map/ppermute | solution.py:297
  55.1 18.9 %collective-permute-start.6 = (bf16[512,256]{1,0:T(8,128)(2,1)S(1)}, bf16[512,256]{1,0:T(8,128)(2,1)S(1)}, u32[]{:S(2)}, u32[]{:S(2)}) collective-permute-start(bf16[512,256]{1,0:T(8,128)(2,1)S(1)} %get-tuple-element.43.kv_ref), channel_id=1, source_target_pairs={{0,16},{4,20},{8,24},{12,28},{16,0},{20,4},{24,8},{28,12},{1,17},{... | collective-permute-start | bytes 786440 | tf_op jit(solution)/shard_map/ppermute | solution.py:297
  70.3 10.1 %copy-start.3 = (bf16[1024,1024]{1,0:T(8,128)(2,1)S(1)}, bf16[1024,1024]{1,0:T(8,128)(2,1)}, u32[]{:S(2)}) copy-start(bf16[1024,1024]{1,0:T(8,128)(2,1)} %w_ref.9) | copy-start | bytes 6291460
  70.3 8.6 %collective-permute-start.14 = (bf16[64,1024]{1,0:T(8,128)(2,1)S(1)}, bf16[64,1024]{1,0:T(8,128)(2,1)S(1)}, u32[]{:S(2)}, u32[]{:S(2)}) collective-permute-start(bf16[64,1024]{1,0:T(8,128)(2,1)S(1)} %get-tuple-element.56), channel_id=1, source_target_pairs={{0,4},{4,0},{8,12},{12,8},{16,20},{20,16},{24,28},{28,24},{1,5},{5... | collective-permute-start | bytes 393224 | tf_op jit(solution)/shard_map/ppermute | solution.py:297
  72.5 7.9 %collective-permute-start.15 = (bf16[64,1024]{1,0:T(8,128)(2,1)S(1)}, bf16[64,1024]{1,0:T(8,128)(2,1)S(1)}, u32[]{:S(2)}, u32[]{:S(2)}) collective-permute-start(bf16[64,1024]{1,0:T(8,128)(2,1)S(1)} %get-tuple-element.57), channel_id=1, source_target_pairs={{0,8},{4,12},{8,0},{12,4},{16,24},{20,28},{24,16},{28,20},{1,9},{5... | collective-permute-start | bytes 393224 | tf_op jit(solution)/shard_map/ppermute | solution.py:297
  72.5 7.9 %collective-permute-start.16 = (bf16[64,1024]{1,0:T(8,128)(2,1)S(1)}, bf16[64,1024]{1,0:T(8,128)(2,1)S(1)}, u32[]{:S(2)}, u32[]{:S(2)}) collective-permute-start(bf16[64,1024]{1,0:T(8,128)(2,1)S(1)} %get-tuple-element.58), channel_id=1, source_target_pairs={{0,12},{4,8},{8,4},{12,0},{16,28},{20,24},{24,20},{28,16},{1,13},{... | collective-permute-start | bytes 393224 | tf_op jit(solution)/shard_map/ppermute | solution.py:297
  76.8 5.8 %collective-permute-start.7 = (bf16[64,1024]{1,0:T(8,128)(2,1)S(1)}, bf16[64,1024]{1,0:T(8,128)(2,1)S(1)}, u32[]{:S(2)}, u32[]{:S(2)}) collective-permute-start(bf16[64,1024]{1,0:T(8,128)(2,1)S(1)} %get-tuple-element.45), channel_id=1, source_target_pairs={{0,4},{4,0},{8,12},{12,8},{16,20},{20,16},{24,28},{28,24},{1,5},{5... | collective-permute-start | bytes 393224 | tf_op jit(solution)/shard_map/ppermute | solution.py:297
  78.8 5.0 %collective-permute-start.8 = (bf16[64,1024]{1,0:T(8,128)(2,1)S(1)}, bf16[64,1024]{1,0:T(8,128)(2,1)S(1)}, u32[]{:S(2)}, u32[]{:S(2)}) collective-permute-start(bf16[64,1024]{1,0:T(8,128)(2,1)S(1)} %get-tuple-element.46), channel_id=1, source_target_pairs={{0,8},{4,12},{8,0},{12,4},{16,24},{20,28},{24,16},{28,20},{1,9},{5... | collective-permute-start | bytes 393224 | tf_op jit(solution)/shard_map/ppermute | solution.py:297
  78.9 5.9 %collective-permute-start.9 = (bf16[64,1024]{1,0:T(8,128)(2,1)S(1)}, bf16[64,1024]{1,0:T(8,128)(2,1)S(1)}, u32[]{:S(2)}, u32[]{:S(2)}) collective-permute-start(bf16[64,1024]{1,0:T(8,128)(2,1)S(1)} %get-tuple-element.47), channel_id=1, source_target_pairs={{0,12},{4,8},{8,4},{12,0},{16,28},{20,24},{24,20},{28,16},{1,13},{... | collective-permute-start | bytes 393224 | tf_op jit(solution)/shard_map/ppermute | solution.py:297

commit v5 on v4

--- a/solution.py
+++ b/solution.py
@@ -52,7 +52,7 @@
     return jnp.concatenate([padded(q, odd) for q in heads], axis=1)
 
 
-def keyval_kernel(me_ref, x_hbm, norm_hbm, w_hbm, gain_hbm, normed_ref, kv_ref, x_ref, norm_ref, w_ref, gain_ref, sems):
+def keyval_kernel(me_ref, x_hbm, norm_hbm, w_hbm, gain_hbm, kv_hbm, x_ref, norm_ref, w_ref, gain_ref, kv_ref, sems, out_sems):
     frames, rows = x_hbm.shape[0], x_hbm.shape[1]
     half = w_ref.shape[1] // 2
     small = [pltpu.make_async_copy(norm_hbm, norm_ref, sems.at[frames]), pltpu.make_async_copy(gain_hbm, gain_ref, sems.at[frames + 1])]
@@ -63,16 +63,19 @@
     for copy in small:
         copy.wait()
     gain = column(gain_ref[1:2, :])
+    outs = []
     for f in range(frames):
         x_copies[f].wait()
-        part = slice(f * rows, (f + 1) * rows)
         normed = row_rms(x_ref[f], norm_ref[...]).astype(BF16)
-        normed_ref[part] = normed
         if f == 0:
             w_copy.wait()
         kv = dot(normed, w_ref[...]).T
         kv_ref[f, :rows] = feature_rms(kv[:half], gain).T.astype(BF16)
         kv_ref[f, rows:] = kv[half:].astype(BF16)
+        outs.append(pltpu.make_async_copy(kv_ref.at[f], kv_hbm.at[f], out_sems.at[f]))
+        outs[-1].start()
+    for copy in outs:
+        copy.wait()
 
 
 def over_key_heads(frames, kv_heads, score, finish, bufs):
@@ -84,28 +87,33 @@
 
     score(0, 0, False, bufs[0])
 
-    def step(n, carry):
+    def half_step(n):
         f, g = split(n)
-        f_next, g_next = split(jnp.minimum(n + 1, total - 1))
         score(f, g + 1, True, bufs[1])
         finish(f, g, bufs[0])
-        score(f_next, g_next, False, bufs[0])
+
+    def step(n, carry):
+        half_step(n)
+        f, g = split(n)
+        score(*split(n + 1), False, bufs[0])
         finish(f, g + 1, bufs[1])
         return carry
 
-    lax.fori_loop(0, total, step, 0)
-
-
-def near_kernel(head, pieces, x_ref, w_ref, gain_ref, *refs):
+    lax.fori_loop(0, total - 1, step, 0)
+    half_step(total - 1)
+    f, g = split(total - 1)
+    finish(f, g + 1, bufs[1])
+
+
+def near_kernel(head, pieces, x_ref, norm_ref, w_ref, gain_ref, *refs):
     kv_refs, refs = refs[:pieces], refs[pieces:]
     q_ref, o_ref, ml_ref, s0, s1 = refs
-    frames, rows = kv_refs[0].shape[0], x_ref.shape[0] // kv_refs[0].shape[0]
-    half = kv_refs[0].shape[2]
+    frames, rows, half = x_ref.shape[0], x_ref.shape[1], kv_refs[0].shape[2]
     heads, kv_heads = w_ref.shape[1] // head, half // head
     group, wide = heads // kv_heads, 2 * head
     gain = column(gain_ref[0:1, :])
     for f in range(frames):
-        q = dot(x_ref[f * rows : (f + 1) * rows], w_ref[...]).T
+        q = dot(row_rms(x_ref[f], norm_ref[...]).astype(BF16), w_ref[...]).T
         q_ref[f] = (feature_rms(q, gain).astype(BF16).astype(F32) * head**-0.5).astype(BF16)
 
     def score(f, g, odd, buf):
@@ -286,7 +294,7 @@
     )(*args)
 
 
-FIRST_ROOM = 57 << 20
+FIRST_ROOM = 62976 << 10
 
 
 def shaped(*dims, dtype=BF16):
@@ -315,18 +323,21 @@
         index = lax.axis_index("frames").astype(jnp.int32).reshape(1)
         me = index if by_partner else jnp.zeros((1,), jnp.int32)
 
-        normed, kv = call(
+        (kv,) = call(
             keyval_kernel,
             (index, tokens, norm_space, keyval_space, qk_space),
-            [shaped(flat, width), shaped(frames, rows + half, half)],
+            [shaped(frames, rows + half, half)],
             4 * flat * width * half,
             [
                 pltpu.VMEM(tokens.shape, BF16),
                 pltpu.VMEM((1, width), F32),
                 pltpu.VMEM(keyval_space.shape, BF16),
                 pltpu.VMEM(qk_space.shape, F32),
+                pltpu.VMEM((frames, rows + half, half), BF16),
                 pltpu.SemaphoreType.DMA((frames + 3,)),
+                pltpu.SemaphoreType.DMA((frames,)),
             ],
+            out_anywhere=True,
             anywhere=(1, 2, 3, 4),
             smem=(0,),
             room=FIRST_ROOM,
@@ -342,7 +353,7 @@
         near_keys, far_keys = rows * len(near), rows * len(far)
         state = call(
             functools.partial(near_kernel, head, len(near)),
-            (normed, query_space, qk_space, *near),
+            (tokens, norm_space, query_space, qk_space, *near),
             [shaped(frames, q_width, rows), shaped(frames, q_width, rows, dtype=F32), shaped(frames, half // head, 2 * q_width // half, rows, dtype=F32)],
             2 * flat * width * q_width + 8 * flat * near_keys * q_width,
             [pltpu.VMEM((near_keys, rows * (q_width // half)), F32)] * 2,

time: 86.6 us -> 84.8 us (0.979)
  Pallas kernels: 31.6 us -> 29.4 us
    pallas_call x10, Pallas kernels: 31.6 us -> 29.4 us  [call(): pl.pallas_call(kernel, out_shape=outs, in_specs=in_specs, out_specs=[pl.B...]
  transfers between devices with their start and end apart: 17 -> 17, of which waited for: 8 -> 8; matrix products, arithmetic and copies ran while one was open for 0% -> 0% of each run, Pallas kernels for 25% -> 24%
where the time goes in v5:
time: 84.8 us; the launch traced here: 84.6 us
  waiting for transfers between devices  30.7 us (36%)
  Pallas kernels  29.4 us (35%)
  starting transfers between devices  21.5 us (25%)
  local copies, waits for them, and re-layouts  2.67 us (3%)
    ppermute x17, waiting for transfers between devices, permuted(): return lax.ppermute(x, axis, [(i, i ^ bit) for i in range(size)])  30.7 us
    pallas_call x10, Pallas kernels, call(): pl.pallas_call(kernel, out_shape=outs, in_specs=in_specs, out_specs=[pl.B...  29.4 us
    ppermute x17, starting transfers between devices, permuted(): return lax.ppermute(x, axis, [(i, i ^ bit) for i in range(size)])  21.5 us
    unnamed x22, local copies, waits for them, and re-layouts  2.67 us
  transfers between devices with their start and end apart: 17, of which 8 were waited for; matrix products, arithmetic and copies ran while one was open for 0% of the time, Pallas kernels for 24%

profile of v5, /device:TPU:0, one launch (start us, length us, event | category | flops | bytes accessed | tf_op | source)
XLA Modules:
  0.0 84.6 jit_solution(13792957747708145887)
XLA Ops:
  0.0 0.0 copy-start
  0.0 0.0 copy-start.7
  0.0 0.0 copy-start.9
  0.0 0.0 copy-start.6
  0.0 3.6 %shard_map.109.refs_0_ = bf16[2,512,256]{2,1,0:T(8,128)(2,1)} custom-call(s32[1]{0:T(128)} %bitcast.me_ref, bf16[2,256,1024]{2,1,0:T(8,128)(2,1)} %x_ref.5, f32[1,1024]{1,0:T(1,128)} %bitcast.5, bf16[1024,512]{1,0:T(8,128)(2,1)} %w_hbm.1, f32[2,64]{1,0:T(2,128)} %gain_ref.3), custom_call_target="tpu_custom_call" | custom-call | flops 536870912 | bytes 2626052 | tf_op jit(solution)/shard_map/pallas_call | solution.py:285
  3.7 0.0 copy-start.1
  3.7 3.0 %collective-permute-start.1 = (bf16[2,512,256]{2,1,0:T(8,128)(2,1)}, bf16[2,512,256]{2,1,0:T(8,128)(2,1)S(1)}, u32[]{:S(2)}, u32[]{:S(2)}) collective-permute-start(bf16[2,512,256]{2,1,0:T(8,128)(2,1)} %shard_map.109.refs_0_), channel_id=1, source_target_pairs={{0,2},{1,3},{2,0},{3,1},{4,6},{5,7},{6,4},{7,5},{8,10},{9,11},{10,... | collective-permute-start | bytes 1572872 | tf_op jit(solution)/shard_map/ppermute | solution.py:305
  6.7 0.0 collective-permute-start
  6.7 12.1 %collective-permute-done.1.refs_0_ = bf16[2,512,256]{2,1,0:T(8,128)(2,1)S(1)} collective-permute-done((bf16[2,512,256]{2,1,0:T(8,128)(2,1)}, bf16[2,512,256]{2,1,0:T(8,128)(2,1)S(1)}, u32[]{:S(2)}, u32[]{:S(2)}) %collective-permute-start.1) | collective-permute-done | bytes 524320 | tf_op jit(solution)/shard_map/ppermute | solution.py:305
  18.9 0.0 collective-permute-start.2
  18.9 0.0 collective-permute-done.refs_1_
  18.9 0.0 copy-done
  18.9 0.0 copy-done.7
  18.9 0.0 copy-done.9
  18.9 0.0 copy-start.5
  18.9 1.0 %copy-done.5 = bf16[2,512,256]{2,1,0:T(8,128)(2,1)S(1)} copy-done((bf16[2,512,256]{2,1,0:T(8,128)(2,1)S(1)}, bf16[2,512,256]{2,1,0:T(8,128)(2,1)}, u32[]{:S(2)}) %copy-start.5) | copy-done | bytes 524312
  19.9 0.0 copy-start.10
  19.9 1.6 %copy-done.10 = bf16[1024,1024]{1,0:T(8,128)(2,1)S(1)} copy-done((bf16[1024,1024]{1,0:T(8,128)(2,1)S(1)}, bf16[1024,1024]{1,0:T(8,128)(2,1)}, u32[]{:S(2)}) %copy-start.10) | copy-done | bytes 2097176
  21.5 6.7 %shard_map.110 = (bf16[2,1024,256]{2,1,0:T(8,128)(2,1)S(1)}, f32[2,1024,256]{2,1,0:T(8,128)S(1)}, f32[2,4,8,256]{3,2,1,0:T(8,128)S(1)}) custom-call(bf16[2,256,1024]{2,1,0:T(8,128)(2,1)S(1)} %copy-done, f32[1,1024]{1,0:T(1,128)S(1)} %bitcast.6, bf16[1024,1024]{1,0:T(8,128)(2,1)S(1)} %copy-done.10, f32[2,64]{1,0:T(2,128)S(1)} %copy-done.9, ...), custom_call_target="tpu_custom_call" | custom-call | flops 3221225472 | bytes 7410176 | tf_op jit(solution)/shard_map/pallas_call | solution.py:285
  28.2 0.0 collective-permute-done.2.refs_1_
  28.2 0.0 copy-done.6
  28.2 0.0 copy-done.1
  28.2 4.0 %shard_map.114 = (bf16[2,128,1024]{2,1,0:T(8,128)(2,1)S(1)}, bf16[64,1024]{1,0:T(8,128)(2,1)S(1)}, bf16[64,1024]{1,0:T(8,128)(2,1)S(1)}, bf16[64,1024]{1,0:T(8,128)(2,1)S(1)}, bf16[64,1024]{1,0:T(8,128)(2,1)S(1)}) custom-call(s32[1]{0:T(128)} %bitcast.me_ref, bf16[2,1024,256]{2,1,0:T(8,128)(2,1)S(1)} %get-tuple-element.30.q_ref, ...), custom_call_target="tpu_custom_call" | custom-call | flops 1610612736 | bytes 8458244 | tf_op jit(solution)/shard_map/pallas_call | solution.py:285
  32.2 1.8 %collective-permute-start.10 = (bf16[64,1024]{1,0:T(8,128)(2,1)S(1)}, bf16[64,1024]{1,0:T(8,128)(2,1)S(1)}, u32[]{:S(2)}, u32[]{:S(2)}) collective-permute-start(bf16[64,1024]{1,0:T(8,128)(2,1)S(1)} %get-tuple-element.46), channel_id=1, source_target_pairs={{0,4},{4,0},{8,12},{12,8},{16,20},{20,16},{24,28},{28,24},{1,5},{5... | collective-permute-start | bytes 393224 | tf_op jit(solution)/shard_map/ppermute | solution.py:305
  34.0 1.6 %collective-permute-start.11 = (bf16[64,1024]{1,0:T(8,128)(2,1)S(1)}, bf16[64,1024]{1,0:T(8,128)(2,1)S(1)}, u32[]{:S(2)}, u32[]{:S(2)}) collective-permute-start(bf16[64,1024]{1,0:T(8,128)(2,1)S(1)} %get-tuple-element.47), channel_id=1, source_target_pairs={{0,8},{4,12},{8,0},{12,4},{16,24},{20,28},{24,16},{28,20},{1,9},{5... | collective-permute-start | bytes 393224 | tf_op jit(solution)/shard_map/ppermute | solution.py:305
  35.6 0.0 copy-start.2
  35.6 0.1 collective-permute-start.12
  35.8 4.2 %shard_map.111 = (bf16[2,128,1024]{2,1,0:T(8,128)(2,1)S(1)}, bf16[64,1024]{1,0:T(8,128)(2,1)S(1)}, bf16[64,1024]{1,0:T(8,128)(2,1)S(1)}, bf16[64,1024]{1,0:T(8,128)(2,1)S(1)}, bf16[64,1024]{1,0:T(8,128)(2,1)S(1)}) custom-call(s32[1]{0:T(128)} %bitcast.me_ref, bf16[2,1024,256]{2,1,0:T(8,128)(2,1)S(1)} %get-tuple-element.30.q_ref, ...), custom_call_target="tpu_custom_call" | custom-call | flops 1610612736 | bytes 8458244 | tf_op jit(solution)/shard_map/pallas_call | solution.py:285
  39.9 1.8 %collective-permute-start.3 = (bf16[64,1024]{1,0:T(8,128)(2,1)S(1)}, bf16[64,1024]{1,0:T(8,128)(2,1)S(1)}, u32[]{:S(2)}, u32[]{:S(2)}) collective-permute-start(bf16[64,1024]{1,0:T(8,128)(2,1)S(1)} %get-tuple-element.35), channel_id=1, source_target_pairs={{0,4},{4,0},{8,12},{12,8},{16,20},{20,16},{24,28},{28,24},{1,5},{5... | collective-permute-start | bytes 393224 | tf_op jit(solution)/shard_map/ppermute | solution.py:305
  41.8 1.6 %collective-permute-start.4 = (bf16[64,1024]{1,0:T(8,128)(2,1)S(1)}, bf16[64,1024]{1,0:T(8,128)(2,1)S(1)}, u32[]{:S(2)}, u32[]{:S(2)}) collective-permute-start(bf16[64,1024]{1,0:T(8,128)(2,1)S(1)} %get-tuple-element.36), channel_id=1, source_target_pairs={{0,8},{4,12},{8,0},{12,4},{16,24},{20,28},{24,16},{28,20},{1,9},{5... | collective-permute-start | bytes 393224 | tf_op jit(solution)/shard_map/ppermute | solution.py:305
  43.3 0.0 collective-permute-done.10.refs_1_
  43.3 0.1 collective-permute-start.5
  43.5 0.0 collective-permute-done.11.refs_2_
  43.5 0.0 collective-permute-done.12.refs_3_
  43.5 0.0 copy-done.2
  43.5 0.0 copy-done.4
  43.5 0.0 copy-done.8
  43.5 1.2 %shard_map.115 = (bf16[1024,256]{1,0:T(8,128)(2,1)S(1)}, bf16[512,256]{1,0:T(8,128)(2,1)S(1)}) custom-call(f32[2,64]{1,0:T(2,128)S(1)} %copy-done.8, bf16[1024,512]{1,0:T(8,128)(2,1)S(1)} %copy-done.4, bf16[1024,1024]{1,0:T(8,128)(2,1)S(1)} %copy-done.2, bf16[64,1024]{1,0:T(8,128)(2,1)S(1)} %get-tuple-element.45.refs_0_, ...), custom_call_target="tpu_custom_call" | custom-call | flops 805306368 | bytes 4456960 | tf_op jit(solution)/shard_map/pallas_call | solution.py:285
  44.7 2.9 %collective-permute-start.13 = (bf16[512,256]{1,0:T(8,128)(2,1)S(1)}, bf16[512,256]{1,0:T(8,128)(2,1)S(1)}, u32[]{:S(2)}, u32[]{:S(2)}) collective-permute-start(bf16[512,256]{1,0:T(8,128)(2,1)S(1)} %get-tuple-element.50.kv_ref), channel_id=1, source_target_pairs={{0,16},{4,20},{8,24},{12,28},{16,0},{20,4},{24,8},{28,12},{1,17},{... | collective-permute-start | bytes 786440 | tf_op jit(solution)/shard_map/ppermute | solution.py:305
  47.6 0.0 collective-permute-done.3.refs_1_
  47.6 3.3 %collective-permute-done.4.refs_2_ = bf16[64,1024]{1,0:T(8,128)(2,1)S(1)} collective-permute-done((bf16[64,1024]{1,0:T(8,128)(2,1)S(1)}, bf16[64,1024]{1,0:T(8,128)(2,1)S(1)}, u32[]{:S(2)}, u32[]{:S(2)}) %collective-permute-start.4) | collective-permute-done | bytes 131104 | tf_op jit(solution)/shard_map/ppermute | solution.py:305
  51.0 1.1 %collective-permute-done.5.refs_3_ = bf16[64,1024]{1,0:T(8,128)(2,1)S(1)} collective-permute-done((bf16[64,1024]{1,0:T(8,128)(2,1)S(1)}, bf16[64,1024]{1,0:T(8,128)(2,1)S(1)}, u32[]{:S(2)}, u32[]{:S(2)}) %collective-permute-start.5) | collective-permute-done | bytes 131104 | tf_op jit(solution)/shard_map/ppermute | solution.py:305
  52.1 1.2 %shard_map.112 = (bf16[1024,256]{1,0:T(8,128)(2,1)S(1)}, bf16[512,256]{1,0:T(8,128)(2,1)S(1)}) custom-call(f32[2,64]{1,0:T(2,128)S(1)} %copy-done.8, bf16[1024,512]{1,0:T(8,128)(2,1)S(1)} %copy-done.4, bf16[1024,1024]{1,0:T(8,128)(2,1)S(1)} %copy-done.2, bf16[64,1024]{1,0:T(8,128)(2,1)S(1)} %get-tuple-element.34.refs_0_, ...), custom_call_target="tpu_custom_call" | custom-call | flops 805306368 | bytes 4456960 | tf_op jit(solution)/shard_map/pallas_call | solution.py:285
  53.3 1.2 %collective-permute-start.6 = (bf16[512,256]{1,0:T(8,128)(2,1)S(1)}, bf16[512,256]{1,0:T(8,128)(2,1)S(1)}, u32[]{:S(2)}, u32[]{:S(2)}) collective-permute-start(bf16[512,256]{1,0:T(8,128)(2,1)S(1)} %get-tuple-element.39.kv_ref), channel_id=1, source_target_pairs={{0,16},{4,20},{8,24},{12,28},{16,0},{20,4},{24,8},{28,12},{1,17},{... | collective-permute-start | bytes 786440 | tf_op jit(solution)/shard_map/ppermute | solution.py:305
  54.5 11.2 %collective-permute-done.13.kv_other = bf16[512,256]{1,0:T(8,128)(2,1)S(1)} collective-permute-done((bf16[512,256]{1,0:T(8,128)(2,1)S(1)}, bf16[512,256]{1,0:T(8,128)(2,1)S(1)}, u32[]{:S(2)}, u32[]{:S(2)}) %collective-permute-start.13) | collective-permute-done | bytes 262176 | tf_op jit(solution)/shard_map/ppermute | solution.py:305
  65.7 2.8 %shard_map.116 = (bf16[64,1024]{1,0:T(8,128)(2,1)S(1)}, bf16[64,1024]{1,0:T(8,128)(2,1)S(1)}, bf16[64,1024]{1,0:T(8,128)(2,1)S(1)}, bf16[64,1024]{1,0:T(8,128)(2,1)S(1)}) custom-call(s32[1]{0:T(128)} %bitcast.me_ref, bf16[1024,256]{1,0:T(8,128)(2,1)S(1)} %get-tuple-element.49.q_ref, bf16[512,256]{1,0:T(8,128)(2,1)S(1)} %get-tuple-element.50.kv_ref, ...), custom_call_target="tpu_custom_call" | custom-call | flops 1073741824 | bytes 1572868 | tf_op jit(solution)/shard_map/pallas_call | solution.py:285
  68.5 0.0 copy-start.3
  68.5 2.2 %collective-permute-start.14 = (bf16[64,1024]{1,0:T(8,128)(2,1)S(1)}, bf16[64,1024]{1,0:T(8,128)(2,1)S(1)}, u32[]{:S(2)}, u32[]{:S(2)}) collective-permute-start(bf16[64,1024]{1,0:T(8,128)(2,1)S(1)} %get-tuple-element.52), channel_id=1, source_target_pairs={{0,4},{4,0},{8,12},{12,8},{16,20},{20,16},{24,28},{28,24},{1,5},{5... | collective-permute-start | bytes 393224 | tf_op jit(solution)/shard_map/ppermute | solution.py:305
  70.7 0.0 collective-permute-start.15
  70.7 1.5 %collective-permute-start.16 = (bf16[64,1024]{1,0:T(8,128)(2,1)S(1)}, bf16[64,1024]{1,0:T(8,128)(2,1)S(1)}, u32[]{:S(2)}, u32[]{:S(2)}) collective-permute-start(bf16[64,1024]{1,0:T(8,128)(2,1)S(1)} %get-tuple-element.54), channel_id=1, source_target_pairs={{0,12},{4,8},{8,4},{12,0},{16,28},{20,24},{24,20},{28,16},{1,13},{... | collective-permute-start | bytes 393224 | tf_op jit(solution)/shard_map/ppermute | solution.py:305
  72.2 0.0 collective-permute-done.6.kv_other
  72.2 2.8 %shard_map.113 = (bf16[64,1024]{1,0:T(8,128)(2,1)S(1)}, bf16[64,1024]{1,0:T(8,128)(2,1)S(1)}, bf16[64,1024]{1,0:T(8,128)(2,1)S(1)}, bf16[64,1024]{1,0:T(8,128)(2,1)S(1)}) custom-call(s32[1]{0:T(128)} %bitcast.me_ref, bf16[1024,256]{1,0:T(8,128)(2,1)S(1)} %get-tuple-element.38.q_ref, bf16[512,256]{1,0:T(8,128)(2,1)S(1)} %get-tuple-element.39.kv_ref, ...), custom_call_target="tpu_custom_call" | custom-call | flops 1073741824 | bytes 1572868 | tf_op jit(solution)/shard_map/pallas_call | solution.py:285
  75.0 2.0 %collective-permute-start.7 = (bf16[64,1024]{1,0:T(8,128)(2,1)S(1)}, bf16[64,1024]{1,0:T(8,128)(2,1)S(1)}, u32[]{:S(2)}, u32[]{:S(2)}) collective-permute-start(bf16[64,1024]{1,0:T(8,128)(2,1)S(1)} %get-tuple-element.41), channel_id=1, source_target_pairs={{0,4},{4,0},{8,12},{12,8},{16,20},{20,16},{24,28},{28,24},{1,5},{5... | collective-permute-start | bytes 393224 | tf_op jit(solution)/shard_map/ppermute | solution.py:305
  77.1 0.0 collective-permute-start.8
  77.1 0.1 collective-permute-done.14.refs_1_
  77.1 1.5 %collective-permute-start.9 = (bf16[64,1024]{1,0:T(8,128)(2,1)S(1)}, bf16[64,1024]{1,0:T(8,128)(2,1)S(1)}, u32[]{:S(2)}, u32[]{:S(2)}) collective-permute-start(bf16[64,1024]{1,0:T(8,128)(2,1)S(1)} %get-tuple-element.43), channel_id=1, source_target_pairs={{0,12},{4,8},{8,4},{12,0},{16,28},{20,24},{24,20},{28,16},{1,13},{... | collective-permute-start | bytes 393224 | tf_op jit(solution)/shard_map/ppermute | solution.py:305
  78.6 0.0 collective-permute-done.15.refs_2_
  78.6 0.0 collective-permute-done.16.refs_3_
  78.6 0.0 copy-done.3
  78.6 1.5 %shard_map.117.refs_4_ = bf16[2,256,1024]{2,1,0:T(8,128)(2,1)} custom-call(s32[1]{0:T(128)} %bitcast.me_ref, bf16[1024,1024]{1,0:T(8,128)(2,1)S(1)} %copy-done.3, bf16[2,128,1024]{2,1,0:T(8,128)(2,1)S(1)} %get-tuple-element.44.x_ref, bf16[64,1024]{1,0:T(8,128)(2,1)S(1)} %get-tuple-element.51.refs_0_, bf16[64,1024]{1,0:T(8,128)(2,1)S(1)} %collective-permute-done.14.refs_1_, ...), custom_call_target="tpu_custom_call" | custom-call | flops 536870912 | bytes 4194308 | tf_op jit(solution)/shard_map/pallas_call | solution.py:285
  80.1 0.7 collective-permute-done.7.refs_1_
  80.8 1.2 %collective-permute-done.8.refs_2_ = bf16[64,1024]{1,0:T(8,128)(2,1)S(1)} collective-permute-done((bf16[64,1024]{1,0:T(8,128)(2,1)S(1)}, bf16[64,1024]{1,0:T(8,128)(2,1)S(1)}, u32[]{:S(2)}, u32[]{:S(2)}) %collective-permute-start.8) | collective-permute-done | bytes 131104 | tf_op jit(solution)/shard_map/ppermute | solution.py:305
  82.0 1.0 %collective-permute-done.9.refs_3_ = bf16[64,1024]{1,0:T(8,128)(2,1)S(1)} collective-permute-done((bf16[64,1024]{1,0:T(8,128)(2,1)S(1)}, bf16[64,1024]{1,0:T(8,128)(2,1)S(1)}, u32[]{:S(2)}, u32[]{:S(2)}) %collective-permute-start.9) | collective-permute-done | bytes 131104 | tf_op jit(solution)/shard_map/ppermute | solution.py:305
  83.0 1.5 %shard_map.118 = bf16[2,256,1024]{2,1,0:T(8,128)(2,1)} custom-call(s32[1]{0:T(128)} %bitcast.me_ref, bf16[1024,1024]{1,0:T(8,128)(2,1)S(1)} %copy-done.3, bf16[2,128,1024]{2,1,0:T(8,128)(2,1)S(1)} %get-tuple-element.33.x_ref, bf16[64,1024]{1,0:T(8,128)(2,1)S(1)} %get-tuple-element.40.refs_0_, ...), custom_call_target="tpu_custom_call", output_to_operand_aliasing={{}: (7, {})} | custom-call | flops 536870912 | bytes 5242884 | tf_op jit(solution)/shard_map/pallas_call | solution.py:285
  (2 shorter events, 0.0 us)
Async XLA Ops:
  0.0 18.9 %copy-start = (bf16[2,256,1024]{2,1,0:T(8,128)(2,1)S(1)}, bf16[2,256,1024]{2,1,0:T(8,128)(2,1)}, u32[]{:S(2)}) copy-start(bf16[2,256,1024]{2,1,0:T(8,128)(2,1)} %x_ref.5) | copy-start | bytes 3145732
  0.0 18.9 %copy-start.7 = (f32[1024]{0:T(1024)S(1)}, f32[1024]{0:T(1024)}, u32[]{:S(2)}) copy-start(f32[1024]{0:T(1024)} %param.12) | copy-start | bytes 12292
  0.0 18.9 %copy-start.9 = (f32[2,64]{1,0:T(2,128)S(1)}, f32[2,64]{1,0:T(2,128)}, u32[]{:S(2)}) copy-start(f32[2,64]{1,0:T(2,128)} %gain_ref.3) | copy-start | bytes 1540
  0.0 28.2 %copy-start.6 = (f32[1024]{0:T(1024)S(1)}, f32[1024]{0:T(1024)}, u32[]{:S(2)}) copy-start(f32[1024]{0:T(1024)} %param.17) | copy-start | bytes 12292
  3.7 24.5 %copy-start.1 = (bf16[1024,1024]{1,0:T(8,128)(2,1)S(1)}, bf16[1024,1024]{1,0:T(8,128)(2,1)}, u32[]{:S(2)}) copy-start(bf16[1024,1024]{1,0:T(8,128)(2,1)} %w_ref.7) | copy-start | bytes 6291460
  3.7 15.2 %collective-permute-start.1 = (bf16[2,512,256]{2,1,0:T(8,128)(2,1)}, bf16[2,512,256]{2,1,0:T(8,128)(2,1)S(1)}, u32[]{:S(2)}, u32[]{:S(2)}) collective-permute-start(bf16[2,512,256]{2,1,0:T(8,128)(2,1)} %shard_map.109.refs_0_), channel_id=1, source_target_pairs={{0,2},{1,3},{2,0},{3,1},{4,6},{5,7},{6,4},{7,5},{8,10},{9,11},{10,... | collective-permute-start | bytes 1572872 | tf_op jit(solution)/shard_map/ppermute | solution.py:305
  6.7 12.1 %collective-permute-start = (bf16[2,512,256]{2,1,0:T(8,128)(2,1)}, bf16[2,512,256]{2,1,0:T(8,128)(2,1)S(1)}, u32[]{:S(2)}, u32[]{:S(2)}) collective-permute-start(bf16[2,512,256]{2,1,0:T(8,128)(2,1)} %shard_map.109.refs_0_), channel_id=1, source_target_pairs={{0,1},{1,0},{2,3},{3,2},{4,5},{5,4},{6,7},{7,6},{8,9},{9,8},{10,11... | collective-permute-start | bytes 1572872 | tf_op jit(solution)/shard_map/ppermute | solution.py:305
  18.9 9.3 %collective-permute-start.2 = (bf16[2,512,256]{2,1,0:T(8,128)(2,1)S(1)}, bf16[2,512,256]{2,1,0:T(8,128)(2,1)S(1)}, u32[]{:S(2)}, u32[]{:S(2)}) collective-permute-start(bf16[2,512,256]{2,1,0:T(8,128)(2,1)S(1)} %collective-permute-done.1.refs_0_), channel_id=1, source_target_pairs={{0,1},{1,0},{2,3},{3,2},{4,5},{5,4},{6,7},{7,6},{8,9},{9,8},{10,11... | collective-permute-start | bytes 1572872 | tf_op jit(solution)/shard_map/ppermute | solution.py:305
  18.9 1.0 %copy-start.5 = (bf16[2,512,256]{2,1,0:T(8,128)(2,1)S(1)}, bf16[2,512,256]{2,1,0:T(8,128)(2,1)}, u32[]{:S(2)}) copy-start(bf16[2,512,256]{2,1,0:T(8,128)(2,1)} %shard_map.109.refs_0_) | copy-start | bytes 1572868
  19.9 1.6 %copy-start.10 = (bf16[1024,1024]{1,0:T(8,128)(2,1)S(1)}, bf16[1024,1024]{1,0:T(8,128)(2,1)}, u32[]{:S(2)}) copy-start(bf16[1024,1024]{1,0:T(8,128)(2,1)} %w_ref.5) | copy-start | bytes 6291460
  32.2 11.2 %collective-permute-start.10 = (bf16[64,1024]{1,0:T(8,128)(2,1)S(1)}, bf16[64,1024]{1,0:T(8,128)(2,1)S(1)}, u32[]{:S(2)}, u32[]{:S(2)}) collective-permute-start(bf16[64,1024]{1,0:T(8,128)(2,1)S(1)} %get-tuple-element.46), channel_id=1, source_target_pairs={{0,4},{4,0},{8,12},{12,8},{16,20},{20,16},{24,28},{28,24},{1,5},{5... | collective-permute-start | bytes 393224 | tf_op jit(solution)/shard_map/ppermute | solution.py:305
  34.0 9.5 %collective-permute-start.11 = (bf16[64,1024]{1,0:T(8,128)(2,1)S(1)}, bf16[64,1024]{1,0:T(8,128)(2,1)S(1)}, u32[]{:S(2)}, u32[]{:S(2)}) collective-permute-start(bf16[64,1024]{1,0:T(8,128)(2,1)S(1)} %get-tuple-element.47), channel_id=1, source_target_pairs={{0,8},{4,12},{8,0},{12,4},{16,24},{20,28},{24,16},{28,20},{1,9},{5... | collective-permute-start | bytes 393224 | tf_op jit(solution)/shard_map/ppermute | solution.py:305
  35.6 7.9 %copy-start.2 = (bf16[1024,1024]{1,0:T(8,128)(2,1)S(1)}, bf16[1024,1024]{1,0:T(8,128)(2,1)}, u32[]{:S(2)}) copy-start(bf16[1024,1024]{1,0:T(8,128)(2,1)} %wq_ref.3) | copy-start | bytes 6291460
  35.6 7.9 %copy-start.4 = (bf16[1024,512]{1,0:T(8,128)(2,1)S(1)}, bf16[1024,512]{1,0:T(8,128)(2,1)}, u32[]{:S(2)}) copy-start(bf16[1024,512]{1,0:T(8,128)(2,1)} %wkv_ref.3) | copy-start | bytes 3145732
  35.6 7.9 %copy-start.8 = (f32[2,64]{1,0:T(2,128)S(1)}, f32[2,64]{1,0:T(2,128)}, u32[]{:S(2)}) copy-start(f32[2,64]{1,0:T(2,128)} %gain_ref.5) | copy-start | bytes 1540
  35.6 7.9 %collective-permute-start.12 = (bf16[64,1024]{1,0:T(8,128)(2,1)S(1)}, bf16[64,1024]{1,0:T(8,128)(2,1)S(1)}, u32[]{:S(2)}, u32[]{:S(2)}) collective-permute-start(bf16[64,1024]{1,0:T(8,128)(2,1)S(1)} %get-tuple-element.48), channel_id=1, source_target_pairs={{0,12},{4,8},{8,4},{12,0},{16,28},{20,24},{24,20},{28,16},{1,13},{... | collective-permute-start | bytes 393224 | tf_op jit(solution)/shard_map/ppermute | solution.py:305
  39.9 7.7 %collective-permute-start.3 = (bf16[64,1024]{1,0:T(8,128)(2,1)S(1)}, bf16[64,1024]{1,0:T(8,128)(2,1)S(1)}, u32[]{:S(2)}, u32[]{:S(2)}) collective-permute-start(bf16[64,1024]{1,0:T(8,128)(2,1)S(1)} %get-tuple-element.35), channel_id=1, source_target_pairs={{0,4},{4,0},{8,12},{12,8},{16,20},{20,16},{24,28},{28,24},{1,5},{5... | collective-permute-start | bytes 393224 | tf_op jit(solution)/shard_map/ppermute | solution.py:305
  41.8 9.2 %collective-permute-start.4 = (bf16[64,1024]{1,0:T(8,128)(2,1)S(1)}, bf16[64,1024]{1,0:T(8,128)(2,1)S(1)}, u32[]{:S(2)}, u32[]{:S(2)}) collective-permute-start(bf16[64,1024]{1,0:T(8,128)(2,1)S(1)} %get-tuple-element.36), channel_id=1, source_target_pairs={{0,8},{4,12},{8,0},{12,4},{16,24},{20,28},{24,16},{28,20},{1,9},{5... | collective-permute-start | bytes 393224 | tf_op jit(solution)/shard_map/ppermute | solution.py:305
  43.3 8.7 %collective-permute-start.5 = (bf16[64,1024]{1,0:T(8,128)(2,1)S(1)}, bf16[64,1024]{1,0:T(8,128)(2,1)S(1)}, u32[]{:S(2)}, u32[]{:S(2)}) collective-permute-start(bf16[64,1024]{1,0:T(8,128)(2,1)S(1)} %get-tuple-element.37), channel_id=1, source_target_pairs={{0,12},{4,8},{8,4},{12,0},{16,28},{20,24},{24,20},{28,16},{1,13},{... | collective-permute-start | bytes 393224 | tf_op jit(solution)/shard_map/ppermute | solution.py:305
  44.7 21.0 %collective-permute-start.13 = (bf16[512,256]{1,0:T(8,128)(2,1)S(1)}, bf16[512,256]{1,0:T(8,128)(2,1)S(1)}, u32[]{:S(2)}, u32[]{:S(2)}) collective-permute-start(bf16[512,256]{1,0:T(8,128)(2,1)S(1)} %get-tuple-element.50.kv_ref), channel_id=1, source_target_pairs={{0,16},{4,20},{8,24},{12,28},{16,0},{20,4},{24,8},{28,12},{1,17},{... | collective-permute-start | bytes 786440 | tf_op jit(solution)/shard_map/ppermute | solution.py:305
  53.3 18.9 %collective-permute-start.6 = (bf16[512,256]{1,0:T(8,128)(2,1)S(1)}, bf16[512,256]{1,0:T(8,128)(2,1)S(1)}, u32[]{:S(2)}, u32[]{:S(2)}) collective-permute-start(bf16[512,256]{1,0:T(8,128)(2,1)S(1)} %get-tuple-element.39.kv_ref), channel_id=1, source_target_pairs={{0,16},{4,20},{8,24},{12,28},{16,0},{20,4},{24,8},{28,12},{1,17},{... | collective-permute-start | bytes 786440 | tf_op jit(solution)/shard_map/ppermute | solution.py:305
  68.5 10.1 %copy-start.3 = (bf16[1024,1024]{1,0:T(8,128)(2,1)S(1)}, bf16[1024,1024]{1,0:T(8,128)(2,1)}, u32[]{:S(2)}) copy-start(bf16[1024,1024]{1,0:T(8,128)(2,1)} %w_ref.9) | copy-start | bytes 6291460
  68.5 8.6 %collective-permute-start.14 = (bf16[64,1024]{1,0:T(8,128)(2,1)S(1)}, bf16[64,1024]{1,0:T(8,128)(2,1)S(1)}, u32[]{:S(2)}, u32[]{:S(2)}) collective-permute-start(bf16[64,1024]{1,0:T(8,128)(2,1)S(1)} %get-tuple-element.52), channel_id=1, source_target_pairs={{0,4},{4,0},{8,12},{12,8},{16,20},{20,16},{24,28},{28,24},{1,5},{5... | collective-permute-start | bytes 393224 | tf_op jit(solution)/shard_map/ppermute | solution.py:305
  70.7 7.9 %collective-permute-start.15 = (bf16[64,1024]{1,0:T(8,128)(2,1)S(1)}, bf16[64,1024]{1,0:T(8,128)(2,1)S(1)}, u32[]{:S(2)}, u32[]{:S(2)}) collective-permute-start(bf16[64,1024]{1,0:T(8,128)(2,1)S(1)} %get-tuple-element.53), channel_id=1, source_target_pairs={{0,8},{4,12},{8,0},{12,4},{16,24},{20,28},{24,16},{28,20},{1,9},{5... | collective-permute-start | bytes 393224 | tf_op jit(solution)/shard_map/ppermute | solution.py:305
  70.7 7.9 %collective-permute-start.16 = (bf16[64,1024]{1,0:T(8,128)(2,1)S(1)}, bf16[64,1024]{1,0:T(8,128)(2,1)S(1)}, u32[]{:S(2)}, u32[]{:S(2)}) collective-permute-start(bf16[64,1024]{1,0:T(8,128)(2,1)S(1)} %get-tuple-element.54), channel_id=1, source_target_pairs={{0,12},{4,8},{8,4},{12,0},{16,28},{20,24},{24,20},{28,16},{1,13},{... | collective-permute-start | bytes 393224 | tf_op jit(solution)/shard_map/ppermute | solution.py:305
  75.0 5.8 %collective-permute-start.7 = (bf16[64,1024]{1,0:T(8,128)(2,1)S(1)}, bf16[64,1024]{1,0:T(8,128)(2,1)S(1)}, u32[]{:S(2)}, u32[]{:S(2)}) collective-permute-start(bf16[64,1024]{1,0:T(8,128)(2,1)S(1)} %get-tuple-element.41), channel_id=1, source_target_pairs={{0,4},{4,0},{8,12},{12,8},{16,20},{20,16},{24,28},{28,24},{1,5},{5... | collective-permute-start | bytes 393224 | tf_op jit(solution)/shard_map/ppermute | solution.py:305
  77.1 5.0 %collective-permute-start.8 = (bf16[64,1024]{1,0:T(8,128)(2,1)S(1)}, bf16[64,1024]{1,0:T(8,128)(2,1)S(1)}, u32[]{:S(2)}, u32[]{:S(2)}) collective-permute-start(bf16[64,1024]{1,0:T(8,128)(2,1)S(1)} %get-tuple-element.42), channel_id=1, source_target_pairs={{0,8},{4,12},{8,0},{12,4},{16,24},{20,28},{24,16},{28,20},{1,9},{5... | collective-permute-start | bytes 393224 | tf_op jit(solution)/shard_map/ppermute | solution.py:305
  77.1 5.9 %collective-permute-start.9 = (bf16[64,1024]{1,0:T(8,128)(2,1)S(1)}, bf16[64,1024]{1,0:T(8,128)(2,1)S(1)}, u32[]{:S(2)}, u32[]{:S(2)}) collective-permute-start(bf16[64,1024]{1,0:T(8,128)(2,1)S(1)} %get-tuple-element.43), channel_id=1, source_target_pairs={{0,12},{4,8},{8,4},{12,0},{16,28},{20,24},{24,20},{28,16},{1,13},{... | collective-permute-start | bytes 393224 | tf_op jit(solution)/shard_map/ppermute | solution.py:305

commit v6 on v5

--- a/solution.py
+++ b/solution.py
@@ -204,31 +204,48 @@
     q_ref[...] = (q.astype(BF16).astype(F32) * head**-0.5).astype(BF16)
 
 
-def attend_time(head, q_ref, kv_refs, bias, att, groups):
+def attend_time(head, q_ref, kv_refs, bias, att, groups, before=None, after=None):
     count = q_ref.shape[1]
     kv_heads = (kv_refs[0].shape[0] - count) // head
     group, wide, cols = q_ref.shape[0] // head // kv_heads, 2 * head, count // groups
     for h in range(groups):
         lanes = slice(h * cols, (h + 1) * cols)
         for g in range(kv_heads):
+            places = [slice((g * group + i) * head, (g * group + i + 1) * head) for i in range(group)]
             keys = jnp.concatenate([ref[lanes, (g // 2) * wide : (g // 2 + 1) * wide] for ref in kv_refs], axis=0)
             s = dot(keys, query_columns(q_ref, (), g, group, head, g % 2 == 1, lanes))
             s = jnp.concatenate([s[:, i * cols : (i + 1) * cols] + bias[...] for i in range(group)], axis=1)
             largest = jnp.max(s, axis=0, keepdims=True)
+            if before is not None:
+                ml = before[1][h, g]
+                old = jnp.concatenate([ml[i : i + 1] for i in range(group)], axis=1)
+                largest = jnp.maximum(largest, old)
+                scale = jnp.exp2((old - largest) * LOG2E)
             e = jnp.exp2((s - largest) * LOG2E)
             total = jnp.sum(e, axis=0, keepdims=True)
             values = jnp.concatenate([ref[count + g * head : count + (g + 1) * head, lanes] for ref in kv_refs], axis=1)
-            out = (dot(values, e.astype(BF16)) / total).astype(BF16)
-            for i in range(group):
-                att[(g * group + i) * head : (g * group + i + 1) * head, lanes] = out[:, i * cols : (i + 1) * cols]
-
-
-def causal_bias(bias, frames, sub, me_ref):
-    def place(axis):
+            out = dot(values, e.astype(BF16))
+            if before is not None:
+                total += scale * jnp.concatenate([ml[group + i : group + i + 1] for i in range(group)], axis=1)
+                out += scale * jnp.concatenate([before[0][place, lanes] for place in places], axis=1)
+            if after is None:
+                out = (out / total).astype(BF16)
+            for i, place in enumerate(places):
+                mine = slice(i * cols, (i + 1) * cols)
+                if after is None:
+                    att[place, lanes] = out[:, mine]
+                else:
+                    after[0][place, lanes] = out[:, mine]
+                    after[1][h, g, i : i + 1] = largest[:, mine]
+                    after[1][h, g, group + i : group + i + 1] = total[:, mine]
+
+
+def causal_bias(bias, frames, sub, me_ref, first=0):
+    def place(axis, first):
         n = lax.broadcasted_iota(jnp.int32, bias.shape, axis)
-        return (n // (frames * sub) ^ me_ref[0]) * frames + (n // sub) % frames, n % sub
-
-    (frame_k, spot_k), (frame_q, spot_q) = place(0), place(1)
+        return ((n // (frames * sub) + first) ^ me_ref[0]) * frames + (n // sub) % frames, n % sub
+
+    (frame_k, spot_k), (frame_q, spot_q) = place(0, first), place(1, 0)
     bias[...] = jnp.where((spot_q == spot_k) & (frame_q >= frame_k), 0.0, -1e30)
 
 
@@ -241,6 +258,18 @@
     out_refs, (bias, att) = refs[:pieces], refs[pieces:]
     causal_bias(bias, frames, spots // groups, me_ref)
     attend_time(head, q_ref, (kv_ref, kv_other), bias, att, groups)
+    out_of_groups(att[...].T, out_refs, frames, spots, groups)
+
+
+def time_own_kernel(head, frames, spots, groups, me_ref, q_ref, kv_ref, o_ref, ml_ref, bias):
+    causal_bias(bias, frames, spots // groups, me_ref)
+    attend_time(head, q_ref, (kv_ref,), bias, None, groups, after=(o_ref, ml_ref))
+
+
+def time_other_kernel(head, frames, spots, groups, pieces, me_ref, q_ref, o_ref, ml_ref, kv_other, *refs):
+    out_refs, (bias, att) = refs[:pieces], refs[pieces:]
+    causal_bias(bias, frames, spots // groups, me_ref, pieces)
+    attend_time(head, q_ref, (kv_other,), bias, att, groups, before=(o_ref, ml_ref))
     out_of_groups(att[...].T, out_refs, frames, spots, groups)
 
 
@@ -406,7 +435,10 @@
             return mixed
 
         def exchange(xs):
-            return [permuted(x, "frames", frame_devices, k) if k else x for k, x in enumerate(xs)]
+            out = [xs[0]]
+            for k in range(1, len(xs)):
+                out.append(permuted(xs[k], "frames", frame_devices, k))
+            return out
 
         sub = n // groups
         streams, moved, projected, back = [], [], [], []
@@ -423,12 +455,24 @@
             )
             projected.append((q, kv_time, permuted(kv_time, "frames", frame_devices, top)))
         for c in range(chunks):
+            kernel, args, seen = time_attend_kernel, (me, *projected[c]), 2 * sub
+            if c == chunks - 1:
+                q, own, other = projected[c]
+                state = call(
+                    functools.partial(time_own_kernel, head, frames, spots, groups),
+                    (me, q, own),
+                    [shaped(q_width, n, dtype=F32), shaped(groups, half // head, 2 * q_width // half, sub, dtype=F32)],
+                    8 * n * 2 * sub * q_width,
+                    [pltpu.VMEM((sub, sub), F32)],
+                    smem=(0,),
+                )
+                kernel, args, seen = time_other_kernel, (me, q, *state, other), sub
             atts = call(
-                functools.partial(time_attend_kernel, head, frames, spots, groups, top),
-                (me, *projected[c]),
+                functools.partial(kernel, head, frames, spots, groups, top),
+                args,
                 [shaped(frames * spots, q_width)] * top,
-                16 * n * 2 * sub * q_width,
-                [pltpu.VMEM((2 * sub, sub), F32), pltpu.VMEM((q_width, n), BF16)],
+                8 * n * seen * q_width,
+                [pltpu.VMEM((seen, sub), F32), pltpu.VMEM((q_width, n), BF16)],
                 smem=(0,),
             )
             back.append(exchange(atts))

time: 84.8 us -> 86.2 us (1.017)
  Pallas kernels: 29.4 us -> 30.8 us
    pallas_call x10 -> x11, Pallas kernels: 29.4 us -> 30.8 us  [call(): pl.pallas_call(kernel, out_shape=outs, in_specs=in_specs, out_specs=[pl.B...]
  transfers between devices with their start and end apart: 17 -> 17, of which waited for: 8 -> 6; matrix products, arithmetic and copies ran while one was open for 0% -> 0% of each run, Pallas kernels for 24% -> 25%
where the time goes in v6:
time: 86.2 us; the launch traced here: 86 us
  Pallas kernels  30.8 us (36%)
  waiting for transfers between devices  30.7 us (36%)
  starting transfers between devices  21.5 us (25%)
  local copies, waits for them, and re-layouts  2.67 us (3%)
    pallas_call x11, Pallas kernels, call(): pl.pallas_call(kernel, out_shape=outs, in_specs=in_specs, out_specs=[pl.B...  30.8 us
    ppermute x17, waiting for transfers between devices, permuted(): return lax.ppermute(x, axis, [(i, i ^ bit) for i in range(size)])  30.7 us
    ppermute x17, starting transfers between devices, permuted(): return lax.ppermute(x, axis, [(i, i ^ bit) for i in range(size)])  21.5 us
    unnamed x22, local copies, waits for them, and re-layouts  2.67 us
  transfers between devices with their start and end apart: 17, of which 6 were waited for; matrix products, arithmetic and copies ran while one was open for 0% of the time, Pallas kernels for 25%

profile of v6, /device:TPU:0, one launch (start us, length us, event | category | flops | bytes accessed | tf_op | source)
XLA Modules:
  0.0 86.0 jit_solution(17932169761440315024)
XLA Ops:
  0.0 0.0 copy-start
  0.0 0.0 copy-start.9
  0.0 0.0 copy-start.7
  0.0 0.0 copy-start.6
  0.0 3.6 %shard_map.109.refs_0_ = bf16[2,512,256]{2,1,0:T(8,128)(2,1)} custom-call(s32[1]{0:T(128)} %bitcast.me_ref, bf16[2,256,1024]{2,1,0:T(8,128)(2,1)} %x_ref.5, f32[1,1024]{1,0:T(1,128)} %bitcast.5, bf16[1024,512]{1,0:T(8,128)(2,1)} %w_hbm.1, f32[2,64]{1,0:T(2,128)} %gain_ref.3), custom_call_target="tpu_custom_call" | custom-call | flops 536870912 | bytes 2626052 | tf_op jit(solution)/shard_map/pallas_call | solution.py:314
  3.7 0.0 copy-start.1
  3.7 3.0 %collective-permute-start.1 = (bf16[2,512,256]{2,1,0:T(8,128)(2,1)}, bf16[2,512,256]{2,1,0:T(8,128)(2,1)S(1)}, u32[]{:S(2)}, u32[]{:S(2)}) collective-permute-start(bf16[2,512,256]{2,1,0:T(8,128)(2,1)} %shard_map.109.refs_0_), channel_id=1, source_target_pairs={{0,2},{1,3},{2,0},{3,1},{4,6},{5,7},{6,4},{7,5},{8,10},{9,11},{10,... | collective-permute-start | bytes 1572872 | tf_op jit(solution)/shard_map/ppermute | solution.py:334
  6.7 0.0 collective-permute-start
  6.7 12.1 %collective-permute-done.1.refs_0_ = bf16[2,512,256]{2,1,0:T(8,128)(2,1)S(1)} collective-permute-done((bf16[2,512,256]{2,1,0:T(8,128)(2,1)}, bf16[2,512,256]{2,1,0:T(8,128)(2,1)S(1)}, u32[]{:S(2)}, u32[]{:S(2)}) %collective-permute-start.1) | collective-permute-done | bytes 524320 | tf_op jit(solution)/shard_map/ppermute | solution.py:334
  18.9 0.0 collective-permute-start.2
  18.9 0.0 collective-permute-done.refs_1_
  18.9 0.0 copy-done
  18.9 0.0 copy-done.9
  18.9 0.0 copy-done.7
  18.9 0.0 copy-start.5
  18.9 1.0 %copy-done.5 = bf16[2,512,256]{2,1,0:T(8,128)(2,1)S(1)} copy-done((bf16[2,512,256]{2,1,0:T(8,128)(2,1)S(1)}, bf16[2,512,256]{2,1,0:T(8,128)(2,1)}, u32[]{:S(2)}) %copy-start.5) | copy-done | bytes 524312
  19.9 0.0 copy-start.10
  19.9 1.6 %copy-done.10 = bf16[1024,1024]{1,0:T(8,128)(2,1)S(1)} copy-done((bf16[1024,1024]{1,0:T(8,128)(2,1)S(1)}, bf16[1024,1024]{1,0:T(8,128)(2,1)}, u32[]{:S(2)}) %copy-start.10) | copy-done | bytes 2097176
  21.5 6.7 %shard_map.110 = (bf16[2,1024,256]{2,1,0:T(8,128)(2,1)S(1)}, f32[2,1024,256]{2,1,0:T(8,128)S(1)}, f32[2,4,8,256]{3,2,1,0:T(8,128)S(1)}) custom-call(bf16[2,256,1024]{2,1,0:T(8,128)(2,1)S(1)} %copy-done, f32[1,1024]{1,0:T(1,128)S(1)} %bitcast.6, bf16[1024,1024]{1,0:T(8,128)(2,1)S(1)} %copy-done.10, f32[2,64]{1,0:T(2,128)S(1)} %copy-done.9, ...), custom_call_target="tpu_custom_call" | custom-call | flops 3221225472 | bytes 7410176 | tf_op jit(solution)/shard_map/pallas_call | solution.py:314
  28.2 0.0 collective-permute-done.2.refs_1_
  28.2 0.0 copy-done.6
  28.2 0.0 copy-done.1
  28.2 4.0 %shard_map.115 = (bf16[2,128,1024]{2,1,0:T(8,128)(2,1)S(1)}, bf16[64,1024]{1,0:T(8,128)(2,1)S(1)}, bf16[64,1024]{1,0:T(8,128)(2,1)S(1)}, bf16[64,1024]{1,0:T(8,128)(2,1)S(1)}, bf16[64,1024]{1,0:T(8,128)(2,1)S(1)}) custom-call(s32[1]{0:T(128)} %bitcast.me_ref, bf16[2,1024,256]{2,1,0:T(8,128)(2,1)S(1)} %get-tuple-element.32.q_ref, ...), custom_call_target="tpu_custom_call" | custom-call | flops 1610612736 | bytes 8458244 | tf_op jit(solution)/shard_map/pallas_call | solution.py:314
  32.2 1.8 %collective-permute-start.10 = (bf16[64,1024]{1,0:T(8,128)(2,1)S(1)}, bf16[64,1024]{1,0:T(8,128)(2,1)S(1)}, u32[]{:S(2)}, u32[]{:S(2)}) collective-permute-start(bf16[64,1024]{1,0:T(8,128)(2,1)S(1)} %get-tuple-element.50), channel_id=1, source_target_pairs={{0,4},{4,0},{8,12},{12,8},{16,20},{20,16},{24,28},{28,24},{1,5},{5... | collective-permute-start | bytes 393224 | tf_op jit(solution)/shard_map/ppermute | solution.py:334
  34.0 1.6 %collective-permute-start.11 = (bf16[64,1024]{1,0:T(8,128)(2,1)S(1)}, bf16[64,1024]{1,0:T(8,128)(2,1)S(1)}, u32[]{:S(2)}, u32[]{:S(2)}) collective-permute-start(bf16[64,1024]{1,0:T(8,128)(2,1)S(1)} %get-tuple-element.51), channel_id=1, source_target_pairs={{0,8},{4,12},{8,0},{12,4},{16,24},{20,28},{24,16},{28,20},{1,9},{5... | collective-permute-start | bytes 393224 | tf_op jit(solution)/shard_map/ppermute | solution.py:334
  35.6 0.1 collective-permute-start.12
  35.8 4.2 %shard_map.111 = (bf16[2,128,1024]{2,1,0:T(8,128)(2,1)S(1)}, bf16[64,1024]{1,0:T(8,128)(2,1)S(1)}, bf16[64,1024]{1,0:T(8,128)(2,1)S(1)}, bf16[64,1024]{1,0:T(8,128)(2,1)S(1)}, bf16[64,1024]{1,0:T(8,128)(2,1)S(1)}) custom-call(s32[1]{0:T(128)} %bitcast.me_ref, bf16[2,1024,256]{2,1,0:T(8,128)(2,1)S(1)} %get-tuple-element.32.q_ref, ...), custom_call_target="tpu_custom_call" | custom-call | flops 1610612736 | bytes 8458244 | tf_op jit(solution)/shard_map/pallas_call | solution.py:314
  39.9 1.8 %collective-permute-start.3 = (bf16[64,1024]{1,0:T(8,128)(2,1)S(1)}, bf16[64,1024]{1,0:T(8,128)(2,1)S(1)}, u32[]{:S(2)}, u32[]{:S(2)}) collective-permute-start(bf16[64,1024]{1,0:T(8,128)(2,1)S(1)} %get-tuple-element.37), channel_id=1, source_target_pairs={{0,4},{4,0},{8,12},{12,8},{16,20},{20,16},{24,28},{28,24},{1,5},{5... | collective-permute-start | bytes 393224 | tf_op jit(solution)/shard_map/ppermute | solution.py:334
  41.8 1.6 %collective-permute-start.4 = (bf16[64,1024]{1,0:T(8,128)(2,1)S(1)}, bf16[64,1024]{1,0:T(8,128)(2,1)S(1)}, u32[]{:S(2)}, u32[]{:S(2)}) collective-permute-start(bf16[64,1024]{1,0:T(8,128)(2,1)S(1)} %get-tuple-element.38), channel_id=1, source_target_pairs={{0,8},{4,12},{8,0},{12,4},{16,24},{20,28},{24,16},{28,20},{1,9},{5... | collective-permute-start | bytes 393224 | tf_op jit(solution)/shard_map/ppermute | solution.py:334
  43.3 0.0 collective-permute-done.10.refs_1_
  43.3 0.1 collective-permute-start.5
  43.5 0.0 collective-permute-done.11.refs_2_
  43.5 0.0 collective-permute-done.12.refs_3_
  43.5 0.0 copy-done.2
  43.5 0.0 copy-done.4
  43.5 0.0 copy-done.8
  43.5 1.2 %shard_map.116 = (bf16[1024,256]{1,0:T(8,128)(2,1)S(1)}, bf16[512,256]{1,0:T(8,128)(2,1)S(1)}) custom-call(f32[2,64]{1,0:T(2,128)S(1)} %copy-done.8, bf16[1024,512]{1,0:T(8,128)(2,1)S(1)} %copy-done.4, bf16[1024,1024]{1,0:T(8,128)(2,1)S(1)} %copy-done.2, bf16[64,1024]{1,0:T(8,128)(2,1)S(1)} %get-tuple-element.49.refs_0_, ...), custom_call_target="tpu_custom_call" | custom-call | flops 805306368 | bytes 4456960 | tf_op jit(solution)/shard_map/pallas_call | solution.py:314
  44.7 2.9 %collective-permute-start.13 = (bf16[512,256]{1,0:T(8,128)(2,1)S(1)}, bf16[512,256]{1,0:T(8,128)(2,1)S(1)}, u32[]{:S(2)}, u32[]{:S(2)}) collective-permute-start(bf16[512,256]{1,0:T(8,128)(2,1)S(1)} %get-tuple-element.54.kv_ref), channel_id=1, source_target_pairs={{0,16},{4,20},{8,24},{12,28},{16,0},{20,4},{24,8},{28,12},{1,17},{... | collective-permute-start | bytes 786440 | tf_op jit(solution)/shard_map/ppermute | solution.py:334
  47.6 0.0 collective-permute-done.3.refs_1_
  47.6 3.3 %collective-permute-done.4.refs_2_ = bf16[64,1024]{1,0:T(8,128)(2,1)S(1)} collective-permute-done((bf16[64,1024]{1,0:T(8,128)(2,1)S(1)}, bf16[64,1024]{1,0:T(8,128)(2,1)S(1)}, u32[]{:S(2)}, u32[]{:S(2)}) %collective-permute-start.4) | collective-permute-done | bytes 131104 | tf_op jit(solution)/shard_map/ppermute | solution.py:334
  50.9 1.2 %collective-permute-done.5.refs_3_ = bf16[64,1024]{1,0:T(8,128)(2,1)S(1)} collective-permute-done((bf16[64,1024]{1,0:T(8,128)(2,1)S(1)}, bf16[64,1024]{1,0:T(8,128)(2,1)S(1)}, u32[]{:S(2)}, u32[]{:S(2)}) %collective-permute-start.5) | collective-permute-done | bytes 131104 | tf_op jit(solution)/shard_map/ppermute | solution.py:334
  52.1 1.2 %shard_map.112 = (bf16[1024,256]{1,0:T(8,128)(2,1)S(1)}, bf16[512,256]{1,0:T(8,128)(2,1)S(1)}) custom-call(f32[2,64]{1,0:T(2,128)S(1)} %copy-done.8, bf16[1024,512]{1,0:T(8,128)(2,1)S(1)} %copy-done.4, bf16[1024,1024]{1,0:T(8,128)(2,1)S(1)} %copy-done.2, bf16[64,1024]{1,0:T(8,128)(2,1)S(1)} %get-tuple-element.36.refs_0_, ...), custom_call_target="tpu_custom_call" | custom-call | flops 805306368 | bytes 4456960 | tf_op jit(solution)/shard_map/pallas_call | solution.py:314
  53.3 1.1 %collective-permute-start.6 = (bf16[512,256]{1,0:T(8,128)(2,1)S(1)}, bf16[512,256]{1,0:T(8,128)(2,1)S(1)}, u32[]{:S(2)}, u32[]{:S(2)}) collective-permute-start(bf16[512,256]{1,0:T(8,128)(2,1)S(1)} %get-tuple-element.41.kv_ref), channel_id=1, source_target_pairs={{0,16},{4,20},{8,24},{12,28},{16,0},{20,4},{24,8},{28,12},{1,17},{... | collective-permute-start | bytes 786440 | tf_op jit(solution)/shard_map/ppermute | solution.py:334
  54.5 11.2 %collective-permute-done.13.kv_other = bf16[512,256]{1,0:T(8,128)(2,1)S(1)} collective-permute-done((bf16[512,256]{1,0:T(8,128)(2,1)S(1)}, bf16[512,256]{1,0:T(8,128)(2,1)S(1)}, u32[]{:S(2)}, u32[]{:S(2)}) %collective-permute-start.13) | collective-permute-done | bytes 262176 | tf_op jit(solution)/shard_map/ppermute | solution.py:334
  65.7 2.8 %shard_map.117 = (bf16[64,1024]{1,0:T(8,128)(2,1)S(1)}, bf16[64,1024]{1,0:T(8,128)(2,1)S(1)}, bf16[64,1024]{1,0:T(8,128)(2,1)S(1)}, bf16[64,1024]{1,0:T(8,128)(2,1)S(1)}) custom-call(s32[1]{0:T(128)} %bitcast.me_ref, bf16[1024,256]{1,0:T(8,128)(2,1)S(1)} %get-tuple-element.53.q_ref, bf16[512,256]{1,0:T(8,128)(2,1)S(1)} %get-tuple-element.54.kv_ref, ...), custom_call_target="tpu_custom_call" | custom-call | flops 536870912 | bytes 1572868 | tf_op jit(solution)/shard_map/pallas_call | solution.py:314
  68.5 0.0 copy-start.3
  68.5 2.2 %collective-permute-start.14 = (bf16[64,1024]{1,0:T(8,128)(2,1)S(1)}, bf16[64,1024]{1,0:T(8,128)(2,1)S(1)}, u32[]{:S(2)}, u32[]{:S(2)}) collective-permute-start(bf16[64,1024]{1,0:T(8,128)(2,1)S(1)} %get-tuple-element.56), channel_id=1, source_target_pairs={{0,4},{4,0},{8,12},{12,8},{16,20},{20,16},{24,28},{28,24},{1,5},{5... | collective-permute-start | bytes 393224 | tf_op jit(solution)/shard_map/ppermute | solution.py:334
  70.7 0.0 collective-permute-start.15
  70.7 1.5 %collective-permute-start.16 = (bf16[64,1024]{1,0:T(8,128)(2,1)S(1)}, bf16[64,1024]{1,0:T(8,128)(2,1)S(1)}, u32[]{:S(2)}, u32[]{:S(2)}) collective-permute-start(bf16[64,1024]{1,0:T(8,128)(2,1)S(1)} %get-tuple-element.58), channel_id=1, source_target_pairs={{0,12},{4,8},{8,4},{12,0},{16,28},{20,24},{24,20},{28,16},{1,13},{... | collective-permute-start | bytes 393224 | tf_op jit(solution)/shard_map/ppermute | solution.py:334
  72.3 2.0 %shard_map.113 = (f32[1024,256]{1,0:T(8,128)S(1)}, f32[2,4,8,128]{3,2,1,0:T(8,128)S(1)}) custom-call(s32[1]{0:T(128)} %bitcast.me_ref, bf16[1024,256]{1,0:T(8,128)(2,1)S(1)} %get-tuple-element.40.q_ref, bf16[512,256]{1,0:T(8,128)(2,1)S(1)} %get-tuple-element.41.kv_ref), custom_call_target="tpu_custom_call" | custom-call | flops 536870912 | bytes 1867780 | tf_op jit(solution)/shard_map/pallas_call | solution.py:314
  74.3 0.0 collective-permute-done.6.kv_other
  74.3 2.2 %shard_map.114 = (bf16[64,1024]{1,0:T(8,128)(2,1)S(1)}, bf16[64,1024]{1,0:T(8,128)(2,1)S(1)}, bf16[64,1024]{1,0:T(8,128)(2,1)S(1)}, bf16[64,1024]{1,0:T(8,128)(2,1)S(1)}) custom-call(s32[1]{0:T(128)} %bitcast.me_ref, bf16[1024,256]{1,0:T(8,128)(2,1)S(1)} %get-tuple-element.40.q_ref, f32[1024,256]{1,0:T(8,128)S(1)} %get-tuple-element.42.o_ref, ...), custom_call_target="tpu_custom_call" | custom-call | flops 268435456 | bytes 2392068 | tf_op jit(solution)/shard_map/pallas_call | solution.py:314
  76.4 2.0 %collective-permute-start.7 = (bf16[64,1024]{1,0:T(8,128)(2,1)S(1)}, bf16[64,1024]{1,0:T(8,128)(2,1)S(1)}, u32[]{:S(2)}, u32[]{:S(2)}) collective-permute-start(bf16[64,1024]{1,0:T(8,128)(2,1)S(1)} %get-tuple-element.45), channel_id=1, source_target_pairs={{0,4},{4,0},{8,12},{12,8},{16,20},{20,16},{24,28},{28,24},{1,5},{5... | collective-permute-start | bytes 393224 | tf_op jit(solution)/shard_map/ppermute | solution.py:334
  78.5 0.0 collective-permute-start.8
  78.5 0.0 collective-permute-done.14.refs_1_
  78.5 1.5 %collective-permute-start.9 = (bf16[64,1024]{1,0:T(8,128)(2,1)S(1)}, bf16[64,1024]{1,0:T(8,128)(2,1)S(1)}, u32[]{:S(2)}, u32[]{:S(2)}) collective-permute-start(bf16[64,1024]{1,0:T(8,128)(2,1)S(1)} %get-tuple-element.47), channel_id=1, source_target_pairs={{0,12},{4,8},{8,4},{12,0},{16,28},{20,24},{24,20},{28,16},{1,13},{... | collective-permute-start | bytes 393224 | tf_op jit(solution)/shard_map/ppermute | solution.py:334
  80.0 0.0 collective-permute-done.15.refs_2_
  80.0 0.0 collective-permute-done.16.refs_3_
  80.0 0.0 copy-done.3
  80.0 1.5 %shard_map.118.refs_4_ = bf16[2,256,1024]{2,1,0:T(8,128)(2,1)} custom-call(s32[1]{0:T(128)} %bitcast.me_ref, bf16[1024,1024]{1,0:T(8,128)(2,1)S(1)} %copy-done.3, bf16[2,128,1024]{2,1,0:T(8,128)(2,1)S(1)} %get-tuple-element.48.x_ref, bf16[64,1024]{1,0:T(8,128)(2,1)S(1)} %get-tuple-element.55.refs_0_, bf16[64,1024]{1,0:T(8,128)(2,1)S(1)} %collective-permute-done.14.refs_1_, ...), custom_call_target="tpu_custom_call" | custom-call | flops 536870912 | bytes 4194308 | tf_op jit(solution)/shard_map/pallas_call | solution.py:314
  81.5 0.0 collective-permute-done.7.refs_1_
  81.5 1.9 %collective-permute-done.8.refs_2_ = bf16[64,1024]{1,0:T(8,128)(2,1)S(1)} collective-permute-done((bf16[64,1024]{1,0:T(8,128)(2,1)S(1)}, bf16[64,1024]{1,0:T(8,128)(2,1)S(1)}, u32[]{:S(2)}, u32[]{:S(2)}) %collective-permute-start.8) | collective-permute-done | bytes 131104 | tf_op jit(solution)/shard_map/ppermute | solution.py:334
  83.4 0.9 %collective-permute-done.9.refs_3_ = bf16[64,1024]{1,0:T(8,128)(2,1)S(1)} collective-permute-done((bf16[64,1024]{1,0:T(8,128)(2,1)S(1)}, bf16[64,1024]{1,0:T(8,128)(2,1)S(1)}, u32[]{:S(2)}, u32[]{:S(2)}) %collective-permute-start.9) | collective-permute-done | bytes 131104 | tf_op jit(solution)/shard_map/ppermute | solution.py:334
  84.3 1.5 %shard_map.119 = bf16[2,256,1024]{2,1,0:T(8,128)(2,1)} custom-call(s32[1]{0:T(128)} %bitcast.me_ref, bf16[1024,1024]{1,0:T(8,128)(2,1)S(1)} %copy-done.3, bf16[2,128,1024]{2,1,0:T(8,128)(2,1)S(1)} %get-tuple-element.35.x_ref, bf16[64,1024]{1,0:T(8,128)(2,1)S(1)} %get-tuple-element.44.refs_0_, ...), custom_call_target="tpu_custom_call", output_to_operand_aliasing={{}: (7, {})} | custom-call | flops 536870912 | bytes 5242884 | tf_op jit(solution)/shard_map/pallas_call | solution.py:314
  (3 shorter events, 0.0 us)
Async XLA Ops:
  0.0 18.9 %copy-start = (bf16[2,256,1024]{2,1,0:T(8,128)(2,1)S(1)}, bf16[2,256,1024]{2,1,0:T(8,128)(2,1)}, u32[]{:S(2)}) copy-start(bf16[2,256,1024]{2,1,0:T(8,128)(2,1)} %x_ref.5) | copy-start | bytes 3145732
  0.0 18.9 %copy-start.9 = (f32[2,64]{1,0:T(2,128)S(1)}, f32[2,64]{1,0:T(2,128)}, u32[]{:S(2)}) copy-start(f32[2,64]{1,0:T(2,128)} %gain_ref.3) | copy-start | bytes 1540
  0.0 18.9 %copy-start.7 = (f32[1024]{0:T(1024)S(1)}, f32[1024]{0:T(1024)}, u32[]{:S(2)}) copy-start(f32[1024]{0:T(1024)} %param.12) | copy-start | bytes 12292
  0.0 28.2 %copy-start.6 = (f32[1024]{0:T(1024)S(1)}, f32[1024]{0:T(1024)}, u32[]{:S(2)}) copy-start(f32[1024]{0:T(1024)} %param.17) | copy-start | bytes 12292
  3.7 24.5 %copy-start.1 = (bf16[1024,1024]{1,0:T(8,128)(2,1)S(1)}, bf16[1024,1024]{1,0:T(8,128)(2,1)}, u32[]{:S(2)}) copy-start(bf16[1024,1024]{1,0:T(8,128)(2,1)} %w_ref.7) | copy-start | bytes 6291460
  3.7 15.2 %collective-permute-start.1 = (bf16[2,512,256]{2,1,0:T(8,128)(2,1)}, bf16[2,512,256]{2,1,0:T(8,128)(2,1)S(1)}, u32[]{:S(2)}, u32[]{:S(2)}) collective-permute-start(bf16[2,512,256]{2,1,0:T(8,128)(2,1)} %shard_map.109.refs_0_), channel_id=1, source_target_pairs={{0,2},{1,3},{2,0},{3,1},{4,6},{5,7},{6,4},{7,5},{8,10},{9,11},{10,... | collective-permute-start | bytes 1572872 | tf_op jit(solution)/shard_map/ppermute | solution.py:334
  6.7 12.1 %collective-permute-start = (bf16[2,512,256]{2,1,0:T(8,128)(2,1)}, bf16[2,512,256]{2,1,0:T(8,128)(2,1)S(1)}, u32[]{:S(2)}, u32[]{:S(2)}) collective-permute-start(bf16[2,512,256]{2,1,0:T(8,128)(2,1)} %shard_map.109.refs_0_), channel_id=1, source_target_pairs={{0,1},{1,0},{2,3},{3,2},{4,5},{5,4},{6,7},{7,6},{8,9},{9,8},{10,11... | collective-permute-start | bytes 1572872 | tf_op jit(solution)/shard_map/ppermute | solution.py:334
  18.9 9.3 %collective-permute-start.2 = (bf16[2,512,256]{2,1,0:T(8,128)(2,1)S(1)}, bf16[2,512,256]{2,1,0:T(8,128)(2,1)S(1)}, u32[]{:S(2)}, u32[]{:S(2)}) collective-permute-start(bf16[2,512,256]{2,1,0:T(8,128)(2,1)S(1)} %collective-permute-done.1.refs_0_), channel_id=1, source_target_pairs={{0,1},{1,0},{2,3},{3,2},{4,5},{5,4},{6,7},{7,6},{8,9},{9,8},{10,11... | collective-permute-start | bytes 1572872 | tf_op jit(solution)/shard_map/ppermute | solution.py:334
  18.9 1.0 %copy-start.5 = (bf16[2,512,256]{2,1,0:T(8,128)(2,1)S(1)}, bf16[2,512,256]{2,1,0:T(8,128)(2,1)}, u32[]{:S(2)}) copy-start(bf16[2,512,256]{2,1,0:T(8,128)(2,1)} %shard_map.109.refs_0_) | copy-start | bytes 1572868
  19.9 1.6 %copy-start.10 = (bf16[1024,1024]{1,0:T(8,128)(2,1)S(1)}, bf16[1024,1024]{1,0:T(8,128)(2,1)}, u32[]{:S(2)}) copy-start(bf16[1024,1024]{1,0:T(8,128)(2,1)} %w_ref.5) | copy-start | bytes 6291460
  32.2 11.2 %collective-permute-start.10 = (bf16[64,1024]{1,0:T(8,128)(2,1)S(1)}, bf16[64,1024]{1,0:T(8,128)(2,1)S(1)}, u32[]{:S(2)}, u32[]{:S(2)}) collective-permute-start(bf16[64,1024]{1,0:T(8,128)(2,1)S(1)} %get-tuple-element.50), channel_id=1, source_target_pairs={{0,4},{4,0},{8,12},{12,8},{16,20},{20,16},{24,28},{28,24},{1,5},{5... | collective-permute-start | bytes 393224 | tf_op jit(solution)/shard_map/ppermute | solution.py:334
  34.0 9.5 %collective-permute-start.11 = (bf16[64,1024]{1,0:T(8,128)(2,1)S(1)}, bf16[64,1024]{1,0:T(8,128)(2,1)S(1)}, u32[]{:S(2)}, u32[]{:S(2)}) collective-permute-start(bf16[64,1024]{1,0:T(8,128)(2,1)S(1)} %get-tuple-element.51), channel_id=1, source_target_pairs={{0,8},{4,12},{8,0},{12,4},{16,24},{20,28},{24,16},{28,20},{1,9},{5... | collective-permute-start | bytes 393224 | tf_op jit(solution)/shard_map/ppermute | solution.py:334
  35.6 7.9 %copy-start.2 = (bf16[1024,1024]{1,0:T(8,128)(2,1)S(1)}, bf16[1024,1024]{1,0:T(8,128)(2,1)}, u32[]{:S(2)}) copy-start(bf16[1024,1024]{1,0:T(8,128)(2,1)} %wq_ref.3) | copy-start | bytes 6291460
  35.6 7.9 %copy-start.4 = (bf16[1024,512]{1,0:T(8,128)(2,1)S(1)}, bf16[1024,512]{1,0:T(8,128)(2,1)}, u32[]{:S(2)}) copy-start(bf16[1024,512]{1,0:T(8,128)(2,1)} %wkv_ref.3) | copy-start | bytes 3145732
  35.6 7.9 %copy-start.8 = (f32[2,64]{1,0:T(2,128)S(1)}, f32[2,64]{1,0:T(2,128)}, u32[]{:S(2)}) copy-start(f32[2,64]{1,0:T(2,128)} %gain_ref.5) | copy-start | bytes 1540
  35.6 7.9 %collective-permute-start.12 = (bf16[64,1024]{1,0:T(8,128)(2,1)S(1)}, bf16[64,1024]{1,0:T(8,128)(2,1)S(1)}, u32[]{:S(2)}, u32[]{:S(2)}) collective-permute-start(bf16[64,1024]{1,0:T(8,128)(2,1)S(1)} %get-tuple-element.52), channel_id=1, source_target_pairs={{0,12},{4,8},{8,4},{12,0},{16,28},{20,24},{24,20},{28,16},{1,13},{... | collective-permute-start | bytes 393224 | tf_op jit(solution)/shard_map/ppermute | solution.py:334
  39.9 7.7 %collective-permute-start.3 = (bf16[64,1024]{1,0:T(8,128)(2,1)S(1)}, bf16[64,1024]{1,0:T(8,128)(2,1)S(1)}, u32[]{:S(2)}, u32[]{:S(2)}) collective-permute-start(bf16[64,1024]{1,0:T(8,128)(2,1)S(1)} %get-tuple-element.37), channel_id=1, source_target_pairs={{0,4},{4,0},{8,12},{12,8},{16,20},{20,16},{24,28},{28,24},{1,5},{5... | collective-permute-start | bytes 393224 | tf_op jit(solution)/shard_map/ppermute | solution.py:334
  41.8 9.2 %collective-permute-start.4 = (bf16[64,1024]{1,0:T(8,128)(2,1)S(1)}, bf16[64,1024]{1,0:T(8,128)(2,1)S(1)}, u32[]{:S(2)}, u32[]{:S(2)}) collective-permute-start(bf16[64,1024]{1,0:T(8,128)(2,1)S(1)} %get-tuple-element.38), channel_id=1, source_target_pairs={{0,8},{4,12},{8,0},{12,4},{16,24},{20,28},{24,16},{28,20},{1,9},{5... | collective-permute-start | bytes 393224 | tf_op jit(solution)/shard_map/ppermute | solution.py:334
  43.3 8.8 %collective-permute-start.5 = (bf16[64,1024]{1,0:T(8,128)(2,1)S(1)}, bf16[64,1024]{1,0:T(8,128)(2,1)S(1)}, u32[]{:S(2)}, u32[]{:S(2)}) collective-permute-start(bf16[64,1024]{1,0:T(8,128)(2,1)S(1)} %get-tuple-element.39), channel_id=1, source_target_pairs={{0,12},{4,8},{8,4},{12,0},{16,28},{20,24},{24,20},{28,16},{1,13},{... | collective-permute-start | bytes 393224 | tf_op jit(solution)/shard_map/ppermute | solution.py:334
  44.7 21.0 %collective-permute-start.13 = (bf16[512,256]{1,0:T(8,128)(2,1)S(1)}, bf16[512,256]{1,0:T(8,128)(2,1)S(1)}, u32[]{:S(2)}, u32[]{:S(2)}) collective-permute-start(bf16[512,256]{1,0:T(8,128)(2,1)S(1)} %get-tuple-element.54.kv_ref), channel_id=1, source_target_pairs={{0,16},{4,20},{8,24},{12,28},{16,0},{20,4},{24,8},{28,12},{1,17},{... | collective-permute-start | bytes 786440 | tf_op jit(solution)/shard_map/ppermute | solution.py:334
  53.3 20.9 %collective-permute-start.6 = (bf16[512,256]{1,0:T(8,128)(2,1)S(1)}, bf16[512,256]{1,0:T(8,128)(2,1)S(1)}, u32[]{:S(2)}, u32[]{:S(2)}) collective-permute-start(bf16[512,256]{1,0:T(8,128)(2,1)S(1)} %get-tuple-element.41.kv_ref), channel_id=1, source_target_pairs={{0,16},{4,20},{8,24},{12,28},{16,0},{20,4},{24,8},{28,12},{1,17},{... | collective-permute-start | bytes 786440 | tf_op jit(solution)/shard_map/ppermute | solution.py:334
  68.5 11.5 %copy-start.3 = (bf16[1024,1024]{1,0:T(8,128)(2,1)S(1)}, bf16[1024,1024]{1,0:T(8,128)(2,1)}, u32[]{:S(2)}) copy-start(bf16[1024,1024]{1,0:T(8,128)(2,1)} %w_ref.9) | copy-start | bytes 6291460
  68.5 9.9 %collective-permute-start.14 = (bf16[64,1024]{1,0:T(8,128)(2,1)S(1)}, bf16[64,1024]{1,0:T(8,128)(2,1)S(1)}, u32[]{:S(2)}, u32[]{:S(2)}) collective-permute-start(bf16[64,1024]{1,0:T(8,128)(2,1)S(1)} %get-tuple-element.56), channel_id=1, source_target_pairs={{0,4},{4,0},{8,12},{12,8},{16,20},{20,16},{24,28},{28,24},{1,5},{5... | collective-permute-start | bytes 393224 | tf_op jit(solution)/shard_map/ppermute | solution.py:334
  70.7 9.3 %collective-permute-start.15 = (bf16[64,1024]{1,0:T(8,128)(2,1)S(1)}, bf16[64,1024]{1,0:T(8,128)(2,1)S(1)}, u32[]{:S(2)}, u32[]{:S(2)}) collective-permute-start(bf16[64,1024]{1,0:T(8,128)(2,1)S(1)} %get-tuple-element.57), channel_id=1, source_target_pairs={{0,8},{4,12},{8,0},{12,4},{16,24},{20,28},{24,16},{28,20},{1,9},{5... | collective-permute-start | bytes 393224 | tf_op jit(solution)/shard_map/ppermute | solution.py:334
  70.7 9.3 %collective-permute-start.16 = (bf16[64,1024]{1,0:T(8,128)(2,1)S(1)}, bf16[64,1024]{1,0:T(8,128)(2,1)S(1)}, u32[]{:S(2)}, u32[]{:S(2)}) collective-permute-start(bf16[64,1024]{1,0:T(8,128)(2,1)S(1)} %get-tuple-element.58), channel_id=1, source_target_pairs={{0,12},{4,8},{8,4},{12,0},{16,28},{20,24},{24,20},{28,16},{1,13},{... | collective-permute-start | bytes 393224 | tf_op jit(solution)/shard_map/ppermute | solution.py:334
  76.4 5.1 %collective-permute-start.7 = (bf16[64,1024]{1,0:T(8,128)(2,1)S(1)}, bf16[64,1024]{1,0:T(8,128)(2,1)S(1)}, u32[]{:S(2)}, u32[]{:S(2)}) collective-permute-start(bf16[64,1024]{1,0:T(8,128)(2,1)S(1)} %get-tuple-element.45), channel_id=1, source_target_pairs={{0,4},{4,0},{8,12},{12,8},{16,20},{20,16},{24,28},{28,24},{1,5},{5... | collective-permute-start | bytes 393224 | tf_op jit(solution)/shard_map/ppermute | solution.py:334
  78.5 5.0 %collective-permute-start.8 = (bf16[64,1024]{1,0:T(8,128)(2,1)S(1)}, bf16[64,1024]{1,0:T(8,128)(2,1)S(1)}, u32[]{:S(2)}, u32[]{:S(2)}) collective-permute-start(bf16[64,1024]{1,0:T(8,128)(2,1)S(1)} %get-tuple-element.46), channel_id=1, source_target_pairs={{0,8},{4,12},{8,0},{12,4},{16,24},{20,28},{24,16},{28,20},{1,9},{5... | collective-permute-start | bytes 393224 | tf_op jit(solution)/shard_map/ppermute | solution.py:334
  78.5 5.9 %collective-permute-start.9 = (bf16[64,1024]{1,0:T(8,128)(2,1)S(1)}, bf16[64,1024]{1,0:T(8,128)(2,1)S(1)}, u32[]{:S(2)}, u32[]{:S(2)}) collective-permute-start(bf16[64,1024]{1,0:T(8,128)(2,1)S(1)} %get-tuple-element.47), channel_id=1, source_target_pairs={{0,12},{4,8},{8,4},{12,0},{16,28},{20,24},{24,20},{28,16},{1,13},{... | collective-permute-start | bytes 393224 | tf_op jit(solution)/shard_map/ppermute | solution.py:334
